TPU v7x, 32 devices: a whole 2x2x4 slice. The times are simulated.
32 devices in a mesh: seq: 8 (over z, y), head: 4 (over x, core).
Axes of the slice: x: 2, y: 2, z: 4, core: 2. Of those that a mesh axis runs over, the one named last changes fastest.
Arguments:
- queries: bfloat16 [8192, 512], P('seq', 'head'), may hold values from -6 to 6
- keys: bfloat16 [8192, 512], P('seq', 'head'), may hold values from -6 to 6
- values: bfloat16 [8192, 512], P('seq', 'head'), may hold values from -6 to 6
- out_grad: bfloat16 [8192, 512], P('seq', 'head'), may hold values from -6 to 6
- lengths: int32 [4], replicated, may hold values from 1 to 3072, 8192 in all
- w_proj: bfloat16 [3, 512, 512], P(None, None, 'head'), may hold values from -0.25 to 0.25
Outputs:
- d_input: float32 [8192, 512], P(('seq', 'head'))
Inputs may be any that keep to these rules, and one draw needn't show every extreme that they name: The lengths sum to 8192; the longest is exactly 3072.
All inputs are finite; a program needn't handle non-finite values.
Results may differ from a plain program's by a relative error of at most 0.006.
Values may be sent and summed in bfloat16 or wider, within the bound.
No kernel may reach another device: no remote copies, remote signals or barrier semaphores. Data moves between devices by JAX's collectives and lax.ppermute only.
A program may use at most 64 MiB of HBM per device.

v0:
```python
import math

import jax
import jax.numpy as jnp
from jax import lax
from jax.sharding import PartitionSpec as P

LAGS = 4
MAXLEN = 3072


def from_behind(value, axis, by):
    count = lax.axis_size(axis)
    pairs = [(i, i + by) for i in range(count) if 0 <= i + by < count]
    return lax.ppermute(value, axis, pairs)


def user_of(positions, user_ends):
    return jnp.sum((user_ends[None, :] <= positions[:, None]).astype(jnp.int32), axis=1)


def tile_task(query_side, key_side, query_start, key_start, user_ends):
    tile_rows = query_side.shape[1]
    head_width = query_side.shape[2]
    score_scale = head_width ** (-0.5)
    norm_factor = 1.0 / math.sqrt(MAXLEN)
    offsets = lax.iota(jnp.int32, tile_rows)
    query_pos = query_start + offsets
    key_pos = key_start + offsets
    query_user = user_of(query_pos, user_ends)
    key_user = user_of(key_pos, user_ends)
    visible = (key_pos[None, :] <= query_pos[:, None]) & (query_user[:, None] == key_user[None, :])
    scores = (
        jnp.einsum("qh,kh->qk", query_side[0], key_side[0], preferred_element_type=jnp.float32)
        * score_scale
    )
    gate_prob = jax.nn.sigmoid(scores)
    weights = jnp.where(visible, scores * gate_prob * norm_factor, 0.0).astype(jnp.bfloat16)
    d_weights = jnp.einsum(
        "qh,kh->qk", query_side[1], key_side[1], preferred_element_type=jnp.float32
    )
    d_scores = jnp.where(
        visible, d_weights * gate_prob * (1.0 + scores * (1.0 - gate_prob)) * norm_factor, 0.0
    ).astype(jnp.bfloat16)
    query_grad = (
        jnp.dot(d_scores, key_side[0], preferred_element_type=jnp.float32) * score_scale
    ).astype(jnp.bfloat16)
    key_grad = (
        jnp.einsum("qk,qh->kh", d_scores, query_side[0], preferred_element_type=jnp.float32)
        * score_scale
    ).astype(jnp.bfloat16)
    value_grad = jnp.einsum(
        "qk,qh->kh", weights, query_side[1], preferred_element_type=jnp.float32
    ).astype(jnp.bfloat16)
    return (query_grad, jnp.stack([key_grad, value_grad]))


def shards(queries, keys, values, out_grad, lengths, w_proj):
    tile_rows = queries.shape[0]
    device_count = lax.axis_size("seq")
    my_index = lax.axis_index("seq")
    user_ends = jnp.cumsum(lengths)
    all_tokens = tile_rows * device_count
    tile_start = my_index * tile_rows
    query_pair = jnp.stack([queries, out_grad])
    key_pair = jnp.stack([keys, values])

    def last_user(position):
        return jnp.sum((user_ends <= position).astype(jnp.int32))

    def live_pair(query_start, key_start):
        return (
            (key_start >= 0)
            & (query_start < all_tokens)
            & (last_user(query_start) == last_user(key_start + tile_rows - 1))
        )

    def zero_parts():
        return (jnp.zeros_like(queries), jnp.zeros_like(key_pair))

    def guarded(query_start, key_start, query_side, key_side):
        shared = live_pair(query_start, key_start)
        return lax.cond(
            shared,
            lambda: tile_task(query_side, key_side, query_start, key_start, user_ends),
            zero_parts,
        )

    query_grad, pair_grad = tile_task(query_pair, key_pair, tile_start, tile_start, user_ends)
    query_total = query_grad.astype(jnp.float32)
    pair_total = pair_grad.astype(jnp.float32)
    for offset in range(1, LAGS):
        if offset % 2 == 0:
            arrived = from_behind(key_pair, "seq", offset)
            query_part, pair_part = guarded(
                tile_start, tile_start - offset * tile_rows, query_pair, arrived
            )
            query_total = query_total + query_part.astype(jnp.float32)
            returned = from_behind(pair_part, "seq", -offset)
            pair_total = pair_total + returned.astype(jnp.float32)
        else:
            arrived = from_behind(query_pair, "seq", -offset)
            query_part, pair_part = guarded(
                tile_start + offset * tile_rows, tile_start, arrived, key_pair
            )
            pair_total = pair_total + pair_part.astype(jnp.float32)
            returned = from_behind(query_part, "seq", offset)
            query_total = query_total + returned.astype(jnp.float32)
    stacked_grads = jnp.stack([query_total, pair_total[0], pair_total[1]]).astype(jnp.bfloat16)
    return lax.psum_scatter(
        jnp.einsum("crh,cdh->rd", stacked_grads, w_proj, preferred_element_type=jnp.float32),
        "head",
        scatter_dimension=0,
        tiled=True,
    )


def solution(mesh):
    return jax.shard_map(
        shards,
        mesh=mesh,
        in_specs=(
            P("seq", "head"),
            P("seq", "head"),
            P("seq", "head"),
            P("seq", "head"),
            P(),
            P(None, None, "head"),
        ),
        out_specs=P(("seq", "head"), None),
        check_vma=False,
    )
```

profile of v0, /device:TPU:0, one launch (start us, length us, event | category | flops | bytes accessed | tf_op | source)
XLA Modules:
  0.0 123.3 jit_solution(16917143286057939371)
XLA Ops:
  6.5 0.0 copy-start
  6.5 0.0 reduce-scatter.2.cloned.1.call-start
  6.6 1.2 pad_maximum_fusion.1
  7.7 1.3 %collective-permute-start.3 = (bf16[2,1024,128]{2,1,0:T(8,128)(2,1)S(1)}, bf16[2,1024,128]{2,1,0:T(8,128)(2,1)}, u32[]{:S(2)}, u32[]{:S(2)}) collective-permute-start(bf16[2,1024,128]{2,1,0:T(8,128)(2,1)S(1)} %pad_maximum_fusion.1), channel_id=1, source_target_pairs={{12,0},{16,4},{20,8},{24,12},{28,16},{13,1},{17,5},{21,9},{25,13},... | collective-permute-start | bytes 1572872 | tf_op jit(solution)/shard_map/ppermute | solution.py:15
  9.0 1.3 %collective-permute-start = (bf16[2,1024,128]{2,1,0:T(8,128)(2,1)S(1)}, bf16[2,1024,128]{2,1,0:T(8,128)(2,1)}, u32[]{:S(2)}, u32[]{:S(2)}) collective-permute-start(bf16[2,1024,128]{2,1,0:T(8,128)(2,1)S(1)} %pad_maximum_fusion.1), channel_id=1, source_target_pairs={{4,0},{8,4},{12,8},{16,12},{20,16},{24,20},{28,24},{5,1},{9,5},{13... | collective-permute-start | bytes 1572872 | tf_op jit(solution)/shard_map/ppermute | solution.py:15
  10.3 1.1 pad_maximum_fusion.2
  11.4 7.0 %collective-permute-start.2 = (bf16[2,1024,128]{2,1,0:T(8,128)(2,1)S(1)}, bf16[2,1024,128]{2,1,0:T(8,128)(2,1)S(1)}, u32[]{:S(2)}, u32[]{:S(2)}) collective-permute-start(bf16[2,1024,128]{2,1,0:T(8,128)(2,1)S(1)} %pad_maximum_fusion.2), channel_id=1, source_target_pairs={{0,8},{4,12},{8,16},{12,20},{16,24},{20,28},{1,9},{5,13},{9,17},{1... | collective-permute-start | bytes 1572872 | tf_op jit(solution)/shard_map/ppermute | solution.py:15
  18.5 3.7 %fusion.77 = f32[1024,1024]{1,0:T(8,128)} fusion(bf16[1024,128]{1,0:T(8,128)(2,1)} %param.12, bf16[1024,128]{1,0:T(8,128)(2,1)} %param.13), kind=kOutput, calls=%fused_computation.128 | convolution fusion | flops 268435456 | bytes 4718592 | tf_op jit(solution)/shard_map/qh,kh->qk/dot_general | solution.py:34
  22.1 0.0 copy-done.7
  22.1 0.2 reduce-window.8
  22.3 0.8 fusion.67
  26.9 0.1 convert_reduce_fusion.6
  27.0 0.0 copy-done.5
  27.0 0.0 copy-done.6
  27.0 0.0 copy-start.2
  27.0 5.5 %select_convert_fusion.22 = bf16[1024,1024]{1,0:T(8,128)(2,1)} fusion(f32[1024,1024]{1,0:T(8,128)} %fusion.77, bf16[1024,128]{1,0:T(8,128)(2,1)S(1)} %copy-done.5, bf16[1024,128]{1,0:T(8,128)(2,1)S(1)} %copy-done.6, s32[1024]{0:T(1024)S(1)} %convert_reduce_fusion.6, s32[1024]{0:T(1024)S(1)} %iota_add_fusion.6), kind=kOutput, calls=%fused_computation.90 | convolution fusion | flops 284164096 | bytes 6823936 | tf_op jit(solution)/shard_map/qh,kh->qk/dot_general | solution.py:39
  32.5 0.0 copy-done.2
  32.5 2.9 %fusion.62 = bf16[1,1024,128]{2,1,0:T(8,128)(2,1)} fusion(bf16[1024,128]{1,0:T(8,128)(2,1)S(1)} %copy-done.5, f32[1024,1024]{1,0:T(8,128)S(1)} %copy-done.2, s32[1024]{0:T(1024)S(1)} %convert_reduce_fusion.6, s32[1024]{0:T(1024)S(1)} %iota_add_fusion.6), kind=kOutput, calls=%fused_computation.102 | convolution fusion | flops 280100864 | bytes 4726784 | tf_op jit(solution)/shard_map/qk,qh->kh/dot_general | solution.py:52
  35.4 0.0 collective-permute-done.2
  35.4 0.0 copy-done.3
  35.5 0.9 conditional.4
  35.5 0.9 broadcast.111
  36.4 1.3 %collective-permute-start.5 = (bf16[2,1024,128]{2,1,0:T(8,128)(2,1)}, bf16[2,1024,128]{2,1,0:T(8,128)(2,1)}, u32[]{:S(2)}, u32[]{:S(2)}) collective-permute-start(bf16[2,1024,128]{2,1,0:T(8,128)(2,1)} %get-tuple-element.72), channel_id=1, source_target_pairs={{8,0},{12,4},{16,8},{20,12},{24,16},{28,20},{9,1},{13,5},{17,9},{2... | collective-permute-start | bytes 1572872 | tf_op jit(solution)/shard_map/ppermute | solution.py:15
  37.7 0.0 collective-permute-done
  37.7 0.0 copy-done.1
  37.7 12.1 %conditional.3 = (bf16[1024,128]{1,0:T(8,128)(2,1)}, f32[2,1024,128]{2,1,0:T(8,128)S(1)}) conditional(s32[]{:T(128)} %convert_element_type.147, () %tuple.35, (s32[]{:T(128)}, s32[]{:T(128)}, s32[4]{0:T(128)S(1)}, bf16[2,1024,128]{2,1,0:T(8,128)(2,1)}, bf16[1024,128]{1,0:T(8,128)(2,1)S(1)}, /*index=5*/bf16[1024,128]{1,0:T(8,128)(2,1)S(1)}) %tuple.66), branch_computations={%region_4.5_spmd, %region_5.8_spmd} | conditional | flops 1370644480 | bytes 23126056 | solution.py:83
  37.9 0.1 convert_reduce_fusion.1
  38.0 1.7 %fusion.7 = f32[1024,1024]{1,0:T(8,128)S(1)} fusion(bf16[1024,128]{1,0:T(8,128)(2,1)S(1)} %get-tuple-element.49, bf16[2,1024,128]{2,1,0:T(8,128)(2,1)} %get-tuple-element.47), kind=kOutput, calls=%fused_computation.14 | convolution fusion | flops 268435456 | bytes 4718592 | tf_op jit(solution)/shard_map/cond/branch_1_fun/qh,kh->qk/dot_general | solution.py:34
  39.7 3.2 %fusion.5 = bf16[1,1024,128]{2,1,0:T(8,128)(2,1)S(1)} fusion(f32[1024,1024]{1,0:T(8,128)S(1)} %fusion.7, s32[1024]{0:T(1024)S(1)} %get-tuple-element.75, s32[1024]{0:T(1024)S(1)} %get-tuple-element.86, s32[1024]{0:T(1024)S(1)} %get-tuple-element.74, s32[1024]{0:T(1024)S(1)} %get-tuple-element.85, bf16[2,1024,128]{2,1,0:T(8,128)(2,1)} %get-tuple-element.47), kind=kOutput, calls=%fused_computation.11 | convolution fusion | flops 280100864 | bytes 4734976 | tf_op jit(solution)/shard_map/cond/branch_1_fun/qk,qh->kh/dot_general | solution.py:52
  42.8 3.7 %select_convert_fusion.1 = bf16[1024,1024]{1,0:T(8,128)(2,1)S(1)} fusion(f32[1024,1024]{1,0:T(8,128)S(1)} %fusion.7, bf16[1024,128]{1,0:T(8,128)(2,1)S(1)} %get-tuple-element.48, s32[1024]{0:T(1024)S(1)} %get-tuple-element.75, s32[1024]{0:T(1024)S(1)} %get-tuple-element.86, s32[1024]{0:T(1024)S(1)} %get-tuple-element.74, s32[1024]{0:T(1024)S(1)} %get-tuple-element.85, ...), kind=kOutput, calls=%fused_computation.1 | convolution fusion | flops 284164096 | bytes 6832128 | tf_op jit(solution)/shard_map/cond/branch_1_fun/qh,kh->qk/dot_general | solution.py:39
  46.5 1.7 %fusion.4 = bf16[1,1024,128]{2,1,0:T(8,128)(2,1)S(1)} fusion(bf16[1024,1024]{1,0:T(8,128)(2,1)S(1)} %select_convert_fusion.1, bf16[2,1024,128]{2,1,0:T(8,128)(2,1)} %get-tuple-element.47), kind=kOutput, calls=%fused_computation.10 | convolution fusion | flops 268697600 | bytes 2621440 | tf_op jit(solution)/shard_map/cond/branch_1_fun/qk,qh->kh/dot_general | solution.py:49
  48.2 1.4 %fusion.1 = bf16[1024,128]{1,0:T(8,128)(2,1)} fusion(bf16[1024,1024]{1,0:T(8,128)(2,1)S(1)} %select_convert_fusion.1, bf16[1024,128]{1,0:T(8,128)(2,1)S(1)} %get-tuple-element.49), kind=kOutput, calls=%fused_computation.7 | convolution fusion | flops 268697600 | bytes 2621440 | tf_op jit(solution)/shard_map/cond/branch_1_fun/dot_general | solution.py:46
  49.7 0.1 maximum_convert_fusion
  49.8 3.4 %collective-permute-start.1 = (bf16[1024,128]{1,0:T(8,128)(2,1)}, bf16[1024,128]{1,0:T(8,128)(2,1)}, u32[]{:S(2)}, u32[]{:S(2)}) collective-permute-start(bf16[1024,128]{1,0:T(8,128)(2,1)} %get-tuple-element.68), channel_id=1, source_target_pairs={{0,4},{4,8},{8,12},{12,16},{16,20},{20,24},{24,28},{1,5},{5,9},{9,... | collective-permute-start | bytes 786440 | tf_op jit(solution)/shard_map/ppermute | solution.py:15
  53.1 0.0 collective-permute-done.3
  53.1 0.1 conditional.5
  53.2 0.1 broadcast.118
  53.3 13.9 %collective-permute-start.4 = (bf16[1024,128]{1,0:T(8,128)(2,1)S(1)}, bf16[1024,128]{1,0:T(8,128)(2,1)S(1)}, u32[]{:S(2)}, u32[]{:S(2)}) collective-permute-start(bf16[1024,128]{1,0:T(8,128)(2,1)S(1)} %get-tuple-element.70), channel_id=1, source_target_pairs={{0,12},{4,16},{8,20},{12,24},{16,28},{1,13},{5,17},{9,21},{13,25},... | collective-permute-start | bytes 786440 | tf_op jit(solution)/shard_map/ppermute | solution.py:15
  67.2 2.3 %fusion.58 = f32[1024,128]{1,0:T(8,128)S(1)} fusion(bf16[1024,1024]{1,0:T(8,128)(2,1)} %select_convert_fusion.22, bf16[1024,128]{1,0:T(8,128)(2,1)S(1)} %copy-done.1), kind=kOutput, calls=%fused_computation.98 | convolution fusion | flops 268828672 | bytes 2883584 | tf_op jit(solution)/shard_map/dot_general | solution.py:46
  69.5 2.4 %fusion.61 = bf16[1,1024,128]{2,1,0:T(8,128)(2,1)S(1)} fusion(bf16[1024,1024]{1,0:T(8,128)(2,1)} %select_convert_fusion.22, bf16[1024,128]{1,0:T(8,128)(2,1)S(1)} %copy-done.3), kind=kOutput, calls=%fused_computation.101 | convolution fusion | flops 268697600 | bytes 2621440 | tf_op jit(solution)/shard_map/qk,qh->kh/dot_general | solution.py:49
  71.8 0.0 collective-permute-done.1
  71.8 0.0 collective-permute-done.4
  71.9 1.1 fusion.66
  72.9 0.0 collective-permute-done.5
  72.9 1.3 %add_convert_fusion = bf16[2,1024,128]{2,1,0:T(8,128)(2,1)S(1)} fusion(f32[2,1024,128]{2,1,0:T(8,128)S(1)} %get-tuple-element.73, bf16[2,1024,128]{2,1,0:T(8,128)(2,1)} %collective-permute-done.5, f32[2,1024,128]{2,1,0:T(8,128)S(1)} %get-tuple-element.71, bf16[1,1024,128]{2,1,0:T(8,128)(2,1)S(1)} %copy-done.4, bf16[1,1024,128]{2,1,0:T(8,128)(2,1)S(1)} %fusion.61), kind=kLoop, calls=%fused_computation.103 | loop fusion | flops 1835008 | bytes 3670016 | tf_op jit(solution)/shard_map/convert.1
  74.2 2.1 %convolution_bitcast_fusion = f32[1024,512]{1,0:T(8,128)} fusion(bf16[3,512,128]{2,1,0:T(8,128)(2,1)S(1)} %copy-done, bf16[2,1024,128]{2,1,0:T(8,128)(2,1)S(1)} %add_convert_fusion, bf16[1,1024,128]{2,1,0:T(8,128)(2,1)S(1)} %fusion.66), kind=kOutput, calls=%fused_computation.94 | convolution fusion | flops 403046400 | bytes 3276800 | tf_op jit(solution)/shard_map/crh,cdh->rd/dot_general | solution.py:111
  76.3 0.0 reduce-scatter.2.cloned.1.call-update
  76.3 40.2 %reduce-scatter.2.cloned.1.call-done = f32[256,512]{1,0:T(8,128)} async-done(((f32[1024,512]{1,0:T(8,128)}), f32[256,512]{1,0:T(8,128)}) %reduce-scatter.2.cloned.1.call-update) | async-done | bytes 524304 | tf_op jit(solution)/shard_map/reduce_scatter | solution.py:110
  (12 shorter events, 0.1 us)
Async XLA Ops:
  6.5 67.7 %copy-start = (bf16[3,512,128]{2,1,0:T(8,128)(2,1)S(1)}, bf16[3,512,128]{2,1,0:T(8,128)(2,1)}, u32[]{:S(2)}) copy-start(bf16[3,512,128]{2,1,0:T(8,128)(2,1)} %param.17) | copy-start | bytes 1179652
  6.5 20.5 %copy-start.5 = (bf16[1024,128]{1,0:T(8,128)(2,1)S(1)}, bf16[1024,128]{1,0:T(8,128)(2,1)}, u32[]{:S(2)}) copy-start(bf16[1024,128]{1,0:T(8,128)(2,1)} %param.15) | copy-start | bytes 786436
  6.5 20.5 %copy-start.6 = (bf16[1024,128]{1,0:T(8,128)(2,1)S(1)}, bf16[1024,128]{1,0:T(8,128)(2,1)}, u32[]{:S(2)}) copy-start(bf16[1024,128]{1,0:T(8,128)(2,1)} %param.14) | copy-start | bytes 786436
  6.5 15.6 %copy-start.7 = (s32[4]{0:T(128)S(1)}, s32[4]{0:T(128)}, u32[]{:S(2)}) copy-start(s32[4]{0:T(128)} %param.16) | copy-start | bytes 52
  6.5 110.0 %reduce-scatter.2.cloned.1.call-start = ((), (), s32[]{:S(2)}) async-start(), calls=%async_computation.1 | async-start | bytes 2621440 | tf_op jit(solution)/shard_map/reduce_scatter | solution.py:110
  7.7 45.4 %collective-permute-start.3 = (bf16[2,1024,128]{2,1,0:T(8,128)(2,1)S(1)}, bf16[2,1024,128]{2,1,0:T(8,128)(2,1)}, u32[]{:S(2)}, u32[]{:S(2)}) collective-permute-start(bf16[2,1024,128]{2,1,0:T(8,128)(2,1)S(1)} %pad_maximum_fusion.1), channel_id=1, source_target_pairs={{12,0},{16,4},{20,8},{24,12},{28,16},{13,1},{17,5},{21,9},{25,13},... | collective-permute-start | bytes 1572872 | tf_op jit(solution)/shard_map/ppermute | solution.py:15
  9.0 28.6 %collective-permute-start = (bf16[2,1024,128]{2,1,0:T(8,128)(2,1)S(1)}, bf16[2,1024,128]{2,1,0:T(8,128)(2,1)}, u32[]{:S(2)}, u32[]{:S(2)}) collective-permute-start(bf16[2,1024,128]{2,1,0:T(8,128)(2,1)S(1)} %pad_maximum_fusion.1), channel_id=1, source_target_pairs={{4,0},{8,4},{12,8},{16,12},{20,16},{24,20},{28,24},{5,1},{9,5},{13... | collective-permute-start | bytes 1572872 | tf_op jit(solution)/shard_map/ppermute | solution.py:15
  11.4 24.0 %collective-permute-start.2 = (bf16[2,1024,128]{2,1,0:T(8,128)(2,1)S(1)}, bf16[2,1024,128]{2,1,0:T(8,128)(2,1)S(1)}, u32[]{:S(2)}, u32[]{:S(2)}) collective-permute-start(bf16[2,1024,128]{2,1,0:T(8,128)(2,1)S(1)} %pad_maximum_fusion.2), channel_id=1, source_target_pairs={{0,8},{4,12},{8,16},{12,20},{16,24},{20,28},{1,9},{5,13},{9,17},{1... | collective-permute-start | bytes 1572872 | tf_op jit(solution)/shard_map/ppermute | solution.py:15
  27.0 5.5 %copy-start.2 = (f32[1024,1024]{1,0:T(8,128)S(1)}, f32[1024,1024]{1,0:T(8,128)}, u32[]{:S(2)}) copy-start(f32[1024,1024]{1,0:T(8,128)} %fusion.77) | copy-start | bytes 12582916
  32.5 2.9 %copy-start.3 = (bf16[1024,128]{1,0:T(8,128)(2,1)S(1)}, bf16[1024,128]{1,0:T(8,128)(2,1)}, u32[]{:S(2)}) copy-start(bf16[1024,128]{1,0:T(8,128)(2,1)} %param.12) | copy-start | bytes 786436
  35.4 2.2 %copy-start.1 = (bf16[1024,128]{1,0:T(8,128)(2,1)S(1)}, bf16[1024,128]{1,0:T(8,128)(2,1)}, u32[]{:S(2)}) copy-start(bf16[1024,128]{1,0:T(8,128)(2,1)} %param.13) | copy-start | bytes 786436
  36.4 36.5 %collective-permute-start.5 = (bf16[2,1024,128]{2,1,0:T(8,128)(2,1)}, bf16[2,1024,128]{2,1,0:T(8,128)(2,1)}, u32[]{:S(2)}, u32[]{:S(2)}) collective-permute-start(bf16[2,1024,128]{2,1,0:T(8,128)(2,1)} %get-tuple-element.72), channel_id=1, source_target_pairs={{8,0},{12,4},{16,8},{20,12},{24,16},{28,20},{9,1},{13,5},{17,9},{2... | collective-permute-start | bytes 1572872 | tf_op jit(solution)/shard_map/ppermute | solution.py:15
  49.8 22.1 %collective-permute-start.1 = (bf16[1024,128]{1,0:T(8,128)(2,1)}, bf16[1024,128]{1,0:T(8,128)(2,1)}, u32[]{:S(2)}, u32[]{:S(2)}) collective-permute-start(bf16[1024,128]{1,0:T(8,128)(2,1)} %get-tuple-element.68), channel_id=1, source_target_pairs={{0,4},{4,8},{8,12},{12,16},{16,20},{20,24},{24,28},{1,5},{5,9},{9,... | collective-permute-start | bytes 786440 | tf_op jit(solution)/shard_map/ppermute | solution.py:15
  53.3 19.7 %copy-start.4 = (bf16[1,1024,128]{2,1,0:T(8,128)(2,1)S(1)}, bf16[1,1024,128]{2,1,0:T(8,128)(2,1)}, u32[]{:S(2)}) copy-start(bf16[1,1024,128]{2,1,0:T(8,128)(2,1)} %fusion.62) | copy-start | bytes 786436
  53.3 18.6 %collective-permute-start.4 = (bf16[1024,128]{1,0:T(8,128)(2,1)S(1)}, bf16[1024,128]{1,0:T(8,128)(2,1)S(1)}, u32[]{:S(2)}, u32[]{:S(2)}) collective-permute-start(bf16[1024,128]{1,0:T(8,128)(2,1)S(1)} %get-tuple-element.70), channel_id=1, source_target_pairs={{0,12},{4,16},{8,20},{12,24},{16,28},{1,13},{5,17},{9,21},{13,25},... | collective-permute-start | bytes 786440 | tf_op jit(solution)/shard_map/ppermute | solution.py:15
Sparse Core Ops, SparseCore 0:
  76.5 39.9 reduce-scatter.1
where the time goes:
time: 124 us; the launch traced here: 123 us
  waiting for transfers between devices  40.2 us (32%)
  matrix products  30.5 us (25%)
  starting transfers between devices  28.2 us (23%)
  between operations  17.4 us (14%)
  other arithmetic  5.77 us (5%)
    reduce_scatter x1, waiting for transfers between devices, shards(): lax.psum_scatter(jnp.einsum('crh,cdh->rd', stacked_grads, w_proj, preferr...  40.2 us
    ppermute x6, starting transfers between devices, from_behind(): return lax.ppermute(value, axis, pairs)  28.2 us
    dot_general x2, matrix products, tile_task(): jnp.einsum('qh,kh->qk', query_side[1], key_side[1], preferred_element_typ...  9.18 us
    dot_general x2, matrix products, tile_task(): jnp.einsum('qk,qh->kh', weights, query_side[1], preferred_element_type=jn...  6.09 us
    dot_general x2, matrix products, tile_task(): jnp.einsum('qh,kh->qk', query_side[0], key_side[0], preferred_element_typ...  5.32 us
    dot_general x2, matrix products, tile_task(): jnp.einsum('qk,qh->kh', d_scores, query_side[0], preferred_element_type=j...  4.07 us
    dot_general x2, matrix products, tile_task(): jnp.dot(d_scores, key_side[0], preferred_element_type=jnp.float32)  3.73 us
  transfers between devices with their start and end apart: 7, of which 1 were waited for; matrix products, arithmetic and copies ran while one was open for 27% of the time, Pallas kernels for 0%

commit v1 on v0

v1 whole, which is shorter than its diff:
```python
import functools
import math

import jax
import jax.numpy as jnp
from jax import lax
from jax.experimental import pallas as pl
from jax.experimental.pallas import tpu as pltpu
from jax.sharding import PartitionSpec as P

MAXLEN = 3072
BLOCK = 512
F32 = jnp.float32
BF16 = jnp.bfloat16
VMEM = pl.BlockSpec(memory_space=pltpu.VMEM)
SMEM = pl.BlockSpec(memory_space=pltpu.SMEM)


def shift(value, axis, by):
    count = lax.axis_size(axis)
    pairs = [(i, i + by) for i in range(count) if 0 <= i + by < count]
    return lax.ppermute(value, axis, pairs)


def swap(value, axis, bit):
    count = lax.axis_size(axis)
    return lax.ppermute(value, axis, [(i, i ^ bit) for i in range(count)])


def user_bounds(lengths_ref, position):
    def step(u, carry):
        end, first, last = carry
        end = end + lengths_ref[u]
        past = end <= position
        return (
            end,
            jnp.where(past, end, first),
            jnp.where(past, last, jnp.minimum(last, end)),
        )

    zero = jnp.int32(0)
    _, first, last = lax.fori_loop(
        0, lengths_ref.shape[0], step, (zero, zero, jnp.int32(2**30))
    )
    return first, last


def pair_limits(lengths_ref, query_start, key_start, rows):
    first, last = user_bounds(lengths_ref, query_start)
    live = first <= key_start + rows - 1
    query_rows = jnp.where(live, jnp.minimum(last - query_start, rows), 0)
    key_row = jnp.maximum(first - key_start, 0)
    return query_rows, key_row


def scores(q, g, k, v, mask=None):
    nt = (((1,), (1,)), ((), ()))
    half = lax.dot_general(k, q, nt, preferred_element_type=F32) * (0.5 * q.shape[1] ** -0.5)
    da = lax.dot_general(v, g, nt, preferred_element_type=F32)
    t = jnp.tanh(half)
    p = half * t
    a = half + p
    f = (1.0 + t) * (1.0 + (half - p)) * da
    if mask is not None:
        a = jnp.where(mask, a, 0.0)
        f = jnp.where(mask, f, 0.0)
    return a.astype(BF16), f.astype(BF16)


def add_block(qs, ks, q, g, k, v, a, f, dq_ref, dk_ref, dv_ref):
    dv_ref[ks, :] += jnp.dot(a, g, preferred_element_type=F32)
    dk_ref[ks, :] += jnp.dot(f, q, preferred_element_type=F32)
    dq_ref[qs, :] += lax.dot_general(f, k, (((0,), (0,)), ((), ())), preferred_element_type=F32)


def sweep(q_ref, g_ref, k_ref, v_ref, dq_ref, dk_ref, dv_ref, query_rows, key_row, q0=0, nq=None, k0=0, nk=None):
    width = q_ref.shape[1]
    nk = k_ref.shape[0] // BLOCK if nk is None else nk
    zero = jnp.zeros((), BF16)

    def key_block(kb, carry):
        kk = pl.multiple_of(kb * BLOCK, BLOCK)
        ks = pl.ds(kk + k0, BLOCK)
        kept_keys = lax.broadcasted_iota(jnp.int32, (BLOCK, width), 0) + kk >= key_row

        def query_block(qb, carry):
            qq = pl.multiple_of(qb * BLOCK, BLOCK)
            qs = pl.ds(qq + q0, BLOCK)
            kept = lax.broadcasted_iota(jnp.int32, (BLOCK, width), 0) + qq < query_rows
            q = jnp.where(kept, q_ref[qs, :], zero)
            g = jnp.where(kept, g_ref[qs, :], zero)
            k = jnp.where(kept_keys, k_ref[ks, :], zero)
            v = jnp.where(kept_keys, v_ref[ks, :], zero)
            a, f = scores(q, g, k, v)
            add_block(qs, ks, q, g, k, v, a, f, dq_ref, dk_ref, dv_ref)
            return carry

        return lax.fori_loop(0, (query_rows + BLOCK - 1) // BLOCK, query_block, carry)

    first = jnp.where(query_rows > 0, key_row // BLOCK, nk)
    lax.fori_loop(first, nk, key_block, 0)


def own_kernel(lengths_ref, q_ref, g_ref, k_ref, v_ref, dq_ref, dk_ref, dv_ref):
    rows = q_ref.shape[0]
    start = lax.axis_index("seq") * rows
    dq_ref[...] = jnp.zeros_like(dq_ref)
    dk_ref[...] = jnp.zeros_like(dk_ref)
    dv_ref[...] = jnp.zeros_like(dv_ref)

    def diagonal(b, carry):
        off = pl.multiple_of(b * BLOCK, BLOCK)
        rs = pl.ds(off, BLOCK)
        query = lax.broadcasted_iota(jnp.int32, (1, BLOCK), 1) + start + off

        def step(u, carry):
            end, first = carry
            end = end + lengths_ref[u]
            return end, jnp.where(end <= query, end, first)

        _, first = lax.fori_loop(
            0, lengths_ref.shape[0], step, (jnp.int32(0), jnp.zeros((1, BLOCK), jnp.int32))
        )
        key = lax.broadcasted_iota(jnp.int32, (BLOCK, BLOCK), 0) + start + off
        mask = (key <= query) & (key >= first)
        q, g, k, v = q_ref[rs, :], g_ref[rs, :], k_ref[rs, :], v_ref[rs, :]
        a, f = scores(q, g, k, v, mask)
        add_block(rs, rs, q, g, k, v, a, f, dq_ref, dk_ref, dv_ref)
        return carry

    lax.fori_loop(0, rows // BLOCK, diagonal, 0)
    for b in range(1, rows // BLOCK):
        query_rows, key_row = pair_limits(lengths_ref, start + b * BLOCK, start + (b - 1) * BLOCK, BLOCK)
        key_row = jnp.where(
            query_rows > 0, jnp.maximum(user_bounds(lengths_ref, start + b * BLOCK)[0] - start, 0), 0
        )
        sweep(
            q_ref, g_ref, k_ref, v_ref, dq_ref, dk_ref, dv_ref, query_rows, key_row,
            q0=b * BLOCK, nk=b,
        )


def far_kernel(
    lengths_ref, q_ref, g_ref, qn_ref, gn_ref, k_ref, v_ref, dq_in,
    dq_ref, dqn_ref, dkv_ref, dk_ref, dv_ref,
):
    rows, width = q_ref.shape
    me = lax.axis_index("seq")
    dq_ref[...] = dq_in[...]
    dqn_ref[...] = jnp.zeros_like(dqn_ref)
    dk_ref[...] = jnp.zeros_like(dk_ref)
    dv_ref[...] = jnp.zeros_like(dv_ref)
    key_start = (me - 2) * rows
    near = pair_limits(lengths_ref, me * rows, key_start, rows)
    sweep(q_ref, g_ref, k_ref, v_ref, dq_ref, dk_ref, dv_ref, *near)
    far = pair_limits(lengths_ref, (me + 1) * rows, key_start, rows)
    sweep(qn_ref, gn_ref, k_ref, v_ref, dqn_ref, dk_ref, dv_ref, *far)
    norm = MAXLEN**-0.5
    dkv_ref[0] = (dk_ref[...] * (0.5 * norm * width**-0.5)).astype(BF16)
    dkv_ref[1] = (dv_ref[...] * norm).astype(BF16)


def next_kernel(
    lengths_ref, qn_ref, gn_ref, k_ref, v_ref, dqn_in, dk_in, dv_in,
    dqn_out, dk_ref, dv_ref, dqn_ref,
):
    rows, width = qn_ref.shape
    me = lax.axis_index("seq")
    dqn_ref[...] = dqn_in[...]
    dk_ref[...] = dk_in[...]
    dv_ref[...] = dv_in[...]
    limits = pair_limits(lengths_ref, (me + 1) * rows, me * rows, rows)
    sweep(qn_ref, gn_ref, k_ref, v_ref, dqn_ref, dk_ref, dv_ref, *limits)
    dqn_out[...] = (dqn_ref[...] * (0.5 * MAXLEN**-0.5 * width**-0.5)).astype(BF16)


def total_kernel(dq_ref, dk_ref, dv_ref, dq_got, dkv_got, keep_ref, send_ref):
    width = dq_ref.shape[1]
    block = keep_ref.shape[0] // 2
    norm = MAXLEN**-0.5
    inner = 0.5 * norm * width**-0.5
    low = lax.axis_index("head") % 2
    for out_ref, bit in ((send_ref, 1 - low), (keep_ref, low)):
        for high in range(2):
            src = pl.ds(pl.multiple_of((2 * high + bit) * block, block), block)
            dst = pl.ds(high * block, block)
            parts = (
                dq_ref[src, :] * inner + dq_got[src, :].astype(F32),
                dk_ref[src, :] * inner + dkv_got[0, src, :].astype(F32),
                dv_ref[src, :] * norm + dkv_got[1, src, :].astype(F32),
            )
            for c, part in enumerate(parts):
                out_ref[dst, c * width : (c + 1) * width] = part.astype(BF16)


def project_kernel(keep_ref, got_ref, w_ref, wp_ref, mine_ref, send_ref):
    width = w_ref.shape[2]
    block = mine_ref.shape[0]
    high = lax.axis_index("head") // 2

    def rows_of(index):
        src = pl.ds(pl.multiple_of(index * block, block), block)
        total = None
        for grads, weights in ((keep_ref, w_ref), (got_ref, wp_ref)):
            for c in range(3):
                part = lax.dot_general(
                    grads[src, c * width : (c + 1) * width], weights[c],
                    (((1,), (1,)), ((), ())), preferred_element_type=F32,
                )
                total = part if total is None else total + part
        return total

    send_ref[...] = rows_of(1 - high).astype(BF16)
    mine_ref[...] = rows_of(high)


def call(body, name, outs, args, flops, scratch=(), lengths=True):
    specs = [SMEM if lengths and n == 0 else VMEM for n in range(len(args))]
    moved = sum(math.prod(a.shape) * a.dtype.itemsize for a in (*args, *outs))
    return pl.pallas_call(
        body,
        name=name,
        out_shape=outs,
        in_specs=specs,
        out_specs=tuple(VMEM for _ in outs),
        scratch_shapes=scratch,
        compiler_params=pltpu.CompilerParams(vmem_limit_bytes=24 * 2**20),
        cost_estimate=pl.CostEstimate(flops=flops, bytes_accessed=moved, transcendentals=0),
    )(*args)


def shards(queries, keys, values, out_grad, lengths, w_proj):
    rows, width = queries.shape
    model = w_proj.shape[1]
    heads = lax.axis_size("head")
    like = jax.ShapeDtypeStruct
    wide = like((rows, width), F32)
    pair_flops = 10 * rows * rows * width

    keys_got = shift(keys, "seq", 2)
    values_got = shift(values, "seq", 2)
    queries_got = shift(queries, "seq", -1)
    grad_got = shift(out_grad, "seq", -1)
    w_got = swap(w_proj, "head", 1)

    dq, dk, dv = call(
        own_kernel, "own", (wide, wide, wide), (lengths, queries, out_grad, keys, values), pair_flops
    )
    dq, dqn, dkv = call(
        far_kernel, "far", (wide, wide, like((2, rows, width), BF16)),
        (lengths, queries, out_grad, queries_got, grad_got, keys_got, values_got, dq),
        pair_flops,
        scratch=[pltpu.VMEM((rows, width), F32), pltpu.VMEM((rows, width), F32)],
    )
    dkv_got = shift(dkv, "seq", -2)
    dqn, dk, dv = call(
        next_kernel, "next", (like((rows, width), BF16), wide, wide),
        (lengths, queries_got, grad_got, keys, values, dqn, dk, dv),
        pair_flops,
        scratch=[pltpu.VMEM((rows, width), F32)],
    )
    dq_got = shift(dqn, "seq", 1)

    block = rows // heads
    packed = like((2 * block, 3 * width), BF16)
    keep, send = call(
        total_kernel, "total", (packed, packed), (dq, dk, dv, dq_got, dkv_got), 1000, lengths=False
    )
    got = swap(send, "head", 1)
    mine, send = call(
        project_kernel, "project", (like((block, model), F32), like((block, model), BF16)),
        (keep, got, w_proj, w_got), 12 * block * width * model, lengths=False,
    )
    return mine + swap(send, "head", 2).astype(F32)


def solution(mesh):
    return jax.shard_map(
        shards,
        mesh=mesh,
        in_specs=(
            P("seq", "head"),
            P("seq", "head"),
            P("seq", "head"),
            P("seq", "head"),
            P(),
            P(None, None, "head"),
        ),
        out_specs=P(("seq", "head"), None),
        check_vma=False,
    )
```

time: 124 us -> 56.7 us (0.46)
  the two profiles are of different devices: /device:TPU:0 before, /device:TPU:18 now
where the time goes in v1:
time: 56.7 us; the launch traced here: 55.6 us
  waiting for transfers between devices  17.6 us (31%)
  Pallas kernels  16.8 us (30%)
  starting transfers between devices  15.7 us (28%)
  local copies, waits for them, and re-layouts  4.46 us (8%)
  other arithmetic  0.87 us (2%)
    pallas_call x5, Pallas kernels, call(): pl.pallas_call(body, name=name, out_shape=outs, in_specs=specs, out_specs...  16.8 us
    ppermute x6, starting transfers between devices, shift(): return lax.ppermute(value, axis, pairs)  15 us
    ppermute x3, waiting for transfers between devices, swap(): return lax.ppermute(value, axis, [(i, i ^ bit) for i in range(count)])  9.52 us
    ppermute x6, waiting for transfers between devices, shift(): return lax.ppermute(value, axis, pairs)  8.09 us
    unnamed x16, local copies, waits for them, and re-layouts  4.46 us
  transfers between devices with their start and end apart: 9, of which 4 were waited for; matrix products, arithmetic and copies ran while one was open for 0% of the time, Pallas kernels for 14%

profile of v1, /device:TPU:18, one launch (start us, length us, event | category | flops | bytes accessed | tf_op | source)
XLA Modules:
  0.0 55.6 jit_solution(15776411877633959186)
XLA Ops:
  0.0 3.3 %collective-permute-start = (bf16[1024,128]{1,0:T(8,128)(2,1)}, bf16[1024,128]{1,0:T(8,128)(2,1)S(1)}, u32[]{:S(2)}, u32[]{:S(2)}) collective-permute-start(bf16[1024,128]{1,0:T(8,128)(2,1)} %q_ref.3), channel_id=1, source_target_pairs={{4,0},{8,4},{12,8},{16,12},{20,16},{24,20},{28,24},{5,1},{9,5},{13... | collective-permute-start | bytes 786440 | tf_op jit(solution)/shard_map/ppermute | solution.py:22
  3.3 2.4 %collective-permute-start.1 = (bf16[1024,128]{1,0:T(8,128)(2,1)}, bf16[1024,128]{1,0:T(8,128)(2,1)S(1)}, u32[]{:S(2)}, u32[]{:S(2)}) collective-permute-start(bf16[1024,128]{1,0:T(8,128)(2,1)} %g_ref.3), channel_id=1, source_target_pairs={{4,0},{8,4},{12,8},{16,12},{20,16},{24,20},{28,24},{5,1},{9,5},{13... | collective-permute-start | bytes 786440 | tf_op jit(solution)/shard_map/ppermute | solution.py:22
  5.7 3.5 %collective-permute-start.2 = (bf16[1024,128]{1,0:T(8,128)(2,1)}, bf16[1024,128]{1,0:T(8,128)(2,1)S(1)}, u32[]{:S(2)}, u32[]{:S(2)}) collective-permute-start(bf16[1024,128]{1,0:T(8,128)(2,1)} %k_ref.3), channel_id=1, source_target_pairs={{0,8},{4,12},{8,16},{12,20},{16,24},{20,28},{1,9},{5,13},{9,17},{1... | collective-permute-start | bytes 786440 | tf_op jit(solution)/shard_map/ppermute | solution.py:22
  9.2 1.9 %collective-permute-start.3 = (bf16[1024,128]{1,0:T(8,128)(2,1)}, bf16[1024,128]{1,0:T(8,128)(2,1)S(1)}, u32[]{:S(2)}, u32[]{:S(2)}) collective-permute-start(bf16[1024,128]{1,0:T(8,128)(2,1)} %v_ref.3), channel_id=1, source_target_pairs={{0,8},{4,12},{8,16},{12,20},{16,24},{20,28},{1,9},{5,13},{9,17},{1... | collective-permute-start | bytes 786440 | tf_op jit(solution)/shard_map/ppermute | solution.py:22
  11.2 0.0 copy-start.1
  11.2 0.9 %copy-done.1 = bf16[1024,128]{1,0:T(8,128)(2,1)S(1)} copy-done((bf16[1024,128]{1,0:T(8,128)(2,1)S(1)}, bf16[1024,128]{1,0:T(8,128)(2,1)}, u32[]{:S(2)}) %copy-start.1) | copy-done | bytes 262168
  12.1 0.0 copy-start.2
  12.1 0.9 %copy-done.2 = bf16[1024,128]{1,0:T(8,128)(2,1)S(1)} copy-done((bf16[1024,128]{1,0:T(8,128)(2,1)S(1)}, bf16[1024,128]{1,0:T(8,128)(2,1)}, u32[]{:S(2)}) %copy-start.2) | copy-done | bytes 262168
  13.1 0.0 copy-start.3
  13.1 0.9 %copy-done.3 = bf16[1024,128]{1,0:T(8,128)(2,1)S(1)} copy-done((bf16[1024,128]{1,0:T(8,128)(2,1)S(1)}, bf16[1024,128]{1,0:T(8,128)(2,1)}, u32[]{:S(2)}) %copy-start.3) | copy-done | bytes 262168
  14.0 0.0 copy-start.5
  14.0 0.9 %copy-done.5 = bf16[1024,128]{1,0:T(8,128)(2,1)S(1)} copy-done((bf16[1024,128]{1,0:T(8,128)(2,1)S(1)}, bf16[1024,128]{1,0:T(8,128)(2,1)}, u32[]{:S(2)}) %copy-start.5) | copy-done | bytes 262168
  15.0 0.0 copy-start.7
  15.0 0.7 %copy-done.7 = s32[4]{0:T(128)S(1)} copy-done((s32[4]{0:T(128)S(1)}, s32[4]{0:T(128)}, u32[]{:S(2)}) %copy-start.7) | copy-done | bytes 40
  15.6 4.6 %own.1 = (f32[1024,128]{1,0:T(8,128)S(1)}, f32[1024,128]{1,0:T(8,128)S(1)}, f32[1024,128]{1,0:T(8,128)S(1)}) custom-call(s32[4]{0:T(128)S(1)} %copy-done.7, bf16[1024,128]{1,0:T(8,128)(2,1)S(1)} %copy-done.1, bf16[1024,128]{1,0:T(8,128)(2,1)S(1)} %copy-done.2, bf16[1024,128]{1,0:T(8,128)(2,1)S(1)} %copy-done.3, bf16[1024,128]{1,0:T(8,128)(2,1)S(1)} %copy-done.5), custom_call_target="tpu_custom_call" | custom-call | flops 1342177280 | bytes 2621456 | tf_op jit(solution)/shard_map/own/pallas_call | solution.py:220
  20.2 0.0 collective-permute-done.qn_ref
  20.2 0.0 collective-permute-done.1.gn_ref
  20.3 0.0 collective-permute-done.2.k_ref
  20.3 0.7 %collective-permute-done.3.v_ref = bf16[1024,128]{1,0:T(8,128)(2,1)S(1)} collective-permute-done((bf16[1024,128]{1,0:T(8,128)(2,1)}, bf16[1024,128]{1,0:T(8,128)(2,1)S(1)}, u32[]{:S(2)}, u32[]{:S(2)}) %collective-permute-start.3) | collective-permute-done | bytes 262176 | tf_op jit(solution)/shard_map/ppermute | solution.py:22
  20.9 0.0 copy-start.4
  20.9 0.0 copy-start.6
  20.9 7.9 %far.1 = (f32[1024,128]{1,0:T(8,128)S(1)}, f32[1024,128]{1,0:T(8,128)S(1)}, bf16[2,1024,128]{2,1,0:T(8,128)(2,1)S(1)}) custom-call(s32[4]{0:T(128)S(1)} %copy-done.7, bf16[1024,128]{1,0:T(8,128)(2,1)S(1)} %copy-done.1, bf16[1024,128]{1,0:T(8,128)(2,1)S(1)} %copy-done.2, bf16[1024,128]{1,0:T(8,128)(2,1)S(1)} %collective-permute-done.qn_ref, ...), custom_call_target="tpu_custom_call" | custom-call | flops 1342177280 | bytes 3670032 | tf_op jit(solution)/shard_map/far/pallas_call | solution.py:220
  28.8 1.9 %collective-permute-start.5 = (bf16[2,1024,128]{2,1,0:T(8,128)(2,1)S(1)}, bf16[2,1024,128]{2,1,0:T(8,128)(2,1)S(1)}, u32[]{:S(2)}, u32[]{:S(2)}) collective-permute-start(bf16[2,1024,128]{2,1,0:T(8,128)(2,1)S(1)} %get-tuple-element.26), channel_id=1, source_target_pairs={{8,0},{12,4},{16,8},{20,12},{24,16},{28,20},{9,1},{13,5},{17,9},{2... | collective-permute-start | bytes 1572872 | tf_op jit(solution)/shard_map/ppermute | solution.py:22
  30.8 0.0 copy-done.4
  30.8 0.0 copy-done.6
  30.8 0.0 copy-start
  30.8 3.1 %next.1 = (bf16[1024,128]{1,0:T(8,128)(2,1)S(1)}, f32[1024,128]{1,0:T(8,128)S(1)}, f32[1024,128]{1,0:T(8,128)S(1)}) custom-call(s32[4]{0:T(128)S(1)} %copy-done.7, bf16[1024,128]{1,0:T(8,128)(2,1)S(1)} %collective-permute-done.qn_ref, bf16[1024,128]{1,0:T(8,128)(2,1)S(1)} %collective-permute-done.1.gn_ref, bf16[1024,128]{1,0:T(8,128)(2,1)S(1)} %copy-done.4, ...), custom_call_target="tpu_custom_call" | custom-call | flops 1342177280 | bytes 3932176 | tf_op jit(solution)/shard_map/next/pallas_call | solution.py:220
  33.9 1.9 %collective-permute-start.4 = (bf16[1024,128]{1,0:T(8,128)(2,1)S(1)}, bf16[1024,128]{1,0:T(8,128)(2,1)S(1)}, u32[]{:S(2)}, u32[]{:S(2)}) collective-permute-start(bf16[1024,128]{1,0:T(8,128)(2,1)S(1)} %get-tuple-element.25), channel_id=1, source_target_pairs={{0,4},{4,8},{8,12},{12,16},{16,20},{20,24},{24,28},{1,5},{5,9},{9,... | collective-permute-start | bytes 786440 | tf_op jit(solution)/shard_map/ppermute | solution.py:22
  35.8 0.0 copy-done
  35.8 0.1 collective-permute-start.7
  35.9 7.4 %collective-permute-done.4.dq_got = bf16[1024,128]{1,0:T(8,128)(2,1)S(1)} collective-permute-done((bf16[1024,128]{1,0:T(8,128)(2,1)S(1)}, bf16[1024,128]{1,0:T(8,128)(2,1)S(1)}, u32[]{:S(2)}, u32[]{:S(2)}) %collective-permute-start.4) | collective-permute-done | bytes 262176 | tf_op jit(solution)/shard_map/ppermute | solution.py:22
  43.3 0.0 collective-permute-done.5.dkv_got
  43.3 0.2 total.1
  43.5 0.1 collective-permute-start.6
  43.6 0.0 collective-permute-done.7.wp_ref
  43.6 1.7 %collective-permute-done.6.got_ref = bf16[512,384]{1,0:T(8,128)(2,1)S(1)} collective-permute-done((bf16[512,384]{1,0:T(8,128)(2,1)S(1)}, bf16[512,384]{1,0:T(8,128)(2,1)S(1)}, u32[]{:S(2)}, u32[]{:S(2)}) %collective-permute-start.6) | collective-permute-done | bytes 393248 | tf_op jit(solution)/shard_map/ppermute | solution.py:27
  45.3 1.0 %project.1 = (f32[256,512]{1,0:T(8,128)S(1)}, bf16[256,512]{1,0:T(8,128)(2,1)S(1)}) custom-call(bf16[512,384]{1,0:T(8,128)(2,1)S(1)} %get-tuple-element.27.keep_ref, bf16[512,384]{1,0:T(8,128)(2,1)S(1)} %collective-permute-done.6.got_ref, bf16[3,512,128]{2,1,0:T(8,128)(2,1)S(1)} %copy-done, bf16[3,512,128]{2,1,0:T(8,128)(2,1)S(1)} %collective-permute-done.7.wp_ref), custom_call_target="tpu_custom_call" | custom-call | flops 201326592 | bytes 2359296 | tf_op jit(solution)/shard_map/project/pallas_call | solution.py:220
  46.3 0.6 %collective-permute-start.8 = (bf16[256,512]{1,0:T(8,128)(2,1)S(1)}, bf16[256,512]{1,0:T(8,128)(2,1)S(1)}, u32[]{:S(2)}, u32[]{:S(2)}) collective-permute-start(bf16[256,512]{1,0:T(8,128)(2,1)S(1)} %get-tuple-element.30), channel_id=1, source_target_pairs={{0,2},{1,3},{2,0},{3,1},{4,6},{5,7},{6,4},{7,5},{8,10},{9,11},{10,... | collective-permute-start | bytes 786440 | tf_op jit(solution)/shard_map/ppermute | solution.py:27
  46.9 7.8 %collective-permute-done.8 = bf16[256,512]{1,0:T(8,128)(2,1)S(1)} collective-permute-done((bf16[256,512]{1,0:T(8,128)(2,1)S(1)}, bf16[256,512]{1,0:T(8,128)(2,1)S(1)}, u32[]{:S(2)}, u32[]{:S(2)}) %collective-permute-start.8) | collective-permute-done | bytes 262176 | tf_op jit(solution)/shard_map/ppermute | solution.py:27
  54.7 0.9 %convert_add_fusion = f32[256,512]{1,0:T(8,128)} fusion(f32[256,512]{1,0:T(8,128)S(1)} %get-tuple-element.29, bf16[256,512]{1,0:T(8,128)(2,1)S(1)} %collective-permute-done.8), kind=kLoop, calls=%fused_computation | loop fusion | flops 262144 | bytes 1310720 | tf_op jit(solution)/shard_map/add | solution.py:274
Async XLA Ops:
  0.0 20.2 %collective-permute-start = (bf16[1024,128]{1,0:T(8,128)(2,1)}, bf16[1024,128]{1,0:T(8,128)(2,1)S(1)}, u32[]{:S(2)}, u32[]{:S(2)}) collective-permute-start(bf16[1024,128]{1,0:T(8,128)(2,1)} %q_ref.3), channel_id=1, source_target_pairs={{4,0},{8,4},{12,8},{16,12},{20,16},{24,20},{28,24},{5,1},{9,5},{13... | collective-permute-start | bytes 786440 | tf_op jit(solution)/shard_map/ppermute | solution.py:22
  3.3 16.9 %collective-permute-start.1 = (bf16[1024,128]{1,0:T(8,128)(2,1)}, bf16[1024,128]{1,0:T(8,128)(2,1)S(1)}, u32[]{:S(2)}, u32[]{:S(2)}) collective-permute-start(bf16[1024,128]{1,0:T(8,128)(2,1)} %g_ref.3), channel_id=1, source_target_pairs={{4,0},{8,4},{12,8},{16,12},{20,16},{24,20},{28,24},{5,1},{9,5},{13... | collective-permute-start | bytes 786440 | tf_op jit(solution)/shard_map/ppermute | solution.py:22
  5.7 14.5 %collective-permute-start.2 = (bf16[1024,128]{1,0:T(8,128)(2,1)}, bf16[1024,128]{1,0:T(8,128)(2,1)S(1)}, u32[]{:S(2)}, u32[]{:S(2)}) collective-permute-start(bf16[1024,128]{1,0:T(8,128)(2,1)} %k_ref.3), channel_id=1, source_target_pairs={{0,8},{4,12},{8,16},{12,20},{16,24},{20,28},{1,9},{5,13},{9,17},{1... | collective-permute-start | bytes 786440 | tf_op jit(solution)/shard_map/ppermute | solution.py:22
  9.2 11.7 %collective-permute-start.3 = (bf16[1024,128]{1,0:T(8,128)(2,1)}, bf16[1024,128]{1,0:T(8,128)(2,1)S(1)}, u32[]{:S(2)}, u32[]{:S(2)}) collective-permute-start(bf16[1024,128]{1,0:T(8,128)(2,1)} %v_ref.3), channel_id=1, source_target_pairs={{0,8},{4,12},{8,16},{12,20},{16,24},{20,28},{1,9},{5,13},{9,17},{1... | collective-permute-start | bytes 786440 | tf_op jit(solution)/shard_map/ppermute | solution.py:22
  11.2 1.0 %copy-start.1 = (bf16[1024,128]{1,0:T(8,128)(2,1)S(1)}, bf16[1024,128]{1,0:T(8,128)(2,1)}, u32[]{:S(2)}) copy-start(bf16[1024,128]{1,0:T(8,128)(2,1)} %q_ref.3) | copy-start | bytes 786436
  12.1 0.9 %copy-start.2 = (bf16[1024,128]{1,0:T(8,128)(2,1)S(1)}, bf16[1024,128]{1,0:T(8,128)(2,1)}, u32[]{:S(2)}) copy-start(bf16[1024,128]{1,0:T(8,128)(2,1)} %g_ref.3) | copy-start | bytes 786436
  13.1 0.9 %copy-start.3 = (bf16[1024,128]{1,0:T(8,128)(2,1)S(1)}, bf16[1024,128]{1,0:T(8,128)(2,1)}, u32[]{:S(2)}) copy-start(bf16[1024,128]{1,0:T(8,128)(2,1)} %k_ref.3) | copy-start | bytes 786436
  14.0 0.9 %copy-start.5 = (bf16[1024,128]{1,0:T(8,128)(2,1)S(1)}, bf16[1024,128]{1,0:T(8,128)(2,1)}, u32[]{:S(2)}) copy-start(bf16[1024,128]{1,0:T(8,128)(2,1)} %v_ref.3) | copy-start | bytes 786436
  15.0 0.7 %copy-start.7 = (s32[4]{0:T(128)S(1)}, s32[4]{0:T(128)}, u32[]{:S(2)}) copy-start(s32[4]{0:T(128)} %lengths_ref.5) | copy-start | bytes 52
  20.9 9.8 %copy-start.4 = (bf16[1024,128]{1,0:T(8,128)(2,1)S(1)}, bf16[1024,128]{1,0:T(8,128)(2,1)}, u32[]{:S(2)}) copy-start(bf16[1024,128]{1,0:T(8,128)(2,1)} %k_ref.3) | copy-start | bytes 786436
  20.9 9.8 %copy-start.6 = (bf16[1024,128]{1,0:T(8,128)(2,1)S(1)}, bf16[1024,128]{1,0:T(8,128)(2,1)}, u32[]{:S(2)}) copy-start(bf16[1024,128]{1,0:T(8,128)(2,1)} %v_ref.3) | copy-start | bytes 786436
  28.8 14.5 %collective-permute-start.5 = (bf16[2,1024,128]{2,1,0:T(8,128)(2,1)S(1)}, bf16[2,1024,128]{2,1,0:T(8,128)(2,1)S(1)}, u32[]{:S(2)}, u32[]{:S(2)}) collective-permute-start(bf16[2,1024,128]{2,1,0:T(8,128)(2,1)S(1)} %get-tuple-element.26), channel_id=1, source_target_pairs={{8,0},{12,4},{16,8},{20,12},{24,16},{28,20},{9,1},{13,5},{17,9},{2... | collective-permute-start | bytes 1572872 | tf_op jit(solution)/shard_map/ppermute | solution.py:22
  30.8 5.0 %copy-start = (bf16[3,512,128]{2,1,0:T(8,128)(2,1)S(1)}, bf16[3,512,128]{2,1,0:T(8,128)(2,1)}, u32[]{:S(2)}) copy-start(bf16[3,512,128]{2,1,0:T(8,128)(2,1)} %w_ref.1) | copy-start | bytes 1179652
  33.9 9.4 %collective-permute-start.4 = (bf16[1024,128]{1,0:T(8,128)(2,1)S(1)}, bf16[1024,128]{1,0:T(8,128)(2,1)S(1)}, u32[]{:S(2)}, u32[]{:S(2)}) collective-permute-start(bf16[1024,128]{1,0:T(8,128)(2,1)S(1)} %get-tuple-element.25), channel_id=1, source_target_pairs={{0,4},{4,8},{8,12},{12,16},{16,20},{20,24},{24,28},{1,5},{5,9},{9,... | collective-permute-start | bytes 786440 | tf_op jit(solution)/shard_map/ppermute | solution.py:22
  35.8 7.8 %collective-permute-start.7 = (bf16[3,512,128]{2,1,0:T(8,128)(2,1)S(1)}, bf16[3,512,128]{2,1,0:T(8,128)(2,1)S(1)}, u32[]{:S(2)}, u32[]{:S(2)}) collective-permute-start(bf16[3,512,128]{2,1,0:T(8,128)(2,1)S(1)} %copy-done), channel_id=1, source_target_pairs={{0,1},{1,0},{2,3},{3,2},{4,5},{5,4},{6,7},{7,6},{8,9},{9,8},{10,11... | collective-permute-start | bytes 1179656 | tf_op jit(solution)/shard_map/ppermute | solution.py:27
  43.5 1.8 %collective-permute-start.6 = (bf16[512,384]{1,0:T(8,128)(2,1)S(1)}, bf16[512,384]{1,0:T(8,128)(2,1)S(1)}, u32[]{:S(2)}, u32[]{:S(2)}) collective-permute-start(bf16[512,384]{1,0:T(8,128)(2,1)S(1)} %get-tuple-element.28), channel_id=1, source_target_pairs={{0,1},{1,0},{2,3},{3,2},{4,5},{5,4},{6,7},{7,6},{8,9},{9,8},{10,11... | collective-permute-start | bytes 1179656 | tf_op jit(solution)/shard_map/ppermute | solution.py:27
  46.3 8.4 %collective-permute-start.8 = (bf16[256,512]{1,0:T(8,128)(2,1)S(1)}, bf16[256,512]{1,0:T(8,128)(2,1)S(1)}, u32[]{:S(2)}, u32[]{:S(2)}) collective-permute-start(bf16[256,512]{1,0:T(8,128)(2,1)S(1)} %get-tuple-element.30), channel_id=1, source_target_pairs={{0,2},{1,3},{2,0},{3,1},{4,6},{5,7},{6,4},{7,5},{8,10},{9,11},{10,... | collective-permute-start | bytes 786440 | tf_op jit(solution)/shard_map/ppermute | solution.py:27

commit v2 on v1

v2 whole, which is shorter than its diff:
```python
import functools
import math

import jax
import jax.numpy as jnp
from jax import lax
from jax.experimental import pallas as pl
from jax.experimental.pallas import tpu as pltpu
from jax.sharding import PartitionSpec as P

MAXLEN = 3072
BLOCK = 512
F32 = jnp.float32
BF16 = jnp.bfloat16
VMEM = pl.BlockSpec(memory_space=pltpu.VMEM)
SMEM = pl.BlockSpec(memory_space=pltpu.SMEM)


def shift(value, by, flip=0):
    tiles, heads = lax.axis_size("seq"), lax.axis_size("head")
    pairs = [
        (t * heads + h, (t + by) * heads + (h ^ flip))
        for t in range(tiles)
        for h in range(heads)
        if 0 <= t + by < tiles
    ]
    return lax.ppermute(value, ("seq", "head"), pairs)


def user_bounds(lengths_ref, position):
    def step(u, carry):
        end, first, last = carry
        end = end + lengths_ref[u]
        past = end <= position
        return (
            end,
            jnp.where(past, end, first),
            jnp.where(past, last, jnp.minimum(last, end)),
        )

    zero = jnp.int32(0)
    _, first, last = lax.fori_loop(
        0, lengths_ref.shape[0], step, (zero, zero, jnp.int32(2**30))
    )
    return first, last


def pair_limits(lengths_ref, query_start, key_start, rows):
    first, last = user_bounds(lengths_ref, query_start)
    live = first <= key_start + rows - 1
    query_rows = jnp.where(live, jnp.minimum(last - query_start, rows), 0)
    key_row = jnp.maximum(first - key_start, 0)
    return query_rows, key_row


def scores(q, g, k, v, mask=None):
    nt = (((1,), (1,)), ((), ()))
    half = lax.dot_general(k, q, nt, preferred_element_type=F32) * (0.5 * q.shape[1] ** -0.5)
    da = lax.dot_general(v, g, nt, preferred_element_type=F32)
    t = jnp.tanh(half)
    p = half * t
    a = half + p
    f = (1.0 + t) * (1.0 + (half - p)) * da
    if mask is not None:
        a = jnp.where(mask, a, 0.0)
        f = jnp.where(mask, f, 0.0)
    return a.astype(BF16), f.astype(BF16)


def add_block(qs, ks, q, g, k, v, a, f, dq_ref, dk_ref, dv_ref):
    dv_ref[ks, :] += jnp.dot(a, g, preferred_element_type=F32)
    dk_ref[ks, :] += jnp.dot(f, q, preferred_element_type=F32)
    dq_ref[qs, :] += lax.dot_general(f, k, (((0,), (0,)), ((), ())), preferred_element_type=F32)


def sweep(q_ref, g_ref, k_ref, v_ref, dq_ref, dk_ref, dv_ref, query_rows, key_row, q0=0, nq=None, k0=0, nk=None):
    width = q_ref.shape[1]
    nk = k_ref.shape[0] // BLOCK if nk is None else nk
    zero = jnp.zeros((), BF16)

    def key_block(kb, carry):
        kk = pl.multiple_of(kb * BLOCK, BLOCK)
        ks = pl.ds(kk + k0, BLOCK)
        kept_keys = lax.broadcasted_iota(jnp.int32, (BLOCK, width), 0) + kk >= key_row

        def query_block(qb, carry):
            qq = pl.multiple_of(qb * BLOCK, BLOCK)
            qs = pl.ds(qq + q0, BLOCK)
            kept = lax.broadcasted_iota(jnp.int32, (BLOCK, width), 0) + qq < query_rows
            q = jnp.where(kept, q_ref[qs, :], zero)
            g = jnp.where(kept, g_ref[qs, :], zero)
            k = jnp.where(kept_keys, k_ref[ks, :], zero)
            v = jnp.where(kept_keys, v_ref[ks, :], zero)
            a, f = scores(q, g, k, v)
            add_block(qs, ks, q, g, k, v, a, f, dq_ref, dk_ref, dv_ref)
            return carry

        return lax.fori_loop(0, (query_rows + BLOCK - 1) // BLOCK, query_block, carry)

    first = jnp.where(query_rows > 0, key_row // BLOCK, nk)
    lax.fori_loop(first, nk, key_block, 0)


def pack_kernel(q_hbm, g_hbm, k_hbm, v_hbm, qg_ref, kv_ref, sems):
    copies = [
        pltpu.make_async_copy(q_hbm, qg_ref.at[0], sems.at[0]),
        pltpu.make_async_copy(g_hbm, qg_ref.at[1], sems.at[1]),
        pltpu.make_async_copy(k_hbm, kv_ref.at[0], sems.at[2]),
        pltpu.make_async_copy(v_hbm, kv_ref.at[1], sems.at[3]),
    ]
    for copy in copies:
        copy.start()
    for copy in copies:
        copy.wait()


def own_kernel(lengths_ref, qg_ref, kv_ref, dq_ref, dk_ref, dv_ref):
    q_ref, g_ref, k_ref, v_ref = qg_ref.at[0], qg_ref.at[1], kv_ref.at[0], kv_ref.at[1]
    rows = q_ref.shape[0]
    start = lax.axis_index("seq") * rows
    dq_ref[...] = jnp.zeros_like(dq_ref)
    dk_ref[...] = jnp.zeros_like(dk_ref)
    dv_ref[...] = jnp.zeros_like(dv_ref)

    def diagonal(b, carry):
        off = pl.multiple_of(b * BLOCK, BLOCK)
        rs = pl.ds(off, BLOCK)
        query = lax.broadcasted_iota(jnp.int32, (1, BLOCK), 1) + start + off

        def step(u, carry):
            end, first = carry
            end = end + lengths_ref[u]
            return end, jnp.where(end <= query, end, first)

        _, first = lax.fori_loop(
            0, lengths_ref.shape[0], step, (jnp.int32(0), jnp.zeros((1, BLOCK), jnp.int32))
        )
        key = lax.broadcasted_iota(jnp.int32, (BLOCK, BLOCK), 0) + start + off
        mask = (key <= query) & (key >= first)
        q, g, k, v = q_ref[rs, :], g_ref[rs, :], k_ref[rs, :], v_ref[rs, :]
        a, f = scores(q, g, k, v, mask)
        add_block(rs, rs, q, g, k, v, a, f, dq_ref, dk_ref, dv_ref)
        return carry

    lax.fori_loop(0, rows // BLOCK, diagonal, 0)
    for b in range(1, rows // BLOCK):
        query_rows, key_row = pair_limits(lengths_ref, start + b * BLOCK, start, b * BLOCK)
        query_rows = jnp.minimum(query_rows, BLOCK)
        sweep(
            q_ref, g_ref, k_ref, v_ref, dq_ref, dk_ref, dv_ref, query_rows, key_row,
            q0=b * BLOCK, nk=b,
        )


def next_kernel(lengths_ref, qgn_ref, kv_ref, dk_in, dv_in, dqn_ref, dk_ref, dv_ref):
    rows = qgn_ref.shape[1]
    me = lax.axis_index("seq")
    dqn_ref[...] = jnp.zeros_like(dqn_ref)
    dk_ref[...] = dk_in[...]
    dv_ref[...] = dv_in[...]
    limits = pair_limits(lengths_ref, (me + 1) * rows, me * rows, rows)
    sweep(
        qgn_ref.at[0], qgn_ref.at[1], kv_ref.at[0], kv_ref.at[1], dqn_ref, dk_ref, dv_ref, *limits
    )


def far_kernel(
    lengths_ref, qg_ref, qgn_ref, kv_ref, dq_in, dqn_in, dk_own, dv_own,
    keep_ref, send_ref, dq_same, dq_cross, dkv_same, dkv_cross,
    dq_ref, dqn_ref, dk_ref, dv_ref,
):
    rows, width = dq_in.shape
    me = lax.axis_index("seq")
    dq_ref[...] = dq_in[...]
    dqn_ref[...] = dqn_in[...]
    dk_ref[...] = jnp.zeros_like(dk_ref)
    dv_ref[...] = jnp.zeros_like(dv_ref)
    k_ref, v_ref = kv_ref.at[0], kv_ref.at[1]
    key_start = (me - 2) * rows
    near = pair_limits(lengths_ref, me * rows, key_start, rows)
    sweep(qg_ref.at[0], qg_ref.at[1], k_ref, v_ref, dq_ref, dk_ref, dv_ref, *near)
    far = pair_limits(lengths_ref, (me + 1) * rows, key_start, rows)
    sweep(qgn_ref.at[0], qgn_ref.at[1], k_ref, v_ref, dqn_ref, dk_ref, dv_ref, *far)

    norm = MAXLEN**-0.5
    inner = 0.5 * norm * width**-0.5
    block = dq_same.shape[0] // 2
    low = lax.axis_index("head") % 2
    for high in range(2):
        dst = pl.ds(high * block, block)
        for bit, dq_out, dkv_out, own_out in (
            (low, dq_same, dkv_same, keep_ref),
            (1 - low, dq_cross, dkv_cross, send_ref),
        ):
            src = pl.ds(pl.multiple_of((2 * high + bit) * block, block), block)
            dq_out[dst, :] = (dqn_ref[src, :] * inner).astype(BF16)
            dkv_out[0, dst, :] = (dk_ref[src, :] * inner).astype(BF16)
            dkv_out[1, dst, :] = (dv_ref[src, :] * norm).astype(BF16)
            own = (dq_ref[src, :] * inner, dk_own[src, :] * inner, dv_own[src, :] * norm)
            for c, part in enumerate(own):
                own_out[c, dst, :] = part.astype(own_out.dtype)


def project_kernel(
    keep_ref, got_ref, dq_same, dq_cross, dkv_same, dkv_cross, w_ref, wp_ref, mine_ref, send_ref
):
    block = mine_ref.shape[0]
    high = lax.axis_index("head") // 2

    def rows_of(index):
        src = pl.ds(pl.multiple_of(index * block, block), block)
        total = None
        for own, dq, dkv, weights in (
            (keep_ref, dq_same, dkv_same, w_ref),
            (got_ref, dq_cross, dkv_cross, wp_ref),
        ):
            arrived = (dq[src, :], dkv[0, src, :], dkv[1, src, :])
            for c, add in enumerate(arrived):
                grad = (own[c, src, :].astype(F32) + add.astype(F32)).astype(BF16)
                part = lax.dot_general(
                    grad, weights[c], (((1,), (1,)), ((), ())), preferred_element_type=F32
                )
                total = part if total is None else total + part
        return total

    send_ref[...] = rows_of(1 - high).astype(BF16)
    mine_ref[...] = rows_of(high)


def call(body, name, outs, args, flops, scratch=(), lengths=True, space=VMEM, limit=24):
    specs = [SMEM if lengths and n == 0 else space for n in range(len(args))]
    moved = sum(math.prod(a.shape) * a.dtype.itemsize for a in (*args, *outs))
    return pl.pallas_call(
        body,
        name=name,
        out_shape=outs,
        in_specs=specs,
        out_specs=tuple(VMEM for _ in outs),
        scratch_shapes=scratch,
        compiler_params=pltpu.CompilerParams(vmem_limit_bytes=limit * 2**20),
        cost_estimate=pl.CostEstimate(flops=flops, bytes_accessed=moved, transcendentals=0),
    )(*args)


def shards(queries, keys, values, out_grad, lengths, w_proj):
    rows, width = queries.shape
    model = w_proj.shape[1]
    heads = lax.axis_size("head")
    block = rows // heads
    like = jax.ShapeDtypeStruct
    wide = like((rows, width), F32)
    pair = like((2, rows, width), BF16)
    pair_flops = 10 * rows * rows * width

    query_grad, key_value = call(
        pack_kernel, "pack", (pair, pair), (queries, out_grad, keys, values), 1000,
        scratch=[pltpu.SemaphoreType.DMA((4,))], lengths=False,
        space=pl.BlockSpec(memory_space=pltpu.HBM), limit=60,
    )
    query_grad_got = shift(query_grad, -1)
    key_value_got = shift(key_value, 2)

    dq, dk, dv = call(
        own_kernel, "own", (wide, wide, wide), (lengths, query_grad, key_value), pair_flops
    )
    dqn, dk, dv = call(
        next_kernel, "next", (wide, wide, wide),
        (lengths, query_grad_got, key_value, dk, dv), pair_flops,
    )
    keep, send, dq_same, dq_cross, dkv_same, dkv_cross = call(
        far_kernel, "far",
        (
            like((3, 2 * block, width), F32), like((3, 2 * block, width), BF16),
            like((2 * block, width), BF16), like((2 * block, width), BF16),
            like((2, 2 * block, width), BF16), like((2, 2 * block, width), BF16),
        ),
        (lengths, query_grad, query_grad_got, key_value_got, dq, dqn, dk, dv),
        pair_flops,
        scratch=[pltpu.VMEM((rows, width), F32)] * 4,
    )
    dkv_same = shift(dkv_same, -2)
    dkv_cross = shift(dkv_cross, -2, 1)
    dq_same = shift(dq_same, 1)
    dq_cross = shift(dq_cross, 1, 1)
    got = shift(send, 0, 1)
    w_got = shift(w_proj, 0, 1)

    mine, send = call(
        project_kernel, "project", (like((block, model), F32), like((block, model), BF16)),
        (keep, got, dq_same, dq_cross, dkv_same, dkv_cross, w_proj, w_got),
        12 * block * width * model, lengths=False,
    )
    return mine + shift(send, 0, 2).astype(F32)


def solution(mesh):
    return jax.shard_map(
        shards,
        mesh=mesh,
        in_specs=(
            P("seq", "head"),
            P("seq", "head"),
            P("seq", "head"),
            P("seq", "head"),
            P(),
            P(None, None, "head"),
        ),
        out_specs=P(("seq", "head"), None),
        check_vma=False,
    )
```

time: 56.7 us -> 56 us (0.988)
  the two profiles are of different devices: /device:TPU:18 before, /device:TPU:0 now
where the time goes in v2:
time: 56 us; the launch traced here: 56.8 us
  starting transfers between devices  27.7 us (49%)
  waiting for transfers between devices  14.1 us (25%)
  Pallas kernels  11.8 us (21%)
  local copies, waits for them, and re-layouts  2.1 us (4%)
  other arithmetic  0.87 us (2%)
    ppermute x9, starting transfers between devices, shift(): return lax.ppermute(value, ('seq', 'head'), pairs)  27.7 us
    ppermute x9, waiting for transfers between devices, shift(): return lax.ppermute(value, ('seq', 'head'), pairs)  14.1 us
    pallas_call x5, Pallas kernels, call(): pl.pallas_call(body, name=name, out_shape=outs, in_specs=specs, out_specs...  11.8 us
    unnamed x12, local copies, waits for them, and re-layouts  2.1 us
  transfers between devices with their start and end apart: 9, of which 4 were waited for; matrix products, arithmetic and copies ran while one was open for 0% of the time, Pallas kernels for 15%

profile of v2, /device:TPU:0, one launch (start us, length us, event | category | flops | bytes accessed | tf_op | source)
XLA Modules:
  0.0 56.8 jit_solution(5291317431837361870)
XLA Ops:
  0.0 0.0 copy-start
  0.0 2.2 %pack.1 = (bf16[2,1024,128]{2,1,0:T(8,128)(2,1)}, bf16[2,1024,128]{2,1,0:T(8,128)(2,1)}) custom-call(bf16[1024,128]{1,0:T(8,128)(2,1)} %q_hbm.1, bf16[1024,128]{1,0:T(8,128)(2,1)} %g_hbm.1, bf16[1024,128]{1,0:T(8,128)(2,1)} %k_hbm.1, bf16[1024,128]{1,0:T(8,128)(2,1)} %v_hbm.1), custom_call_target="tpu_custom_call" | custom-call | flops 1000 | bytes 2097152 | tf_op jit(solution)/shard_map/pack/pallas_call | solution.py:233
  2.3 0.0 copy-start.5
  2.3 1.3 %collective-permute-start = (bf16[2,1024,128]{2,1,0:T(8,128)(2,1)}, bf16[2,1024,128]{2,1,0:T(8,128)(2,1)S(1)}, u32[]{:S(2)}, u32[]{:S(2)}) collective-permute-start(bf16[2,1024,128]{2,1,0:T(8,128)(2,1)} %get-tuple-element.21.qg_ref), channel_id=1, source_target_pairs={{4,0},{5,1},{6,2},{7,3},{8,4},{9,5},{10,6},{11,7},{12,8},{13,9},{1... | collective-permute-start | bytes 1572872 | tf_op jit(solution)/shard_map/ppermute | solution.py:27
  3.6 7.0 %collective-permute-start.1 = (bf16[2,1024,128]{2,1,0:T(8,128)(2,1)}, bf16[2,1024,128]{2,1,0:T(8,128)(2,1)S(1)}, u32[]{:S(2)}, u32[]{:S(2)}) collective-permute-start(bf16[2,1024,128]{2,1,0:T(8,128)(2,1)} %get-tuple-element.22.kv_ref), channel_id=1, source_target_pairs={{0,8},{1,9},{2,10},{3,11},{4,12},{5,13},{6,14},{7,15},{8,16},{9,17... | collective-permute-start | bytes 1572872 | tf_op jit(solution)/shard_map/ppermute | solution.py:27
  10.6 0.0 copy-done
  10.6 0.1 collective-permute-start.7
  10.7 0.0 copy-done.5
  10.7 0.0 copy-start.1
  10.7 1.0 %copy-done.1 = bf16[2,1024,128]{2,1,0:T(8,128)(2,1)S(1)} copy-done((bf16[2,1024,128]{2,1,0:T(8,128)(2,1)S(1)}, bf16[2,1024,128]{2,1,0:T(8,128)(2,1)}, u32[]{:S(2)}) %copy-start.1) | copy-done | bytes 524312
  11.7 0.0 copy-start.3
  11.7 1.0 %copy-done.3 = bf16[2,1024,128]{2,1,0:T(8,128)(2,1)S(1)} copy-done((bf16[2,1024,128]{2,1,0:T(8,128)(2,1)S(1)}, bf16[2,1024,128]{2,1,0:T(8,128)(2,1)}, u32[]{:S(2)}) %copy-start.3) | copy-done | bytes 524312
  12.8 0.0 copy-start.4
  12.8 4.5 %own.1 = (f32[1024,128]{1,0:T(8,128)S(1)}, f32[1024,128]{1,0:T(8,128)S(1)}, f32[1024,128]{1,0:T(8,128)S(1)}) custom-call(s32[4]{0:T(128)S(1)} %copy-done.5, bf16[2,1024,128]{2,1,0:T(8,128)(2,1)S(1)} %copy-done.1, bf16[2,1024,128]{2,1,0:T(8,128)(2,1)S(1)} %copy-done.3), custom_call_target="tpu_custom_call" | custom-call | flops 1342177280 | bytes 2621456 | tf_op jit(solution)/shard_map/own/pallas_call | solution.py:233
  17.3 2.0 %collective-permute-done.qgn_ref = bf16[2,1024,128]{2,1,0:T(8,128)(2,1)S(1)} collective-permute-done((bf16[2,1024,128]{2,1,0:T(8,128)(2,1)}, bf16[2,1024,128]{2,1,0:T(8,128)(2,1)S(1)}, u32[]{:S(2)}, u32[]{:S(2)}) %collective-permute-start) | collective-permute-done | bytes 524320 | tf_op jit(solution)/shard_map/ppermute | solution.py:27
  19.3 0.0 copy-done.4
  19.3 0.0 copy-start.2
  19.3 3.0 %next.1 = (f32[1024,128]{1,0:T(8,128)S(1)}, f32[1024,128]{1,0:T(8,128)S(1)}, f32[1024,128]{1,0:T(8,128)S(1)}) custom-call(s32[4]{0:T(128)S(1)} %copy-done.5, bf16[2,1024,128]{2,1,0:T(8,128)(2,1)S(1)} %collective-permute-done.qgn_ref, bf16[2,1024,128]{2,1,0:T(8,128)(2,1)S(1)} %copy-done.4, f32[1024,128]{1,0:T(8,128)S(1)} %get-tuple-element.24.dk_in, ...), custom_call_target="tpu_custom_call" | custom-call | flops 1342177280 | bytes 3670032 | tf_op jit(solution)/shard_map/next/pallas_call | solution.py:233
  22.3 0.0 collective-permute-done.1.kv_ref
  22.3 0.0 copy-done.2
  22.3 1.0 %far.1 = (f32[3,512,128]{2,1,0:T(8,128)S(1)}, bf16[3,512,128]{2,1,0:T(8,128)(2,1)S(1)}, bf16[512,128]{1,0:T(8,128)(2,1)S(1)}, bf16[512,128]{1,0:T(8,128)(2,1)S(1...) custom-call(s32[4]{0:T(128)S(1)} %copy-done.5, bf16[2,1024,128]{2,1,0:T(8,128)(2,1)S(1)} %copy-done.2, ...), custom_call_target="tpu_custom_call" | custom-call | flops 1342177280 | bytes 5636112 | tf_op jit(solution)/shard_map/far/pallas_call | solution.py:233
  23.4 0.1 collective-permute-start.2
  23.5 1.3 %collective-permute-start.5 = (bf16[2,512,128]{2,1,0:T(8,128)(2,1)S(1)}, bf16[2,512,128]{2,1,0:T(8,128)(2,1)S(1)}, u32[]{:S(2)}, u32[]{:S(2)}) collective-permute-start(bf16[2,512,128]{2,1,0:T(8,128)(2,1)S(1)} %get-tuple-element.33), channel_id=1, source_target_pairs={{8,0},{9,1},{10,2},{11,3},{12,4},{13,5},{14,6},{15,7},{16,8},{17,9... | collective-permute-start | bytes 786440 | tf_op jit(solution)/shard_map/ppermute | solution.py:27
  24.8 1.3 %collective-permute-start.6 = (bf16[2,512,128]{2,1,0:T(8,128)(2,1)S(1)}, bf16[2,512,128]{2,1,0:T(8,128)(2,1)S(1)}, u32[]{:S(2)}, u32[]{:S(2)}) collective-permute-start(bf16[2,512,128]{2,1,0:T(8,128)(2,1)S(1)} %get-tuple-element.34), channel_id=1, source_target_pairs={{8,1},{9,0},{10,3},{11,2},{12,5},{13,4},{14,7},{15,6},{16,9},{17,8... | collective-permute-start | bytes 786440 | tf_op jit(solution)/shard_map/ppermute | solution.py:27
  26.1 6.9 %collective-permute-start.3 = (bf16[512,128]{1,0:T(8,128)(2,1)S(1)}, bf16[512,128]{1,0:T(8,128)(2,1)S(1)}, u32[]{:S(2)}, u32[]{:S(2)}) collective-permute-start(bf16[512,128]{1,0:T(8,128)(2,1)S(1)} %get-tuple-element.31), channel_id=1, source_target_pairs={{0,4},{1,5},{2,6},{3,7},{4,8},{5,9},{6,10},{7,11},{8,12},{9,13},{1... | collective-permute-start | bytes 393224 | tf_op jit(solution)/shard_map/ppermute | solution.py:27
  32.9 0.0 collective-permute-done.7.wp_ref
  33.0 8.3 %collective-permute-start.4 = (bf16[512,128]{1,0:T(8,128)(2,1)S(1)}, bf16[512,128]{1,0:T(8,128)(2,1)S(1)}, u32[]{:S(2)}, u32[]{:S(2)}) collective-permute-start(bf16[512,128]{1,0:T(8,128)(2,1)S(1)} %get-tuple-element.32), channel_id=1, source_target_pairs={{0,5},{1,4},{2,7},{3,6},{4,9},{5,8},{6,11},{7,10},{8,13},{9,12},{1... | collective-permute-start | bytes 393224 | tf_op jit(solution)/shard_map/ppermute | solution.py:27
  41.2 0.0 collective-permute-done.3.dq_same
  41.2 3.5 %collective-permute-done.4.dq_cross = bf16[512,128]{1,0:T(8,128)(2,1)S(1)} collective-permute-done((bf16[512,128]{1,0:T(8,128)(2,1)S(1)}, bf16[512,128]{1,0:T(8,128)(2,1)S(1)}, u32[]{:S(2)}, u32[]{:S(2)}) %collective-permute-start.4) | collective-permute-done | bytes 131104 | tf_op jit(solution)/shard_map/ppermute | solution.py:27
  44.7 0.0 collective-permute-done.5.dkv_same
  44.7 1.8 %collective-permute-done.6.dkv_cross = bf16[2,512,128]{2,1,0:T(8,128)(2,1)S(1)} collective-permute-done((bf16[2,512,128]{2,1,0:T(8,128)(2,1)S(1)}, bf16[2,512,128]{2,1,0:T(8,128)(2,1)S(1)}, u32[]{:S(2)}, u32[]{:S(2)}) %collective-permute-start.6) | collective-permute-done | bytes 262176 | tf_op jit(solution)/shard_map/ppermute | solution.py:27
  46.5 0.0 collective-permute-done.2.got_ref
  46.5 1.0 %project.1 = (f32[256,512]{1,0:T(8,128)S(1)}, bf16[256,512]{1,0:T(8,128)(2,1)S(1)}) custom-call(f32[3,512,128]{2,1,0:T(8,128)S(1)} %get-tuple-element.29.keep_ref, bf16[3,512,128]{2,1,0:T(8,128)(2,1)S(1)} %collective-permute-done.2.got_ref, bf16[512,128]{1,0:T(8,128)(2,1)S(1)} %collective-permute-done.3.dq_same, ...), custom_call_target="tpu_custom_call" | custom-call | flops 201326592 | bytes 3538944 | tf_op jit(solution)/shard_map/project/pallas_call | solution.py:233
  47.5 1.6 %collective-permute-start.8 = (bf16[256,512]{1,0:T(8,128)(2,1)S(1)}, bf16[256,512]{1,0:T(8,128)(2,1)S(1)}, u32[]{:S(2)}, u32[]{:S(2)}) collective-permute-start(bf16[256,512]{1,0:T(8,128)(2,1)S(1)} %get-tuple-element.36), channel_id=1, source_target_pairs={{0,2},{1,3},{2,0},{3,1},{4,6},{5,7},{6,4},{7,5},{8,10},{9,11},{10,... | collective-permute-start | bytes 786440 | tf_op jit(solution)/shard_map/ppermute | solution.py:27
  49.1 6.8 %collective-permute-done.8 = bf16[256,512]{1,0:T(8,128)(2,1)S(1)} collective-permute-done((bf16[256,512]{1,0:T(8,128)(2,1)S(1)}, bf16[256,512]{1,0:T(8,128)(2,1)S(1)}, u32[]{:S(2)}, u32[]{:S(2)}) %collective-permute-start.8) | collective-permute-done | bytes 262176 | tf_op jit(solution)/shard_map/ppermute | solution.py:27
  55.9 0.9 %convert_add_fusion = f32[256,512]{1,0:T(8,128)} fusion(f32[256,512]{1,0:T(8,128)S(1)} %get-tuple-element.35, bf16[256,512]{1,0:T(8,128)(2,1)S(1)} %collective-permute-done.8), kind=kLoop, calls=%fused_computation | loop fusion | flops 262144 | bytes 1310720 | tf_op jit(solution)/shard_map/add | solution.py:293
Async XLA Ops:
  0.0 10.6 %copy-start = (bf16[3,512,128]{2,1,0:T(8,128)(2,1)S(1)}, bf16[3,512,128]{2,1,0:T(8,128)(2,1)}, u32[]{:S(2)}) copy-start(bf16[3,512,128]{2,1,0:T(8,128)(2,1)} %w_ref.1) | copy-start | bytes 1179652
  2.3 8.4 %copy-start.5 = (s32[4]{0:T(128)S(1)}, s32[4]{0:T(128)}, u32[]{:S(2)}) copy-start(s32[4]{0:T(128)} %lengths_ref.5) | copy-start | bytes 52
  2.3 17.0 %collective-permute-start = (bf16[2,1024,128]{2,1,0:T(8,128)(2,1)}, bf16[2,1024,128]{2,1,0:T(8,128)(2,1)S(1)}, u32[]{:S(2)}, u32[]{:S(2)}) collective-permute-start(bf16[2,1024,128]{2,1,0:T(8,128)(2,1)} %get-tuple-element.21.qg_ref), channel_id=1, source_target_pairs={{4,0},{5,1},{6,2},{7,3},{8,4},{9,5},{10,6},{11,7},{12,8},{13,9},{1... | collective-permute-start | bytes 1572872 | tf_op jit(solution)/shard_map/ppermute | solution.py:27
  3.6 18.8 %collective-permute-start.1 = (bf16[2,1024,128]{2,1,0:T(8,128)(2,1)}, bf16[2,1024,128]{2,1,0:T(8,128)(2,1)S(1)}, u32[]{:S(2)}, u32[]{:S(2)}) collective-permute-start(bf16[2,1024,128]{2,1,0:T(8,128)(2,1)} %get-tuple-element.22.kv_ref), channel_id=1, source_target_pairs={{0,8},{1,9},{2,10},{3,11},{4,12},{5,13},{6,14},{7,15},{8,16},{9,17... | collective-permute-start | bytes 1572872 | tf_op jit(solution)/shard_map/ppermute | solution.py:27
  10.6 22.4 %collective-permute-start.7 = (bf16[3,512,128]{2,1,0:T(8,128)(2,1)S(1)}, bf16[3,512,128]{2,1,0:T(8,128)(2,1)S(1)}, u32[]{:S(2)}, u32[]{:S(2)}) collective-permute-start(bf16[3,512,128]{2,1,0:T(8,128)(2,1)S(1)} %copy-done), channel_id=1, source_target_pairs={{0,1},{1,0},{2,3},{3,2},{4,5},{5,4},{6,7},{7,6},{8,9},{9,8},{10,11... | collective-permute-start | bytes 1179656 | tf_op jit(solution)/shard_map/ppermute | solution.py:27
  10.7 1.0 %copy-start.1 = (bf16[2,1024,128]{2,1,0:T(8,128)(2,1)S(1)}, bf16[2,1024,128]{2,1,0:T(8,128)(2,1)}, u32[]{:S(2)}) copy-start(bf16[2,1024,128]{2,1,0:T(8,128)(2,1)} %get-tuple-element.21.qg_ref) | copy-start | bytes 1572868
  11.7 1.0 %copy-start.3 = (bf16[2,1024,128]{2,1,0:T(8,128)(2,1)S(1)}, bf16[2,1024,128]{2,1,0:T(8,128)(2,1)}, u32[]{:S(2)}) copy-start(bf16[2,1024,128]{2,1,0:T(8,128)(2,1)} %get-tuple-element.22.kv_ref) | copy-start | bytes 1572868
  12.8 6.5 %copy-start.4 = (bf16[2,1024,128]{2,1,0:T(8,128)(2,1)S(1)}, bf16[2,1024,128]{2,1,0:T(8,128)(2,1)}, u32[]{:S(2)}) copy-start(bf16[2,1024,128]{2,1,0:T(8,128)(2,1)} %get-tuple-element.22.kv_ref) | copy-start | bytes 1572868
  19.3 3.0 %copy-start.2 = (bf16[2,1024,128]{2,1,0:T(8,128)(2,1)S(1)}, bf16[2,1024,128]{2,1,0:T(8,128)(2,1)}, u32[]{:S(2)}) copy-start(bf16[2,1024,128]{2,1,0:T(8,128)(2,1)} %get-tuple-element.21.qg_ref) | copy-start | bytes 1572868
  23.4 23.1 %collective-permute-start.2 = (bf16[3,512,128]{2,1,0:T(8,128)(2,1)S(1)}, bf16[3,512,128]{2,1,0:T(8,128)(2,1)S(1)}, u32[]{:S(2)}, u32[]{:S(2)}) collective-permute-start(bf16[3,512,128]{2,1,0:T(8,128)(2,1)S(1)} %get-tuple-element.30), channel_id=1, source_target_pairs={{0,1},{1,0},{2,3},{3,2},{4,5},{5,4},{6,7},{7,6},{8,9},{9,8},{10,11... | collective-permute-start | bytes 1179656 | tf_op jit(solution)/shard_map/ppermute | solution.py:27
  23.5 21.3 %collective-permute-start.5 = (bf16[2,512,128]{2,1,0:T(8,128)(2,1)S(1)}, bf16[2,512,128]{2,1,0:T(8,128)(2,1)S(1)}, u32[]{:S(2)}, u32[]{:S(2)}) collective-permute-start(bf16[2,512,128]{2,1,0:T(8,128)(2,1)S(1)} %get-tuple-element.33), channel_id=1, source_target_pairs={{8,0},{9,1},{10,2},{11,3},{12,4},{13,5},{14,6},{15,7},{16,8},{17,9... | collective-permute-start | bytes 786440 | tf_op jit(solution)/shard_map/ppermute | solution.py:27
  24.8 21.8 %collective-permute-start.6 = (bf16[2,512,128]{2,1,0:T(8,128)(2,1)S(1)}, bf16[2,512,128]{2,1,0:T(8,128)(2,1)S(1)}, u32[]{:S(2)}, u32[]{:S(2)}) collective-permute-start(bf16[2,512,128]{2,1,0:T(8,128)(2,1)S(1)} %get-tuple-element.34), channel_id=1, source_target_pairs={{8,1},{9,0},{10,3},{11,2},{12,5},{13,4},{14,7},{15,6},{16,9},{17,8... | collective-permute-start | bytes 786440 | tf_op jit(solution)/shard_map/ppermute | solution.py:27
  26.1 15.2 %collective-permute-start.3 = (bf16[512,128]{1,0:T(8,128)(2,1)S(1)}, bf16[512,128]{1,0:T(8,128)(2,1)S(1)}, u32[]{:S(2)}, u32[]{:S(2)}) collective-permute-start(bf16[512,128]{1,0:T(8,128)(2,1)S(1)} %get-tuple-element.31), channel_id=1, source_target_pairs={{0,4},{1,5},{2,6},{3,7},{4,8},{5,9},{6,10},{7,11},{8,12},{9,13},{1... | collective-permute-start | bytes 393224 | tf_op jit(solution)/shard_map/ppermute | solution.py:27
  33.0 11.8 %collective-permute-start.4 = (bf16[512,128]{1,0:T(8,128)(2,1)S(1)}, bf16[512,128]{1,0:T(8,128)(2,1)S(1)}, u32[]{:S(2)}, u32[]{:S(2)}) collective-permute-start(bf16[512,128]{1,0:T(8,128)(2,1)S(1)} %get-tuple-element.32), channel_id=1, source_target_pairs={{0,5},{1,4},{2,7},{3,6},{4,9},{5,8},{6,11},{7,10},{8,13},{9,12},{1... | collective-permute-start | bytes 393224 | tf_op jit(solution)/shard_map/ppermute | solution.py:27
  47.5 8.4 %collective-permute-start.8 = (bf16[256,512]{1,0:T(8,128)(2,1)S(1)}, bf16[256,512]{1,0:T(8,128)(2,1)S(1)}, u32[]{:S(2)}, u32[]{:S(2)}) collective-permute-start(bf16[256,512]{1,0:T(8,128)(2,1)S(1)} %get-tuple-element.36), channel_id=1, source_target_pairs={{0,2},{1,3},{2,0},{3,1},{4,6},{5,7},{6,4},{7,5},{8,10},{9,11},{10,... | collective-permute-start | bytes 786440 | tf_op jit(solution)/shard_map/ppermute | solution.py:27

commit v3 on v2

--- a/solution.py
+++ b/solution.py
@@ -253,9 +253,9 @@
     pair_flops = 10 * rows * rows * width
 
     query_grad, key_value = call(
-        pack_kernel, "pack", (pair, pair), (queries, out_grad, keys, values), 1000,
+        pack_kernel, "pack", (pair, pair), tuple(pltpu.with_memory_space_constraint(x, pltpu.HBM) for x in (queries, out_grad, keys, values)), 1000,
         scratch=[pltpu.SemaphoreType.DMA((4,))], lengths=False,
-        space=pl.BlockSpec(memory_space=pltpu.HBM), limit=60,
+        space=pl.BlockSpec(memory_space=pltpu.HBM),
     )
     query_grad_got = shift(query_grad, -1)
     key_value_got = shift(key_value, 2)

time: 56 us -> 53.5 us (0.955); the launches traced: 56.8 us -> 53.2 us
  starting transfers between devices: 27.7 us -> 23 us
  local copies, waits for them, and re-layouts: 2.1 us -> 0.01 us
  waiting for transfers between devices: 14.1 us -> 15.9 us
  Pallas kernels: 11.8 us -> 13.3 us
    ppermute x9, starting transfers between devices: 27.7 us -> 23 us  [shift(): return lax.ppermute(value, ('seq', 'head'), pairs)]
    unnamed x12 -> x4, local copies, waits for them, and re-layouts: 2.1 us -> 0.01 us
    ppermute x9, waiting for transfers between devices: 14.1 us -> 15.9 us  [shift(): return lax.ppermute(value, ('seq', 'head'), pairs)]
    pallas_call x5, Pallas kernels: 11.8 us -> 13.3 us  [call(): pl.pallas_call(body, name=name, out_shape=outs, in_specs=specs, out_specs...]
  transfers between devices with their start and end apart: 9 -> 9, of which waited for: 4 -> 4; matrix products, arithmetic and copies ran while one was open for 0% -> 0% of each run, Pallas kernels for 15% -> 21%
where the time goes in v3:
time: 53.5 us; the launch traced here: 53.2 us
  starting transfers between devices  23 us (43%)
  waiting for transfers between devices  15.9 us (30%)
  Pallas kernels  13.3 us (25%)
  other arithmetic  0.87 us (2%)
    ppermute x9, starting transfers between devices, shift(): return lax.ppermute(value, ('seq', 'head'), pairs)  23 us
    ppermute x9, waiting for transfers between devices, shift(): return lax.ppermute(value, ('seq', 'head'), pairs)  15.9 us
    pallas_call x5, Pallas kernels, call(): pl.pallas_call(body, name=name, out_shape=outs, in_specs=specs, out_specs...  13.3 us
  transfers between devices with their start and end apart: 9, of which 4 were waited for; matrix products, arithmetic and copies ran while one was open for 0% of the time, Pallas kernels for 21%

profile of v3, /device:TPU:0, one launch (start us, length us, event | category | flops | bytes accessed | tf_op | source)
XLA Modules:
  0.0 53.2 jit_solution(101345232664812229)
XLA Ops:
  0.0 0.0 copy-start
  0.0 1.3 %pack.1 = (bf16[2,1024,128]{2,1,0:T(8,128)(2,1)S(1)}, bf16[2,1024,128]{2,1,0:T(8,128)(2,1)S(1)}) custom-call(bf16[1024,128]{1,0:T(8,128)(2,1)} %q_hbm.1, bf16[1024,128]{1,0:T(8,128)(2,1)} %g_hbm.1, bf16[1024,128]{1,0:T(8,128)(2,1)} %k_hbm.1, bf16[1024,128]{1,0:T(8,128)(2,1)} %v_hbm.1), custom_call_target="tpu_custom_call" | custom-call | flops 1000 | bytes 2097152 | tf_op jit(solution)/shard_map/pack/pallas_call | solution.py:233
  1.3 0.0 copy-start.1
  1.3 1.3 %collective-permute-start = (bf16[2,1024,128]{2,1,0:T(8,128)(2,1)S(1)}, bf16[2,1024,128]{2,1,0:T(8,128)(2,1)S(1)}, u32[]{:S(2)}, u32[]{:S(2)}) collective-permute-start(bf16[2,1024,128]{2,1,0:T(8,128)(2,1)S(1)} %get-tuple-element.21.qg_ref), channel_id=1, source_target_pairs={{4,0},{5,1},{6,2},{7,3},{8,4},{9,5},{10,6},{11,7},{12,8},{13,9},{1... | collective-permute-start | bytes 1572872 | tf_op jit(solution)/shard_map/ppermute | solution.py:27
  2.6 7.0 %collective-permute-start.1 = (bf16[2,1024,128]{2,1,0:T(8,128)(2,1)S(1)}, bf16[2,1024,128]{2,1,0:T(8,128)(2,1)S(1)}, u32[]{:S(2)}, u32[]{:S(2)}) collective-permute-start(bf16[2,1024,128]{2,1,0:T(8,128)(2,1)S(1)} %get-tuple-element.22.kv_ref), channel_id=1, source_target_pairs={{0,8},{1,9},{2,10},{3,11},{4,12},{5,13},{6,14},{7,15},{8,16},{9,17... | collective-permute-start | bytes 1572872 | tf_op jit(solution)/shard_map/ppermute | solution.py:27
  9.6 0.0 copy-done
  9.6 0.1 collective-permute-start.7
  9.7 0.0 copy-done.1
  9.7 4.6 %own.1 = (f32[1024,128]{1,0:T(8,128)S(1)}, f32[1024,128]{1,0:T(8,128)S(1)}, f32[1024,128]{1,0:T(8,128)S(1)}) custom-call(s32[4]{0:T(128)S(1)} %copy-done.1, bf16[2,1024,128]{2,1,0:T(8,128)(2,1)S(1)} %get-tuple-element.21.qg_ref, bf16[2,1024,128]{2,1,0:T(8,128)(2,1)S(1)} %get-tuple-element.22.kv_ref), custom_call_target="tpu_custom_call" | custom-call | flops 1342177280 | bytes 2621456 | tf_op jit(solution)/shard_map/own/pallas_call | solution.py:233
  14.3 3.8 %collective-permute-done.qgn_ref = bf16[2,1024,128]{2,1,0:T(8,128)(2,1)S(1)} collective-permute-done((bf16[2,1024,128]{2,1,0:T(8,128)(2,1)S(1)}, bf16[2,1024,128]{2,1,0:T(8,128)(2,1)S(1)}, u32[]{:S(2)}, u32[]{:S(2)}) %collective-permute-start) | collective-permute-done | bytes 524320 | tf_op jit(solution)/shard_map/ppermute | solution.py:27
  18.1 5.4 %next.1 = (f32[1024,128]{1,0:T(8,128)S(1)}, f32[1024,128]{1,0:T(8,128)S(1)}, f32[1024,128]{1,0:T(8,128)S(1)}) custom-call(s32[4]{0:T(128)S(1)} %copy-done.1, bf16[2,1024,128]{2,1,0:T(8,128)(2,1)S(1)} %collective-permute-done.qgn_ref, bf16[2,1024,128]{2,1,0:T(8,128)(2,1)S(1)} %get-tuple-element.22.kv_ref, f32[1024,128]{1,0:T(8,128)S(1)} %get-tuple-element.24.dk_in, ...), custom_call_target="tpu_custom_call" | custom-call | flops 1342177280 | bytes 3670032 | tf_op jit(solution)/shard_map/next/pallas_call | solution.py:233
  23.5 0.0 collective-permute-done.1.kv_ref
  23.5 1.0 %far.1 = (f32[3,512,128]{2,1,0:T(8,128)S(1)}, bf16[3,512,128]{2,1,0:T(8,128)(2,1)S(1)}, bf16[512,128]{1,0:T(8,128)(2,1)S(1)}, bf16[512,128]{1,0:T(8,128)(2,1)S(1...) custom-call(s32[4]{0:T(128)S(1)} %copy-done.1, ...), custom_call_target="tpu_custom_call" | custom-call | flops 1342177280 | bytes 5636112 | tf_op jit(solution)/shard_map/far/pallas_call | solution.py:233
  24.5 0.1 collective-permute-start.2
  24.6 1.3 %collective-permute-start.5 = (bf16[2,512,128]{2,1,0:T(8,128)(2,1)S(1)}, bf16[2,512,128]{2,1,0:T(8,128)(2,1)S(1)}, u32[]{:S(2)}, u32[]{:S(2)}) collective-permute-start(bf16[2,512,128]{2,1,0:T(8,128)(2,1)S(1)} %get-tuple-element.33), channel_id=1, source_target_pairs={{8,0},{9,1},{10,2},{11,3},{12,4},{13,5},{14,6},{15,7},{16,8},{17,9... | collective-permute-start | bytes 786440 | tf_op jit(solution)/shard_map/ppermute | solution.py:27
  25.9 1.3 %collective-permute-start.6 = (bf16[2,512,128]{2,1,0:T(8,128)(2,1)S(1)}, bf16[2,512,128]{2,1,0:T(8,128)(2,1)S(1)}, u32[]{:S(2)}, u32[]{:S(2)}) collective-permute-start(bf16[2,512,128]{2,1,0:T(8,128)(2,1)S(1)} %get-tuple-element.34), channel_id=1, source_target_pairs={{8,1},{9,0},{10,3},{11,2},{12,5},{13,4},{14,7},{15,6},{16,9},{17,8... | collective-permute-start | bytes 786440 | tf_op jit(solution)/shard_map/ppermute | solution.py:27
  27.2 4.5 %collective-permute-start.3 = (bf16[512,128]{1,0:T(8,128)(2,1)S(1)}, bf16[512,128]{1,0:T(8,128)(2,1)S(1)}, u32[]{:S(2)}, u32[]{:S(2)}) collective-permute-start(bf16[512,128]{1,0:T(8,128)(2,1)S(1)} %get-tuple-element.31), channel_id=1, source_target_pairs={{0,4},{1,5},{2,6},{3,7},{4,8},{5,9},{6,10},{7,11},{8,12},{9,13},{1... | collective-permute-start | bytes 393224 | tf_op jit(solution)/shard_map/ppermute | solution.py:27
  31.8 0.0 collective-permute-done.7.wp_ref
  31.8 5.9 %collective-permute-start.4 = (bf16[512,128]{1,0:T(8,128)(2,1)S(1)}, bf16[512,128]{1,0:T(8,128)(2,1)S(1)}, u32[]{:S(2)}, u32[]{:S(2)}) collective-permute-start(bf16[512,128]{1,0:T(8,128)(2,1)S(1)} %get-tuple-element.32), channel_id=1, source_target_pairs={{0,5},{1,4},{2,7},{3,6},{4,9},{5,8},{6,11},{7,10},{8,13},{9,12},{1... | collective-permute-start | bytes 393224 | tf_op jit(solution)/shard_map/ppermute | solution.py:27
  37.7 0.0 collective-permute-done.3.dq_same
  37.7 3.5 %collective-permute-done.4.dq_cross = bf16[512,128]{1,0:T(8,128)(2,1)S(1)} collective-permute-done((bf16[512,128]{1,0:T(8,128)(2,1)S(1)}, bf16[512,128]{1,0:T(8,128)(2,1)S(1)}, u32[]{:S(2)}, u32[]{:S(2)}) %collective-permute-start.4) | collective-permute-done | bytes 131104 | tf_op jit(solution)/shard_map/ppermute | solution.py:27
  41.2 0.0 collective-permute-done.5.dkv_same
  41.2 1.8 %collective-permute-done.6.dkv_cross = bf16[2,512,128]{2,1,0:T(8,128)(2,1)S(1)} collective-permute-done((bf16[2,512,128]{2,1,0:T(8,128)(2,1)S(1)}, bf16[2,512,128]{2,1,0:T(8,128)(2,1)S(1)}, u32[]{:S(2)}, u32[]{:S(2)}) %collective-permute-start.6) | collective-permute-done | bytes 262176 | tf_op jit(solution)/shard_map/ppermute | solution.py:27
  43.0 0.0 collective-permute-done.2.got_ref
  43.0 1.0 %project.1 = (f32[256,512]{1,0:T(8,128)S(1)}, bf16[256,512]{1,0:T(8,128)(2,1)S(1)}) custom-call(f32[3,512,128]{2,1,0:T(8,128)S(1)} %get-tuple-element.29.keep_ref, bf16[3,512,128]{2,1,0:T(8,128)(2,1)S(1)} %collective-permute-done.2.got_ref, bf16[512,128]{1,0:T(8,128)(2,1)S(1)} %collective-permute-done.3.dq_same, ...), custom_call_target="tpu_custom_call" | custom-call | flops 201326592 | bytes 3538944 | tf_op jit(solution)/shard_map/project/pallas_call | solution.py:233
  44.0 1.6 %collective-permute-start.8 = (bf16[256,512]{1,0:T(8,128)(2,1)S(1)}, bf16[256,512]{1,0:T(8,128)(2,1)S(1)}, u32[]{:S(2)}, u32[]{:S(2)}) collective-permute-start(bf16[256,512]{1,0:T(8,128)(2,1)S(1)} %get-tuple-element.36), channel_id=1, source_target_pairs={{0,2},{1,3},{2,0},{3,1},{4,6},{5,7},{6,4},{7,5},{8,10},{9,11},{10,... | collective-permute-start | bytes 786440 | tf_op jit(solution)/shard_map/ppermute | solution.py:27
  45.5 6.8 %collective-permute-done.8 = bf16[256,512]{1,0:T(8,128)(2,1)S(1)} collective-permute-done((bf16[256,512]{1,0:T(8,128)(2,1)S(1)}, bf16[256,512]{1,0:T(8,128)(2,1)S(1)}, u32[]{:S(2)}, u32[]{:S(2)}) %collective-permute-start.8) | collective-permute-done | bytes 262176 | tf_op jit(solution)/shard_map/ppermute | solution.py:27
  52.4 0.9 %convert_add_fusion = f32[256,512]{1,0:T(8,128)} fusion(f32[256,512]{1,0:T(8,128)S(1)} %get-tuple-element.35, bf16[256,512]{1,0:T(8,128)(2,1)S(1)} %collective-permute-done.8), kind=kLoop, calls=%fused_computation | loop fusion | flops 262144 | bytes 1310720 | tf_op jit(solution)/shard_map/add | solution.py:293
Async XLA Ops:
  0.0 9.6 %copy-start = (bf16[3,512,128]{2,1,0:T(8,128)(2,1)S(1)}, bf16[3,512,128]{2,1,0:T(8,128)(2,1)}, u32[]{:S(2)}) copy-start(bf16[3,512,128]{2,1,0:T(8,128)(2,1)} %w_ref.1) | copy-start | bytes 1179652
  1.3 8.4 %copy-start.1 = (s32[4]{0:T(128)S(1)}, s32[4]{0:T(128)}, u32[]{:S(2)}) copy-start(s32[4]{0:T(128)} %lengths_ref.5) | copy-start | bytes 52
  1.3 16.8 %collective-permute-start = (bf16[2,1024,128]{2,1,0:T(8,128)(2,1)S(1)}, bf16[2,1024,128]{2,1,0:T(8,128)(2,1)S(1)}, u32[]{:S(2)}, u32[]{:S(2)}) collective-permute-start(bf16[2,1024,128]{2,1,0:T(8,128)(2,1)S(1)} %get-tuple-element.21.qg_ref), channel_id=1, source_target_pairs={{4,0},{5,1},{6,2},{7,3},{8,4},{9,5},{10,6},{11,7},{12,8},{13,9},{1... | collective-permute-start | bytes 1572872 | tf_op jit(solution)/shard_map/ppermute | solution.py:27
  2.6 20.9 %collective-permute-start.1 = (bf16[2,1024,128]{2,1,0:T(8,128)(2,1)S(1)}, bf16[2,1024,128]{2,1,0:T(8,128)(2,1)S(1)}, u32[]{:S(2)}, u32[]{:S(2)}) collective-permute-start(bf16[2,1024,128]{2,1,0:T(8,128)(2,1)S(1)} %get-tuple-element.22.kv_ref), channel_id=1, source_target_pairs={{0,8},{1,9},{2,10},{3,11},{4,12},{5,13},{6,14},{7,15},{8,16},{9,17... | collective-permute-start | bytes 1572872 | tf_op jit(solution)/shard_map/ppermute | solution.py:27
  9.6 22.2 %collective-permute-start.7 = (bf16[3,512,128]{2,1,0:T(8,128)(2,1)S(1)}, bf16[3,512,128]{2,1,0:T(8,128)(2,1)S(1)}, u32[]{:S(2)}, u32[]{:S(2)}) collective-permute-start(bf16[3,512,128]{2,1,0:T(8,128)(2,1)S(1)} %copy-done), channel_id=1, source_target_pairs={{0,1},{1,0},{2,3},{3,2},{4,5},{5,4},{6,7},{7,6},{8,9},{9,8},{10,11... | collective-permute-start | bytes 1179656 | tf_op jit(solution)/shard_map/ppermute | solution.py:27
  24.5 18.4 %collective-permute-start.2 = (bf16[3,512,128]{2,1,0:T(8,128)(2,1)S(1)}, bf16[3,512,128]{2,1,0:T(8,128)(2,1)S(1)}, u32[]{:S(2)}, u32[]{:S(2)}) collective-permute-start(bf16[3,512,128]{2,1,0:T(8,128)(2,1)S(1)} %get-tuple-element.30), channel_id=1, source_target_pairs={{0,1},{1,0},{2,3},{3,2},{4,5},{5,4},{6,7},{7,6},{8,9},{9,8},{10,11... | collective-permute-start | bytes 1179656 | tf_op jit(solution)/shard_map/ppermute | solution.py:27
  24.6 16.6 %collective-permute-start.5 = (bf16[2,512,128]{2,1,0:T(8,128)(2,1)S(1)}, bf16[2,512,128]{2,1,0:T(8,128)(2,1)S(1)}, u32[]{:S(2)}, u32[]{:S(2)}) collective-permute-start(bf16[2,512,128]{2,1,0:T(8,128)(2,1)S(1)} %get-tuple-element.33), channel_id=1, source_target_pairs={{8,0},{9,1},{10,2},{11,3},{12,4},{13,5},{14,6},{15,7},{16,8},{17,9... | collective-permute-start | bytes 786440 | tf_op jit(solution)/shard_map/ppermute | solution.py:27
  25.9 17.1 %collective-permute-start.6 = (bf16[2,512,128]{2,1,0:T(8,128)(2,1)S(1)}, bf16[2,512,128]{2,1,0:T(8,128)(2,1)S(1)}, u32[]{:S(2)}, u32[]{:S(2)}) collective-permute-start(bf16[2,512,128]{2,1,0:T(8,128)(2,1)S(1)} %get-tuple-element.34), channel_id=1, source_target_pairs={{8,1},{9,0},{10,3},{11,2},{12,5},{13,4},{14,7},{15,6},{16,9},{17,8... | collective-permute-start | bytes 786440 | tf_op jit(solution)/shard_map/ppermute | solution.py:27
  27.2 10.5 %collective-permute-start.3 = (bf16[512,128]{1,0:T(8,128)(2,1)S(1)}, bf16[512,128]{1,0:T(8,128)(2,1)S(1)}, u32[]{:S(2)}, u32[]{:S(2)}) collective-permute-start(bf16[512,128]{1,0:T(8,128)(2,1)S(1)} %get-tuple-element.31), channel_id=1, source_target_pairs={{0,4},{1,5},{2,6},{3,7},{4,8},{5,9},{6,10},{7,11},{8,12},{9,13},{1... | collective-permute-start | bytes 393224 | tf_op jit(solution)/shard_map/ppermute | solution.py:27
  31.8 9.4 %collective-permute-start.4 = (bf16[512,128]{1,0:T(8,128)(2,1)S(1)}, bf16[512,128]{1,0:T(8,128)(2,1)S(1)}, u32[]{:S(2)}, u32[]{:S(2)}) collective-permute-start(bf16[512,128]{1,0:T(8,128)(2,1)S(1)} %get-tuple-element.32), channel_id=1, source_target_pairs={{0,5},{1,4},{2,7},{3,6},{4,9},{5,8},{6,11},{7,10},{8,13},{9,12},{1... | collective-permute-start | bytes 393224 | tf_op jit(solution)/shard_map/ppermute | solution.py:27
  44.0 8.4 %collective-permute-start.8 = (bf16[256,512]{1,0:T(8,128)(2,1)S(1)}, bf16[256,512]{1,0:T(8,128)(2,1)S(1)}, u32[]{:S(2)}, u32[]{:S(2)}) collective-permute-start(bf16[256,512]{1,0:T(8,128)(2,1)S(1)} %get-tuple-element.36), channel_id=1, source_target_pairs={{0,2},{1,3},{2,0},{3,1},{4,6},{5,7},{6,4},{7,5},{8,10},{9,11},{10,... | collective-permute-start | bytes 786440 | tf_op jit(solution)/shard_map/ppermute | solution.py:27

commit v4 on v3

--- a/solution.py
+++ b/solution.py
@@ -1,4 +1,3 @@
-import functools
 import math
 
 import jax
@@ -7,6 +6,7 @@
 from jax.experimental import pallas as pl
 from jax.experimental.pallas import tpu as pltpu
 from jax.sharding import PartitionSpec as P
+
 
 MAXLEN = 3072
 BLOCK = 512
@@ -67,7 +67,7 @@
     return a.astype(BF16), f.astype(BF16)
 
 
-def add_block(qs, ks, q, g, k, v, a, f, dq_ref, dk_ref, dv_ref):
+def add_block(qs, ks, q, g, k, a, f, dq_ref, dk_ref, dv_ref):
     dv_ref[ks, :] += jnp.dot(a, g, preferred_element_type=F32)
     dk_ref[ks, :] += jnp.dot(f, q, preferred_element_type=F32)
     dq_ref[qs, :] += lax.dot_general(f, k, (((0,), (0,)), ((), ())), preferred_element_type=F32)
@@ -92,7 +92,7 @@
             k = jnp.where(kept_keys, k_ref[ks, :], zero)
             v = jnp.where(kept_keys, v_ref[ks, :], zero)
             a, f = scores(q, g, k, v)
-            add_block(qs, ks, q, g, k, v, a, f, dq_ref, dk_ref, dv_ref)
+            add_block(qs, ks, q, g, k, a, f, dq_ref, dk_ref, dv_ref)
             return carry
 
         return lax.fori_loop(0, (query_rows + BLOCK - 1) // BLOCK, query_block, carry)
@@ -139,7 +139,7 @@
         mask = (key <= query) & (key >= first)
         q, g, k, v = q_ref[rs, :], g_ref[rs, :], k_ref[rs, :], v_ref[rs, :]
         a, f = scores(q, g, k, v, mask)
-        add_block(rs, rs, q, g, k, v, a, f, dq_ref, dk_ref, dv_ref)
+        add_block(rs, rs, q, g, k, a, f, dq_ref, dk_ref, dv_ref)
         return carry
 
     lax.fori_loop(0, rows // BLOCK, diagonal, 0)
@@ -184,55 +184,68 @@
 
     norm = MAXLEN**-0.5
     inner = 0.5 * norm * width**-0.5
-    block = dq_same.shape[0] // 2
-    low = lax.axis_index("head") % 2
-    for high in range(2):
-        dst = pl.ds(high * block, block)
-        for bit, dq_out, dkv_out, own_out in (
-            (low, dq_same, dkv_same, keep_ref),
-            (1 - low, dq_cross, dkv_cross, send_ref),
-        ):
-            src = pl.ds(pl.multiple_of((2 * high + bit) * block, block), block)
-            dq_out[dst, :] = (dqn_ref[src, :] * inner).astype(BF16)
-            dkv_out[0, dst, :] = (dk_ref[src, :] * inner).astype(BF16)
-            dkv_out[1, dst, :] = (dv_ref[src, :] * norm).astype(BF16)
+    half = dq_same.shape[0]
+    block = half // 2
+    head = lax.axis_index("head")
+    high, low = head // 2, head % 2
+    for bit, dq_out, dkv_out in ((high, dq_same, dkv_same), (1 - high, dq_cross, dkv_cross)):
+        src = pl.ds(pl.multiple_of(bit * half, half), half)
+        dq_out[...] = (dqn_ref[src, :] * inner).astype(BF16)
+        dkv_out[0] = (dk_ref[src, :] * inner).astype(BF16)
+        dkv_out[1] = (dv_ref[src, :] * norm).astype(BF16)
+    for bit, out_ref in ((low, keep_ref), (1 - low, send_ref)):
+        for top in range(2):
+            src = pl.ds(pl.multiple_of((2 * top + bit) * block, block), block)
+            dst = pl.ds(top * block, block)
             own = (dq_ref[src, :] * inner, dk_own[src, :] * inner, dv_own[src, :] * norm)
             for c, part in enumerate(own):
-                own_out[c, dst, :] = part.astype(own_out.dtype)
-
-
-def project_kernel(
-    keep_ref, got_ref, dq_same, dq_cross, dkv_same, dkv_cross, w_ref, wp_ref, mine_ref, send_ref
-):
+                out_ref[c, dst, :] = part.astype(BF16)
+
+
+def project(grads, weights, total=None):
+    for grad, weight in zip(grads, weights):
+        part = lax.dot_general(
+            grad, weight, (((1,), (1,)), ((), ())), preferred_element_type=F32
+        )
+        total = part if total is None else total + part
+    return total
+
+
+def local_kernel(keep_ref, got_ref, w_ref, w1_ref, mine_ref, send_ref):
     block = mine_ref.shape[0]
     high = lax.axis_index("head") // 2
-
-    def rows_of(index):
-        src = pl.ds(pl.multiple_of(index * block, block), block)
-        total = None
-        for own, dq, dkv, weights in (
-            (keep_ref, dq_same, dkv_same, w_ref),
-            (got_ref, dq_cross, dkv_cross, wp_ref),
-        ):
-            arrived = (dq[src, :], dkv[0, src, :], dkv[1, src, :])
-            for c, add in enumerate(arrived):
-                grad = (own[c, src, :].astype(F32) + add.astype(F32)).astype(BF16)
-                part = lax.dot_general(
-                    grad, weights[c], (((1,), (1,)), ((), ())), preferred_element_type=F32
-                )
-                total = part if total is None else total + part
-        return total
-
-    send_ref[...] = rows_of(1 - high).astype(BF16)
-    mine_ref[...] = rows_of(high)
-
-
-def call(body, name, outs, args, flops, scratch=(), lengths=True, space=VMEM, limit=24):
+    weights = [ref[c] for ref in (w_ref, w1_ref) for c in range(3)]
+    for bit, out_ref in ((1 - high, send_ref), (high, mine_ref)):
+        src = pl.ds(pl.multiple_of(bit * block, block), block)
+        grads = [ref[c, src, :] for ref in (keep_ref, got_ref) for c in range(3)]
+        out_ref[...] = project(grads, weights).astype(out_ref.dtype)
+
+
+def split_kernel(dq_same, dkv_same, dq_cross, dkv_cross, keep_ref, send_ref):
+    block = keep_ref.shape[2]
+    low = lax.axis_index("head") % 2
+    for bit, out_ref in ((1 - low, send_ref), (low, keep_ref)):
+        src = pl.ds(pl.multiple_of(bit * block, block), block)
+        for n, (dq, dkv) in enumerate(((dq_same, dkv_same), (dq_cross, dkv_cross))):
+            out_ref[n, 0] = dq[src, :]
+            out_ref[n, 1] = dkv[0, src, :]
+            out_ref[n, 2] = dkv[1, src, :]
+
+
+def final_kernel(keep_ref, got_ref, mine_ref, arrived_ref, w_ref, w1_ref, w2_ref, w3_ref, out_ref):
+    grads, weights = [], []
+    for half_ref, pair in ((keep_ref, (w_ref, w2_ref)), (got_ref, (w1_ref, w3_ref))):
+        for n, weight in enumerate(pair):
+            grads += [half_ref[n, c] for c in range(3)]
+            weights += [weight[c] for c in range(3)]
+    out_ref[...] = project(grads, weights, mine_ref[...] + arrived_ref[...].astype(F32))
+
+
+def call(body, outs, args, flops, scratch=(), lengths=True, space=VMEM, limit=24):
     specs = [SMEM if lengths and n == 0 else space for n in range(len(args))]
     moved = sum(math.prod(a.shape) * a.dtype.itemsize for a in (*args, *outs))
     return pl.pallas_call(
         body,
-        name=name,
         out_shape=outs,
         in_specs=specs,
         out_specs=tuple(VMEM for _ in outs),
@@ -253,24 +266,23 @@
     pair_flops = 10 * rows * rows * width
 
     query_grad, key_value = call(
-        pack_kernel, "pack", (pair, pair), tuple(pltpu.with_memory_space_constraint(x, pltpu.HBM) for x in (queries, out_grad, keys, values)), 1000,
+        pack_kernel, (pair, pair), tuple(pltpu.with_memory_space_constraint(x, pltpu.HBM) for x in (queries, out_grad, keys, values)), 1000,
         scratch=[pltpu.SemaphoreType.DMA((4,))], lengths=False,
         space=pl.BlockSpec(memory_space=pltpu.HBM),
     )
     query_grad_got = shift(query_grad, -1)
     key_value_got = shift(key_value, 2)
-
-    dq, dk, dv = call(
-        own_kernel, "own", (wide, wide, wide), (lengths, query_grad, key_value), pair_flops
-    )
+    w1, w2, w3 = (shift(w_proj, 0, flip) for flip in (1, 2, 3))
+
+    dq, dk, dv = call(own_kernel, (wide, wide, wide), (lengths, query_grad, key_value), pair_flops)
     dqn, dk, dv = call(
-        next_kernel, "next", (wide, wide, wide),
+        next_kernel, (wide, wide, wide),
         (lengths, query_grad_got, key_value, dk, dv), pair_flops,
     )
     keep, send, dq_same, dq_cross, dkv_same, dkv_cross = call(
-        far_kernel, "far",
+        far_kernel,
         (
-            like((3, 2 * block, width), F32), like((3, 2 * block, width), BF16),
+            like((3, 2 * block, width), BF16), like((3, 2 * block, width), BF16),
             like((2 * block, width), BF16), like((2 * block, width), BF16),
             like((2, 2 * block, width), BF16), like((2, 2 * block, width), BF16),
         ),
@@ -278,19 +290,28 @@
         pair_flops,
         scratch=[pltpu.VMEM((rows, width), F32)] * 4,
     )
+    dkv_cross = shift(dkv_cross, -2, 2)
     dkv_same = shift(dkv_same, -2)
-    dkv_cross = shift(dkv_cross, -2, 1)
+    dq_cross = shift(dq_cross, 1, 2)
     dq_same = shift(dq_same, 1)
-    dq_cross = shift(dq_cross, 1, 1)
     got = shift(send, 0, 1)
-    w_got = shift(w_proj, 0, 1)
-
     mine, send = call(
-        project_kernel, "project", (like((block, model), F32), like((block, model), BF16)),
-        (keep, got, dq_same, dq_cross, dkv_same, dkv_cross, w_proj, w_got),
-        12 * block * width * model, lengths=False,
-    )
-    return mine + shift(send, 0, 2).astype(F32)
+        local_kernel, (like((block, model), F32), like((block, model), BF16)),
+        (keep, got, w_proj, w1), 12 * block * width * model, lengths=False,
+    )
+    arrived = shift(send, 0, 2)
+
+    quarter = like((2, 3, block, width), BF16)
+    keep, send = call(
+        split_kernel, (quarter, quarter), (dq_same, dkv_same, dq_cross, dkv_cross), 1000,
+        lengths=False,
+    )
+    got = shift(send, 0, 1)
+    (out,) = call(
+        final_kernel, (like((block, model), F32),),
+        (keep, got, mine, arrived, w_proj, w1, w2, w3), 24 * block * width * model, lengths=False,
+    )
+    return out
 
 
 def solution(mesh):

time: 53.5 us -> 74.4 us (1.39)
  the two profiles are of different devices: /device:TPU:0 before, /device:TPU:20 now
where the time goes in v4:
time: 74.4 us; the launch traced here: 74.2 us
  waiting for transfers between devices  34.9 us (47%)
  starting transfers between devices  21.7 us (29%)
  Pallas kernels  17.4 us (23%)
    ppermute x12, waiting for transfers between devices, shift(): return lax.ppermute(value, ('seq', 'head'), pairs)  34.9 us
    ppermute x12, starting transfers between devices, shift(): return lax.ppermute(value, ('seq', 'head'), pairs)  21.7 us
    pallas_call x7, Pallas kernels, call(): pl.pallas_call(body, out_shape=outs, in_specs=specs, out_specs=tuple((VME...  17.4 us
  transfers between devices with their start and end apart: 12, of which 5 were waited for; matrix products, arithmetic and copies ran while one was open for 0% of the time, Pallas kernels for 19%

profile of v4, /device:TPU:20, one launch (start us, length us, event | category | flops | bytes accessed | tf_op | source)
XLA Modules:
  0.0 74.2 jit_solution(16283030911891767946)
XLA Ops:
  0.0 0.0 copy-start
  0.0 1.3 %shard_map.64 = (bf16[2,1024,128]{2,1,0:T(8,128)(2,1)S(1)}, bf16[2,1024,128]{2,1,0:T(8,128)(2,1)S(1)}) custom-call(bf16[1024,128]{1,0:T(8,128)(2,1)} %q_hbm.1, bf16[1024,128]{1,0:T(8,128)(2,1)} %g_hbm.1, bf16[1024,128]{1,0:T(8,128)(2,1)} %k_hbm.1, bf16[1024,128]{1,0:T(8,128)(2,1)} %v_hbm.1), custom_call_target="tpu_custom_call" | custom-call | flops 1000 | bytes 2097152 | tf_op jit(solution)/shard_map/pallas_call | solution.py:247
  1.3 0.0 copy-start.1
  1.3 2.4 %collective-permute-start = (bf16[2,1024,128]{2,1,0:T(8,128)(2,1)S(1)}, bf16[2,1024,128]{2,1,0:T(8,128)(2,1)S(1)}, u32[]{:S(2)}, u32[]{:S(2)}) collective-permute-start(bf16[2,1024,128]{2,1,0:T(8,128)(2,1)S(1)} %get-tuple-element.23.qg_ref), channel_id=1, source_target_pairs={{4,0},{5,1},{6,2},{7,3},{8,4},{9,5},{10,6},{11,7},{12,8},{13,9},{1... | collective-permute-start | bytes 1572872 | tf_op jit(solution)/shard_map/ppermute | solution.py:27
  3.7 3.5 %collective-permute-start.1 = (bf16[2,1024,128]{2,1,0:T(8,128)(2,1)S(1)}, bf16[2,1024,128]{2,1,0:T(8,128)(2,1)S(1)}, u32[]{:S(2)}, u32[]{:S(2)}) collective-permute-start(bf16[2,1024,128]{2,1,0:T(8,128)(2,1)S(1)} %get-tuple-element.24.kv_ref), channel_id=1, source_target_pairs={{0,8},{1,9},{2,10},{3,11},{4,12},{5,13},{6,14},{7,15},{8,16},{9,17... | collective-permute-start | bytes 1572872 | tf_op jit(solution)/shard_map/ppermute | solution.py:27
  7.2 0.0 copy-done
  7.2 0.1 collective-permute-start.8
  7.3 0.0 copy-done.1
  7.3 4.6 %shard_map.65 = (f32[1024,128]{1,0:T(8,128)S(1)}, f32[1024,128]{1,0:T(8,128)S(1)}, f32[1024,128]{1,0:T(8,128)S(1)}) custom-call(s32[4]{0:T(128)S(1)} %copy-done.1, bf16[2,1024,128]{2,1,0:T(8,128)(2,1)S(1)} %get-tuple-element.23.qg_ref, bf16[2,1024,128]{2,1,0:T(8,128)(2,1)S(1)} %get-tuple-element.24.kv_ref), custom_call_target="tpu_custom_call" | custom-call | flops 1342177280 | bytes 2621456 | tf_op jit(solution)/shard_map/pallas_call | solution.py:247
  11.9 5.8 %collective-permute-done.qgn_ref = bf16[2,1024,128]{2,1,0:T(8,128)(2,1)S(1)} collective-permute-done((bf16[2,1024,128]{2,1,0:T(8,128)(2,1)S(1)}, bf16[2,1024,128]{2,1,0:T(8,128)(2,1)S(1)}, u32[]{:S(2)}, u32[]{:S(2)}) %collective-permute-start) | collective-permute-done | bytes 524320 | tf_op jit(solution)/shard_map/ppermute | solution.py:27
  17.8 5.4 %shard_map.66 = (f32[1024,128]{1,0:T(8,128)S(1)}, f32[1024,128]{1,0:T(8,128)S(1)}, f32[1024,128]{1,0:T(8,128)S(1)}) custom-call(s32[4]{0:T(128)S(1)} %copy-done.1, bf16[2,1024,128]{2,1,0:T(8,128)(2,1)S(1)} %collective-permute-done.qgn_ref, bf16[2,1024,128]{2,1,0:T(8,128)(2,1)S(1)} %get-tuple-element.24.kv_ref, f32[1024,128]{1,0:T(8,128)S(1)} %get-tuple-element.26.dk_in, ...), custom_call_target="tpu_custom_call" | custom-call | flops 1342177280 | bytes 3670032 | tf_op jit(solution)/shard_map/pallas_call | solution.py:247
  23.1 0.0 collective-permute-done.1.kv_ref
  23.2 3.4 %shard_map.67 = (bf16[3,512,128]{2,1,0:T(8,128)(2,1)S(1)}, bf16[3,512,128]{2,1,0:T(8,128)(2,1)S(1)}, bf16[512,128]{1,0:T(8,128)(2,1)S(1)}, bf16[512,128]{1,0:T(8...) custom-call(s32[4]{0:T(128)S(1)} %copy-done.1, ...), custom_call_target="tpu_custom_call" | custom-call | flops 1342177280 | bytes 5242896 | tf_op jit(solution)/shard_map/pallas_call | solution.py:247
  26.5 0.1 collective-permute-start.7
  26.6 1.9 %collective-permute-start.2 = (bf16[512,128]{1,0:T(8,128)(2,1)S(1)}, bf16[512,128]{1,0:T(8,128)(2,1)S(1)}, u32[]{:S(2)}, u32[]{:S(2)}) collective-permute-start(bf16[512,128]{1,0:T(8,128)(2,1)S(1)} %get-tuple-element.31), channel_id=1, source_target_pairs={{0,4},{1,5},{2,6},{3,7},{4,8},{5,9},{6,10},{7,11},{8,12},{9,13},{1... | collective-permute-start | bytes 393224 | tf_op jit(solution)/shard_map/ppermute | solution.py:27
  28.5 1.9 %collective-permute-start.3 = (bf16[2,512,128]{2,1,0:T(8,128)(2,1)S(1)}, bf16[2,512,128]{2,1,0:T(8,128)(2,1)S(1)}, u32[]{:S(2)}, u32[]{:S(2)}) collective-permute-start(bf16[2,512,128]{2,1,0:T(8,128)(2,1)S(1)} %get-tuple-element.32), channel_id=1, source_target_pairs={{8,0},{9,1},{10,2},{11,3},{12,4},{13,5},{14,6},{15,7},{16,8},{17,9... | collective-permute-start | bytes 786440 | tf_op jit(solution)/shard_map/ppermute | solution.py:27
  30.5 4.3 %collective-permute-start.5 = (bf16[2,512,128]{2,1,0:T(8,128)(2,1)S(1)}, bf16[2,512,128]{2,1,0:T(8,128)(2,1)S(1)}, u32[]{:S(2)}, u32[]{:S(2)}) collective-permute-start(bf16[2,512,128]{2,1,0:T(8,128)(2,1)S(1)} %get-tuple-element.34), channel_id=1, source_target_pairs={{8,2},{9,3},{10,0},{11,1},{12,6},{13,7},{14,4},{15,5},{16,10},{17,... | collective-permute-start | bytes 786440 | tf_op jit(solution)/shard_map/ppermute | solution.py:27
  34.8 0.0 collective-permute-done.2.dq_same
  34.8 3.9 %collective-permute-start.4 = (bf16[512,128]{1,0:T(8,128)(2,1)S(1)}, bf16[512,128]{1,0:T(8,128)(2,1)S(1)}, u32[]{:S(2)}, u32[]{:S(2)}) collective-permute-start(bf16[512,128]{1,0:T(8,128)(2,1)S(1)} %get-tuple-element.33), channel_id=1, source_target_pairs={{0,6},{1,7},{2,4},{3,5},{4,10},{5,11},{6,8},{7,9},{8,14},{9,15},{1... | collective-permute-start | bytes 393224 | tf_op jit(solution)/shard_map/ppermute | solution.py:27
  38.7 9.5 %collective-permute-done.4.dq_cross = bf16[512,128]{1,0:T(8,128)(2,1)S(1)} collective-permute-done((bf16[512,128]{1,0:T(8,128)(2,1)S(1)}, bf16[512,128]{1,0:T(8,128)(2,1)S(1)}, u32[]{:S(2)}, u32[]{:S(2)}) %collective-permute-start.4) | collective-permute-done | bytes 131104 | tf_op jit(solution)/shard_map/ppermute | solution.py:27
  48.2 1.3 %collective-permute-start.10 = (bf16[3,512,128]{2,1,0:T(8,128)(2,1)S(1)}, bf16[3,512,128]{2,1,0:T(8,128)(2,1)S(1)}, u32[]{:S(2)}, u32[]{:S(2)}) collective-permute-start(bf16[3,512,128]{2,1,0:T(8,128)(2,1)S(1)} %copy-done), channel_id=1, source_target_pairs={{0,2},{1,3},{2,0},{3,1},{4,6},{5,7},{6,4},{7,5},{8,10},{9,11},{10,... | collective-permute-start | bytes 1179656 | tf_op jit(solution)/shard_map/ppermute | solution.py:27
  49.5 0.0 collective-permute-done.3.dkv_same
  49.5 0.0 collective-permute-start.11
  49.5 0.0 collective-permute-done.5.dkv_cross
  49.5 0.1 shard_map.68
  49.6 0.9 %collective-permute-start.6 = (bf16[2,3,256,128]{3,2,1,0:T(8,128)(2,1)S(1)}, bf16[2,3,256,128]{3,2,1,0:T(8,128)(2,1)S(1)}, u32[]{:S(2)}, u32[]{:S(2)}) collective-permute-start(bf16[2,3,256,128]{3,2,1,0:T(8,128)(2,1)S(1)} %get-tuple-element.36), channel_id=1, source_target_pairs={{0,1},{1,0},{2,3},{3,2},{4,5},{5,4},{6,7},{7,6},{8,9},{9,8},{10,11... | collective-permute-start | bytes 1179656 | tf_op jit(solution)/shard_map/ppermute | solution.py:27
  50.5 0.0 collective-permute-done.8.w1_ref
  50.5 0.0 collective-permute-done.7.got_ref
  50.5 1.0 %shard_map.69 = (f32[256,512]{1,0:T(8,128)S(1)}, bf16[256,512]{1,0:T(8,128)(2,1)S(1)}) custom-call(bf16[3,512,128]{2,1,0:T(8,128)(2,1)S(1)} %get-tuple-element.37.keep_ref, bf16[3,512,128]{2,1,0:T(8,128)(2,1)S(1)} %collective-permute-done.7.got_ref, bf16[3,512,128]{2,1,0:T(8,128)(2,1)S(1)} %copy-done, bf16[3,512,128]{2,1,0:T(8,128)(2,1)S(1)} %collective-permute-done.8.w1_ref), custom_call_target="tpu_custom_call" | custom-call | flops 201326592 | bytes 2359296 | tf_op jit(solution)/shard_map/pallas_call | solution.py:247
  51.5 1.4 %collective-permute-start.9 = (bf16[256,512]{1,0:T(8,128)(2,1)S(1)}, bf16[256,512]{1,0:T(8,128)(2,1)S(1)}, u32[]{:S(2)}, u32[]{:S(2)}) collective-permute-start(bf16[256,512]{1,0:T(8,128)(2,1)S(1)} %get-tuple-element.40), channel_id=1, source_target_pairs={{0,2},{1,3},{2,0},{3,1},{4,6},{5,7},{6,4},{7,5},{8,10},{9,11},{10,... | collective-permute-start | bytes 786440 | tf_op jit(solution)/shard_map/ppermute | solution.py:27
  52.8 7.4 %collective-permute-done.10.w2_ref = bf16[3,512,128]{2,1,0:T(8,128)(2,1)S(1)} collective-permute-done((bf16[3,512,128]{2,1,0:T(8,128)(2,1)S(1)}, bf16[3,512,128]{2,1,0:T(8,128)(2,1)S(1)}, u32[]{:S(2)}, u32[]{:S(2)}) %collective-permute-start.10) | collective-permute-done | bytes 393248 | tf_op jit(solution)/shard_map/ppermute | solution.py:27
  60.2 7.3 %collective-permute-done.11.w3_ref = bf16[3,512,128]{2,1,0:T(8,128)(2,1)S(1)} collective-permute-done((bf16[3,512,128]{2,1,0:T(8,128)(2,1)S(1)}, bf16[3,512,128]{2,1,0:T(8,128)(2,1)S(1)}, u32[]{:S(2)}, u32[]{:S(2)}) %collective-permute-start.11) | collective-permute-done | bytes 393248 | tf_op jit(solution)/shard_map/ppermute | solution.py:27
  67.5 0.0 collective-permute-done.6.got_ref
  67.5 4.9 %collective-permute-done.9.arrived_ref = bf16[256,512]{1,0:T(8,128)(2,1)S(1)} collective-permute-done((bf16[256,512]{1,0:T(8,128)(2,1)S(1)}, bf16[256,512]{1,0:T(8,128)(2,1)S(1)}, u32[]{:S(2)}, u32[]{:S(2)}) %collective-permute-start.9) | collective-permute-done | bytes 262176 | tf_op jit(solution)/shard_map/ppermute | solution.py:27
  72.4 1.8 %shard_map.70 = f32[256,512]{1,0:T(8,128)} custom-call(bf16[2,3,256,128]{3,2,1,0:T(8,128)(2,1)S(1)} %get-tuple-element.35.keep_ref, bf16[2,3,256,128]{3,2,1,0:T(8,128)(2,1)S(1)} %collective-permute-done.6.got_ref, f32[256,512]{1,0:T(8,128)S(1)} %get-tuple-element.39.mine_ref, bf16[256,512]{1,0:T(8,128)(2,1)S(1)} %collective-permute-done.9.arrived_ref, ...), custom_call_target="tpu_custom_call" | custom-call | flops 402653184 | bytes 3670016 | tf_op jit(solution)/shard_map/pallas_call | solution.py:247
Async XLA Ops:
  0.0 7.2 %copy-start = (bf16[3,512,128]{2,1,0:T(8,128)(2,1)S(1)}, bf16[3,512,128]{2,1,0:T(8,128)(2,1)}, u32[]{:S(2)}) copy-start(bf16[3,512,128]{2,1,0:T(8,128)(2,1)} %w_ref.3) | copy-start | bytes 1179652
  1.3 6.0 %copy-start.1 = (s32[4]{0:T(128)S(1)}, s32[4]{0:T(128)}, u32[]{:S(2)}) copy-start(s32[4]{0:T(128)} %lengths_ref.5) | copy-start | bytes 52
  1.3 16.5 %collective-permute-start = (bf16[2,1024,128]{2,1,0:T(8,128)(2,1)S(1)}, bf16[2,1024,128]{2,1,0:T(8,128)(2,1)S(1)}, u32[]{:S(2)}, u32[]{:S(2)}) collective-permute-start(bf16[2,1024,128]{2,1,0:T(8,128)(2,1)S(1)} %get-tuple-element.23.qg_ref), channel_id=1, source_target_pairs={{4,0},{5,1},{6,2},{7,3},{8,4},{9,5},{10,6},{11,7},{12,8},{13,9},{1... | collective-permute-start | bytes 1572872 | tf_op jit(solution)/shard_map/ppermute | solution.py:27
  3.7 19.4 %collective-permute-start.1 = (bf16[2,1024,128]{2,1,0:T(8,128)(2,1)S(1)}, bf16[2,1024,128]{2,1,0:T(8,128)(2,1)S(1)}, u32[]{:S(2)}, u32[]{:S(2)}) collective-permute-start(bf16[2,1024,128]{2,1,0:T(8,128)(2,1)S(1)} %get-tuple-element.24.kv_ref), channel_id=1, source_target_pairs={{0,8},{1,9},{2,10},{3,11},{4,12},{5,13},{6,14},{7,15},{8,16},{9,17... | collective-permute-start | bytes 1572872 | tf_op jit(solution)/shard_map/ppermute | solution.py:27
  7.2 43.2 %collective-permute-start.8 = (bf16[3,512,128]{2,1,0:T(8,128)(2,1)S(1)}, bf16[3,512,128]{2,1,0:T(8,128)(2,1)S(1)}, u32[]{:S(2)}, u32[]{:S(2)}) collective-permute-start(bf16[3,512,128]{2,1,0:T(8,128)(2,1)S(1)} %copy-done), channel_id=1, source_target_pairs={{0,1},{1,0},{2,3},{3,2},{4,5},{5,4},{6,7},{7,6},{8,9},{9,8},{10,11... | collective-permute-start | bytes 1179656 | tf_op jit(solution)/shard_map/ppermute | solution.py:27
  26.5 24.0 %collective-permute-start.7 = (bf16[3,512,128]{2,1,0:T(8,128)(2,1)S(1)}, bf16[3,512,128]{2,1,0:T(8,128)(2,1)S(1)}, u32[]{:S(2)}, u32[]{:S(2)}) collective-permute-start(bf16[3,512,128]{2,1,0:T(8,128)(2,1)S(1)} %get-tuple-element.38), channel_id=1, source_target_pairs={{0,1},{1,0},{2,3},{3,2},{4,5},{5,4},{6,7},{7,6},{8,9},{9,8},{10,11... | collective-permute-start | bytes 1179656 | tf_op jit(solution)/shard_map/ppermute | solution.py:27
  26.6 8.1 %collective-permute-start.2 = (bf16[512,128]{1,0:T(8,128)(2,1)S(1)}, bf16[512,128]{1,0:T(8,128)(2,1)S(1)}, u32[]{:S(2)}, u32[]{:S(2)}) collective-permute-start(bf16[512,128]{1,0:T(8,128)(2,1)S(1)} %get-tuple-element.31), channel_id=1, source_target_pairs={{0,4},{1,5},{2,6},{3,7},{4,8},{5,9},{6,10},{7,11},{8,12},{9,13},{1... | collective-permute-start | bytes 393224 | tf_op jit(solution)/shard_map/ppermute | solution.py:27
  28.5 21.0 %collective-permute-start.3 = (bf16[2,512,128]{2,1,0:T(8,128)(2,1)S(1)}, bf16[2,512,128]{2,1,0:T(8,128)(2,1)S(1)}, u32[]{:S(2)}, u32[]{:S(2)}) collective-permute-start(bf16[2,512,128]{2,1,0:T(8,128)(2,1)S(1)} %get-tuple-element.32), channel_id=1, source_target_pairs={{8,0},{9,1},{10,2},{11,3},{12,4},{13,5},{14,6},{15,7},{16,8},{17,9... | collective-permute-start | bytes 786440 | tf_op jit(solution)/shard_map/ppermute | solution.py:27
  30.5 19.1 %collective-permute-start.5 = (bf16[2,512,128]{2,1,0:T(8,128)(2,1)S(1)}, bf16[2,512,128]{2,1,0:T(8,128)(2,1)S(1)}, u32[]{:S(2)}, u32[]{:S(2)}) collective-permute-start(bf16[2,512,128]{2,1,0:T(8,128)(2,1)S(1)} %get-tuple-element.34), channel_id=1, source_target_pairs={{8,2},{9,3},{10,0},{11,1},{12,6},{13,7},{14,4},{15,5},{16,10},{17,... | collective-permute-start | bytes 786440 | tf_op jit(solution)/shard_map/ppermute | solution.py:27
  34.8 13.5 %collective-permute-start.4 = (bf16[512,128]{1,0:T(8,128)(2,1)S(1)}, bf16[512,128]{1,0:T(8,128)(2,1)S(1)}, u32[]{:S(2)}, u32[]{:S(2)}) collective-permute-start(bf16[512,128]{1,0:T(8,128)(2,1)S(1)} %get-tuple-element.33), channel_id=1, source_target_pairs={{0,6},{1,7},{2,4},{3,5},{4,10},{5,11},{6,8},{7,9},{8,14},{9,15},{1... | collective-permute-start | bytes 393224 | tf_op jit(solution)/shard_map/ppermute | solution.py:27
  48.2 12.0 %collective-permute-start.10 = (bf16[3,512,128]{2,1,0:T(8,128)(2,1)S(1)}, bf16[3,512,128]{2,1,0:T(8,128)(2,1)S(1)}, u32[]{:S(2)}, u32[]{:S(2)}) collective-permute-start(bf16[3,512,128]{2,1,0:T(8,128)(2,1)S(1)} %copy-done), channel_id=1, source_target_pairs={{0,2},{1,3},{2,0},{3,1},{4,6},{5,7},{6,4},{7,5},{8,10},{9,11},{10,... | collective-permute-start | bytes 1179656 | tf_op jit(solution)/shard_map/ppermute | solution.py:27
  49.5 17.9 %collective-permute-start.11 = (bf16[3,512,128]{2,1,0:T(8,128)(2,1)S(1)}, bf16[3,512,128]{2,1,0:T(8,128)(2,1)S(1)}, u32[]{:S(2)}, u32[]{:S(2)}) collective-permute-start(bf16[3,512,128]{2,1,0:T(8,128)(2,1)S(1)} %copy-done), channel_id=1, source_target_pairs={{0,3},{1,2},{2,1},{3,0},{4,7},{5,6},{6,5},{7,4},{8,11},{9,10},{10,... | collective-permute-start | bytes 1179656 | tf_op jit(solution)/shard_map/ppermute | solution.py:27
  49.6 17.8 %collective-permute-start.6 = (bf16[2,3,256,128]{3,2,1,0:T(8,128)(2,1)S(1)}, bf16[2,3,256,128]{3,2,1,0:T(8,128)(2,1)S(1)}, u32[]{:S(2)}, u32[]{:S(2)}) collective-permute-start(bf16[2,3,256,128]{3,2,1,0:T(8,128)(2,1)S(1)} %get-tuple-element.36), channel_id=1, source_target_pairs={{0,1},{1,0},{2,3},{3,2},{4,5},{5,4},{6,7},{7,6},{8,9},{9,8},{10,11... | collective-permute-start | bytes 1179656 | tf_op jit(solution)/shard_map/ppermute | solution.py:27
  51.5 20.9 %collective-permute-start.9 = (bf16[256,512]{1,0:T(8,128)(2,1)S(1)}, bf16[256,512]{1,0:T(8,128)(2,1)S(1)}, u32[]{:S(2)}, u32[]{:S(2)}) collective-permute-start(bf16[256,512]{1,0:T(8,128)(2,1)S(1)} %get-tuple-element.40), channel_id=1, source_target_pairs={{0,2},{1,3},{2,0},{3,1},{4,6},{5,7},{6,4},{7,5},{8,10},{9,11},{10,... | collective-permute-start | bytes 786440 | tf_op jit(solution)/shard_map/ppermute | solution.py:27

commit v5 on v4

--- a/solution.py
+++ b/solution.py
@@ -202,13 +202,11 @@
                 out_ref[c, dst, :] = part.astype(BF16)
 
 
-def project(grads, weights, total=None):
-    for grad, weight in zip(grads, weights):
-        part = lax.dot_general(
-            grad, weight, (((1,), (1,)), ((), ())), preferred_element_type=F32
-        )
-        total = part if total is None else total + part
-    return total
+def project(grads, weights):
+    return lax.dot_general(
+        jnp.concatenate(grads, axis=1), jnp.concatenate(weights, axis=1),
+        (((1,), (1,)), ((), ())), preferred_element_type=F32,
+    )
 
 
 def local_kernel(keep_ref, got_ref, w_ref, w1_ref, mine_ref, send_ref):
@@ -238,7 +236,7 @@
         for n, weight in enumerate(pair):
             grads += [half_ref[n, c] for c in range(3)]
             weights += [weight[c] for c in range(3)]
-    out_ref[...] = project(grads, weights, mine_ref[...] + arrived_ref[...].astype(F32))
+    out_ref[...] = project(grads, weights) + mine_ref[...] + arrived_ref[...].astype(F32)
 
 
 def call(body, outs, args, flops, scratch=(), lengths=True, space=VMEM, limit=24):

time: 74.4 us -> 74.1 us (level)
  no operation moved by 1% of the time
where the time goes in v5:
time: 74.1 us; the launch traced here: 73.8 us
  waiting for transfers between devices  35.3 us (48%)
  starting transfers between devices  21.7 us (29%)
  Pallas kernels  16.7 us (23%)
    ppermute x12, waiting for transfers between devices, shift(): return lax.ppermute(value, ('seq', 'head'), pairs)  35.3 us
    ppermute x12, starting transfers between devices, shift(): return lax.ppermute(value, ('seq', 'head'), pairs)  21.7 us
    pallas_call x7, Pallas kernels, call(): pl.pallas_call(body, out_shape=outs, in_specs=specs, out_specs=tuple((VME...  16.7 us
  transfers between devices with their start and end apart: 12, of which 5 were waited for; matrix products, arithmetic and copies ran while one was open for 0% of the time, Pallas kernels for 19%

profile of v5, /device:TPU:20, one launch (start us, length us, event | category | flops | bytes accessed | tf_op | source)
XLA Modules:
  0.0 73.8 jit_solution(11063295967102670723)
XLA Ops:
  0.0 0.0 copy-start
  0.0 1.3 %shard_map.64 = (bf16[2,1024,128]{2,1,0:T(8,128)(2,1)S(1)}, bf16[2,1024,128]{2,1,0:T(8,128)(2,1)S(1)}) custom-call(bf16[1024,128]{1,0:T(8,128)(2,1)} %q_hbm.1, bf16[1024,128]{1,0:T(8,128)(2,1)} %g_hbm.1, bf16[1024,128]{1,0:T(8,128)(2,1)} %k_hbm.1, bf16[1024,128]{1,0:T(8,128)(2,1)} %v_hbm.1), custom_call_target="tpu_custom_call" | custom-call | flops 1000 | bytes 2097152 | tf_op jit(solution)/shard_map/pallas_call | solution.py:245
  1.3 0.0 copy-start.1
  1.3 2.4 %collective-permute-start = (bf16[2,1024,128]{2,1,0:T(8,128)(2,1)S(1)}, bf16[2,1024,128]{2,1,0:T(8,128)(2,1)S(1)}, u32[]{:S(2)}, u32[]{:S(2)}) collective-permute-start(bf16[2,1024,128]{2,1,0:T(8,128)(2,1)S(1)} %get-tuple-element.23.qg_ref), channel_id=1, source_target_pairs={{4,0},{5,1},{6,2},{7,3},{8,4},{9,5},{10,6},{11,7},{12,8},{13,9},{1... | collective-permute-start | bytes 1572872 | tf_op jit(solution)/shard_map/ppermute | solution.py:27
  3.7 3.5 %collective-permute-start.1 = (bf16[2,1024,128]{2,1,0:T(8,128)(2,1)S(1)}, bf16[2,1024,128]{2,1,0:T(8,128)(2,1)S(1)}, u32[]{:S(2)}, u32[]{:S(2)}) collective-permute-start(bf16[2,1024,128]{2,1,0:T(8,128)(2,1)S(1)} %get-tuple-element.24.kv_ref), channel_id=1, source_target_pairs={{0,8},{1,9},{2,10},{3,11},{4,12},{5,13},{6,14},{7,15},{8,16},{9,17... | collective-permute-start | bytes 1572872 | tf_op jit(solution)/shard_map/ppermute | solution.py:27
  7.2 0.0 copy-done
  7.2 0.1 collective-permute-start.8
  7.3 0.0 copy-done.1
  7.3 4.6 %shard_map.65 = (f32[1024,128]{1,0:T(8,128)S(1)}, f32[1024,128]{1,0:T(8,128)S(1)}, f32[1024,128]{1,0:T(8,128)S(1)}) custom-call(s32[4]{0:T(128)S(1)} %copy-done.1, bf16[2,1024,128]{2,1,0:T(8,128)(2,1)S(1)} %get-tuple-element.23.qg_ref, bf16[2,1024,128]{2,1,0:T(8,128)(2,1)S(1)} %get-tuple-element.24.kv_ref), custom_call_target="tpu_custom_call" | custom-call | flops 1342177280 | bytes 2621456 | tf_op jit(solution)/shard_map/pallas_call | solution.py:245
  11.9 5.8 %collective-permute-done.qgn_ref = bf16[2,1024,128]{2,1,0:T(8,128)(2,1)S(1)} collective-permute-done((bf16[2,1024,128]{2,1,0:T(8,128)(2,1)S(1)}, bf16[2,1024,128]{2,1,0:T(8,128)(2,1)S(1)}, u32[]{:S(2)}, u32[]{:S(2)}) %collective-permute-start) | collective-permute-done | bytes 524320 | tf_op jit(solution)/shard_map/ppermute | solution.py:27
  17.8 5.4 %shard_map.66 = (f32[1024,128]{1,0:T(8,128)S(1)}, f32[1024,128]{1,0:T(8,128)S(1)}, f32[1024,128]{1,0:T(8,128)S(1)}) custom-call(s32[4]{0:T(128)S(1)} %copy-done.1, bf16[2,1024,128]{2,1,0:T(8,128)(2,1)S(1)} %collective-permute-done.qgn_ref, bf16[2,1024,128]{2,1,0:T(8,128)(2,1)S(1)} %get-tuple-element.24.kv_ref, f32[1024,128]{1,0:T(8,128)S(1)} %get-tuple-element.26.dk_in, ...), custom_call_target="tpu_custom_call" | custom-call | flops 1342177280 | bytes 3670032 | tf_op jit(solution)/shard_map/pallas_call | solution.py:245
  23.1 0.0 collective-permute-done.1.kv_ref
  23.2 3.4 %shard_map.67 = (bf16[3,512,128]{2,1,0:T(8,128)(2,1)S(1)}, bf16[3,512,128]{2,1,0:T(8,128)(2,1)S(1)}, bf16[512,128]{1,0:T(8,128)(2,1)S(1)}, bf16[512,128]{1,0:T(8...) custom-call(s32[4]{0:T(128)S(1)} %copy-done.1, ...), custom_call_target="tpu_custom_call" | custom-call | flops 1342177280 | bytes 5242896 | tf_op jit(solution)/shard_map/pallas_call | solution.py:245
  26.5 0.1 collective-permute-start.7
  26.6 1.9 %collective-permute-start.2 = (bf16[512,128]{1,0:T(8,128)(2,1)S(1)}, bf16[512,128]{1,0:T(8,128)(2,1)S(1)}, u32[]{:S(2)}, u32[]{:S(2)}) collective-permute-start(bf16[512,128]{1,0:T(8,128)(2,1)S(1)} %get-tuple-element.31), channel_id=1, source_target_pairs={{0,4},{1,5},{2,6},{3,7},{4,8},{5,9},{6,10},{7,11},{8,12},{9,13},{1... | collective-permute-start | bytes 393224 | tf_op jit(solution)/shard_map/ppermute | solution.py:27
  28.5 1.9 %collective-permute-start.3 = (bf16[2,512,128]{2,1,0:T(8,128)(2,1)S(1)}, bf16[2,512,128]{2,1,0:T(8,128)(2,1)S(1)}, u32[]{:S(2)}, u32[]{:S(2)}) collective-permute-start(bf16[2,512,128]{2,1,0:T(8,128)(2,1)S(1)} %get-tuple-element.32), channel_id=1, source_target_pairs={{8,0},{9,1},{10,2},{11,3},{12,4},{13,5},{14,6},{15,7},{16,8},{17,9... | collective-permute-start | bytes 786440 | tf_op jit(solution)/shard_map/ppermute | solution.py:27
  30.5 4.3 %collective-permute-start.5 = (bf16[2,512,128]{2,1,0:T(8,128)(2,1)S(1)}, bf16[2,512,128]{2,1,0:T(8,128)(2,1)S(1)}, u32[]{:S(2)}, u32[]{:S(2)}) collective-permute-start(bf16[2,512,128]{2,1,0:T(8,128)(2,1)S(1)} %get-tuple-element.34), channel_id=1, source_target_pairs={{8,2},{9,3},{10,0},{11,1},{12,6},{13,7},{14,4},{15,5},{16,10},{17,... | collective-permute-start | bytes 786440 | tf_op jit(solution)/shard_map/ppermute | solution.py:27
  34.8 0.0 collective-permute-done.2.dq_same
  34.8 3.9 %collective-permute-start.4 = (bf16[512,128]{1,0:T(8,128)(2,1)S(1)}, bf16[512,128]{1,0:T(8,128)(2,1)S(1)}, u32[]{:S(2)}, u32[]{:S(2)}) collective-permute-start(bf16[512,128]{1,0:T(8,128)(2,1)S(1)} %get-tuple-element.33), channel_id=1, source_target_pairs={{0,6},{1,7},{2,4},{3,5},{4,10},{5,11},{6,8},{7,9},{8,14},{9,15},{1... | collective-permute-start | bytes 393224 | tf_op jit(solution)/shard_map/ppermute | solution.py:27
  38.7 9.5 %collective-permute-done.4.dq_cross = bf16[512,128]{1,0:T(8,128)(2,1)S(1)} collective-permute-done((bf16[512,128]{1,0:T(8,128)(2,1)S(1)}, bf16[512,128]{1,0:T(8,128)(2,1)S(1)}, u32[]{:S(2)}, u32[]{:S(2)}) %collective-permute-start.4) | collective-permute-done | bytes 131104 | tf_op jit(solution)/shard_map/ppermute | solution.py:27
  48.2 1.3 %collective-permute-start.10 = (bf16[3,512,128]{2,1,0:T(8,128)(2,1)S(1)}, bf16[3,512,128]{2,1,0:T(8,128)(2,1)S(1)}, u32[]{:S(2)}, u32[]{:S(2)}) collective-permute-start(bf16[3,512,128]{2,1,0:T(8,128)(2,1)S(1)} %copy-done), channel_id=1, source_target_pairs={{0,2},{1,3},{2,0},{3,1},{4,6},{5,7},{6,4},{7,5},{8,10},{9,11},{10,... | collective-permute-start | bytes 1179656 | tf_op jit(solution)/shard_map/ppermute | solution.py:27
  49.5 0.0 collective-permute-done.3.dkv_same
  49.5 0.0 collective-permute-start.11
  49.5 0.0 collective-permute-done.5.dkv_cross
  49.5 0.1 shard_map.68
  49.6 0.9 %collective-permute-start.6 = (bf16[2,3,256,128]{3,2,1,0:T(8,128)(2,1)S(1)}, bf16[2,3,256,128]{3,2,1,0:T(8,128)(2,1)S(1)}, u32[]{:S(2)}, u32[]{:S(2)}) collective-permute-start(bf16[2,3,256,128]{3,2,1,0:T(8,128)(2,1)S(1)} %get-tuple-element.36), channel_id=1, source_target_pairs={{0,1},{1,0},{2,3},{3,2},{4,5},{5,4},{6,7},{7,6},{8,9},{9,8},{10,11... | collective-permute-start | bytes 1179656 | tf_op jit(solution)/shard_map/ppermute | solution.py:27
  50.5 0.0 collective-permute-done.8.w1_ref
  50.5 0.0 collective-permute-done.7.got_ref
  50.5 0.6 shard_map.69
  51.1 1.4 %collective-permute-start.9 = (bf16[256,512]{1,0:T(8,128)(2,1)S(1)}, bf16[256,512]{1,0:T(8,128)(2,1)S(1)}, u32[]{:S(2)}, u32[]{:S(2)}) collective-permute-start(bf16[256,512]{1,0:T(8,128)(2,1)S(1)} %get-tuple-element.40), channel_id=1, source_target_pairs={{0,2},{1,3},{2,0},{3,1},{4,6},{5,7},{6,4},{7,5},{8,10},{9,11},{10,... | collective-permute-start | bytes 786440 | tf_op jit(solution)/shard_map/ppermute | solution.py:27
  52.5 7.7 %collective-permute-done.10.w2_ref = bf16[3,512,128]{2,1,0:T(8,128)(2,1)S(1)} collective-permute-done((bf16[3,512,128]{2,1,0:T(8,128)(2,1)S(1)}, bf16[3,512,128]{2,1,0:T(8,128)(2,1)S(1)}, u32[]{:S(2)}, u32[]{:S(2)}) %collective-permute-start.10) | collective-permute-done | bytes 393248 | tf_op jit(solution)/shard_map/ppermute | solution.py:27
  60.2 7.3 %collective-permute-done.11.w3_ref = bf16[3,512,128]{2,1,0:T(8,128)(2,1)S(1)} collective-permute-done((bf16[3,512,128]{2,1,0:T(8,128)(2,1)S(1)}, bf16[3,512,128]{2,1,0:T(8,128)(2,1)S(1)}, u32[]{:S(2)}, u32[]{:S(2)}) %collective-permute-start.11) | collective-permute-done | bytes 393248 | tf_op jit(solution)/shard_map/ppermute | solution.py:27
  67.5 0.0 collective-permute-done.6.got_ref
  67.5 4.9 %collective-permute-done.9.arrived_ref = bf16[256,512]{1,0:T(8,128)(2,1)S(1)} collective-permute-done((bf16[256,512]{1,0:T(8,128)(2,1)S(1)}, bf16[256,512]{1,0:T(8,128)(2,1)S(1)}, u32[]{:S(2)}, u32[]{:S(2)}) %collective-permute-start.9) | collective-permute-done | bytes 262176 | tf_op jit(solution)/shard_map/ppermute | solution.py:27
  72.4 1.4 %shard_map.70 = f32[256,512]{1,0:T(8,128)} custom-call(bf16[2,3,256,128]{3,2,1,0:T(8,128)(2,1)S(1)} %get-tuple-element.35.keep_ref, bf16[2,3,256,128]{3,2,1,0:T(8,128)(2,1)S(1)} %collective-permute-done.6.got_ref, f32[256,512]{1,0:T(8,128)S(1)} %get-tuple-element.39.mine_ref, bf16[256,512]{1,0:T(8,128)(2,1)S(1)} %collective-permute-done.9.arrived_ref, ...), custom_call_target="tpu_custom_call" | custom-call | flops 402653184 | bytes 3670016 | tf_op jit(solution)/shard_map/pallas_call | solution.py:245
Async XLA Ops:
  0.0 7.2 %copy-start = (bf16[3,512,128]{2,1,0:T(8,128)(2,1)S(1)}, bf16[3,512,128]{2,1,0:T(8,128)(2,1)}, u32[]{:S(2)}) copy-start(bf16[3,512,128]{2,1,0:T(8,128)(2,1)} %w_ref.3) | copy-start | bytes 1179652
  1.3 6.0 %copy-start.1 = (s32[4]{0:T(128)S(1)}, s32[4]{0:T(128)}, u32[]{:S(2)}) copy-start(s32[4]{0:T(128)} %lengths_ref.5) | copy-start | bytes 52
  1.3 16.5 %collective-permute-start = (bf16[2,1024,128]{2,1,0:T(8,128)(2,1)S(1)}, bf16[2,1024,128]{2,1,0:T(8,128)(2,1)S(1)}, u32[]{:S(2)}, u32[]{:S(2)}) collective-permute-start(bf16[2,1024,128]{2,1,0:T(8,128)(2,1)S(1)} %get-tuple-element.23.qg_ref), channel_id=1, source_target_pairs={{4,0},{5,1},{6,2},{7,3},{8,4},{9,5},{10,6},{11,7},{12,8},{13,9},{1... | collective-permute-start | bytes 1572872 | tf_op jit(solution)/shard_map/ppermute | solution.py:27
  3.7 19.4 %collective-permute-start.1 = (bf16[2,1024,128]{2,1,0:T(8,128)(2,1)S(1)}, bf16[2,1024,128]{2,1,0:T(8,128)(2,1)S(1)}, u32[]{:S(2)}, u32[]{:S(2)}) collective-permute-start(bf16[2,1024,128]{2,1,0:T(8,128)(2,1)S(1)} %get-tuple-element.24.kv_ref), channel_id=1, source_target_pairs={{0,8},{1,9},{2,10},{3,11},{4,12},{5,13},{6,14},{7,15},{8,16},{9,17... | collective-permute-start | bytes 1572872 | tf_op jit(solution)/shard_map/ppermute | solution.py:27
  7.2 43.2 %collective-permute-start.8 = (bf16[3,512,128]{2,1,0:T(8,128)(2,1)S(1)}, bf16[3,512,128]{2,1,0:T(8,128)(2,1)S(1)}, u32[]{:S(2)}, u32[]{:S(2)}) collective-permute-start(bf16[3,512,128]{2,1,0:T(8,128)(2,1)S(1)} %copy-done), channel_id=1, source_target_pairs={{0,1},{1,0},{2,3},{3,2},{4,5},{5,4},{6,7},{7,6},{8,9},{9,8},{10,11... | collective-permute-start | bytes 1179656 | tf_op jit(solution)/shard_map/ppermute | solution.py:27
  26.5 24.0 %collective-permute-start.7 = (bf16[3,512,128]{2,1,0:T(8,128)(2,1)S(1)}, bf16[3,512,128]{2,1,0:T(8,128)(2,1)S(1)}, u32[]{:S(2)}, u32[]{:S(2)}) collective-permute-start(bf16[3,512,128]{2,1,0:T(8,128)(2,1)S(1)} %get-tuple-element.38), channel_id=1, source_target_pairs={{0,1},{1,0},{2,3},{3,2},{4,5},{5,4},{6,7},{7,6},{8,9},{9,8},{10,11... | collective-permute-start | bytes 1179656 | tf_op jit(solution)/shard_map/ppermute | solution.py:27
  26.6 8.1 %collective-permute-start.2 = (bf16[512,128]{1,0:T(8,128)(2,1)S(1)}, bf16[512,128]{1,0:T(8,128)(2,1)S(1)}, u32[]{:S(2)}, u32[]{:S(2)}) collective-permute-start(bf16[512,128]{1,0:T(8,128)(2,1)S(1)} %get-tuple-element.31), channel_id=1, source_target_pairs={{0,4},{1,5},{2,6},{3,7},{4,8},{5,9},{6,10},{7,11},{8,12},{9,13},{1... | collective-permute-start | bytes 393224 | tf_op jit(solution)/shard_map/ppermute | solution.py:27
  28.5 21.0 %collective-permute-start.3 = (bf16[2,512,128]{2,1,0:T(8,128)(2,1)S(1)}, bf16[2,512,128]{2,1,0:T(8,128)(2,1)S(1)}, u32[]{:S(2)}, u32[]{:S(2)}) collective-permute-start(bf16[2,512,128]{2,1,0:T(8,128)(2,1)S(1)} %get-tuple-element.32), channel_id=1, source_target_pairs={{8,0},{9,1},{10,2},{11,3},{12,4},{13,5},{14,6},{15,7},{16,8},{17,9... | collective-permute-start | bytes 786440 | tf_op jit(solution)/shard_map/ppermute | solution.py:27
  30.5 19.1 %collective-permute-start.5 = (bf16[2,512,128]{2,1,0:T(8,128)(2,1)S(1)}, bf16[2,512,128]{2,1,0:T(8,128)(2,1)S(1)}, u32[]{:S(2)}, u32[]{:S(2)}) collective-permute-start(bf16[2,512,128]{2,1,0:T(8,128)(2,1)S(1)} %get-tuple-element.34), channel_id=1, source_target_pairs={{8,2},{9,3},{10,0},{11,1},{12,6},{13,7},{14,4},{15,5},{16,10},{17,... | collective-permute-start | bytes 786440 | tf_op jit(solution)/shard_map/ppermute | solution.py:27
  34.8 13.5 %collective-permute-start.4 = (bf16[512,128]{1,0:T(8,128)(2,1)S(1)}, bf16[512,128]{1,0:T(8,128)(2,1)S(1)}, u32[]{:S(2)}, u32[]{:S(2)}) collective-permute-start(bf16[512,128]{1,0:T(8,128)(2,1)S(1)} %get-tuple-element.33), channel_id=1, source_target_pairs={{0,6},{1,7},{2,4},{3,5},{4,10},{5,11},{6,8},{7,9},{8,14},{9,15},{1... | collective-permute-start | bytes 393224 | tf_op jit(solution)/shard_map/ppermute | solution.py:27
  48.2 12.0 %collective-permute-start.10 = (bf16[3,512,128]{2,1,0:T(8,128)(2,1)S(1)}, bf16[3,512,128]{2,1,0:T(8,128)(2,1)S(1)}, u32[]{:S(2)}, u32[]{:S(2)}) collective-permute-start(bf16[3,512,128]{2,1,0:T(8,128)(2,1)S(1)} %copy-done), channel_id=1, source_target_pairs={{0,2},{1,3},{2,0},{3,1},{4,6},{5,7},{6,4},{7,5},{8,10},{9,11},{10,... | collective-permute-start | bytes 1179656 | tf_op jit(solution)/shard_map/ppermute | solution.py:27
  49.5 17.9 %collective-permute-start.11 = (bf16[3,512,128]{2,1,0:T(8,128)(2,1)S(1)}, bf16[3,512,128]{2,1,0:T(8,128)(2,1)S(1)}, u32[]{:S(2)}, u32[]{:S(2)}) collective-permute-start(bf16[3,512,128]{2,1,0:T(8,128)(2,1)S(1)} %copy-done), channel_id=1, source_target_pairs={{0,3},{1,2},{2,1},{3,0},{4,7},{5,6},{6,5},{7,4},{8,11},{9,10},{10,... | collective-permute-start | bytes 1179656 | tf_op jit(solution)/shard_map/ppermute | solution.py:27
  49.6 17.8 %collective-permute-start.6 = (bf16[2,3,256,128]{3,2,1,0:T(8,128)(2,1)S(1)}, bf16[2,3,256,128]{3,2,1,0:T(8,128)(2,1)S(1)}, u32[]{:S(2)}, u32[]{:S(2)}) collective-permute-start(bf16[2,3,256,128]{3,2,1,0:T(8,128)(2,1)S(1)} %get-tuple-element.36), channel_id=1, source_target_pairs={{0,1},{1,0},{2,3},{3,2},{4,5},{5,4},{6,7},{7,6},{8,9},{9,8},{10,11... | collective-permute-start | bytes 1179656 | tf_op jit(solution)/shard_map/ppermute | solution.py:27
  51.1 21.3 %collective-permute-start.9 = (bf16[256,512]{1,0:T(8,128)(2,1)S(1)}, bf16[256,512]{1,0:T(8,128)(2,1)S(1)}, u32[]{:S(2)}, u32[]{:S(2)}) collective-permute-start(bf16[256,512]{1,0:T(8,128)(2,1)S(1)} %get-tuple-element.40), channel_id=1, source_target_pairs={{0,2},{1,3},{2,0},{3,1},{4,6},{5,7},{6,4},{7,5},{8,10},{9,11},{10,... | collective-permute-start | bytes 786440 | tf_op jit(solution)/shard_map/ppermute | solution.py:27

commit v6 on v5

--- a/solution.py
+++ b/solution.py
@@ -9,7 +9,6 @@
 
 
 MAXLEN = 3072
-BLOCK = 512
 F32 = jnp.float32
 BF16 = jnp.bfloat16
 VMEM = pl.BlockSpec(memory_space=pltpu.VMEM)
@@ -73,59 +72,59 @@
     dq_ref[qs, :] += lax.dot_general(f, k, (((0,), (0,)), ((), ())), preferred_element_type=F32)
 
 
-def sweep(q_ref, g_ref, k_ref, v_ref, dq_ref, dk_ref, dv_ref, query_rows, key_row, q0=0, nq=None, k0=0, nk=None):
-    width = q_ref.shape[1]
-    nk = k_ref.shape[0] // BLOCK if nk is None else nk
+def sweep(qg_ref, kv_ref, dq_ref, dk_ref, dv_ref, query_rows, key_row, key_blocks):
+    block, width = qg_ref.shape[1:]
     zero = jnp.zeros((), BF16)
+    row = lax.broadcasted_iota(jnp.int32, (block, width), 0)
+    everything = pl.ds(0, block)
 
     def key_block(kb, carry):
-        kk = pl.multiple_of(kb * BLOCK, BLOCK)
-        ks = pl.ds(kk + k0, BLOCK)
-        kept_keys = lax.broadcasted_iota(jnp.int32, (BLOCK, width), 0) + kk >= key_row
-
-        def query_block(qb, carry):
-            qq = pl.multiple_of(qb * BLOCK, BLOCK)
-            qs = pl.ds(qq + q0, BLOCK)
-            kept = lax.broadcasted_iota(jnp.int32, (BLOCK, width), 0) + qq < query_rows
-            q = jnp.where(kept, q_ref[qs, :], zero)
-            g = jnp.where(kept, g_ref[qs, :], zero)
-            k = jnp.where(kept_keys, k_ref[ks, :], zero)
-            v = jnp.where(kept_keys, v_ref[ks, :], zero)
-            a, f = scores(q, g, k, v)
-            add_block(qs, ks, q, g, k, a, f, dq_ref, dk_ref, dv_ref)
-            return carry
-
-        return lax.fori_loop(0, (query_rows + BLOCK - 1) // BLOCK, query_block, carry)
-
-    first = jnp.where(query_rows > 0, key_row // BLOCK, nk)
-    lax.fori_loop(first, nk, key_block, 0)
-
-
-def pack_kernel(q_hbm, g_hbm, k_hbm, v_hbm, qg_ref, kv_ref, sems):
+        off = pl.multiple_of(kb * block, block)
+        ks = pl.ds(off, block)
+        kept, kept_keys = row < query_rows, row + off >= key_row
+        q = jnp.where(kept, qg_ref[0], zero)
+        g = jnp.where(kept, qg_ref[1], zero)
+        k = jnp.where(kept_keys, kv_ref[0, ks, :], zero)
+        v = jnp.where(kept_keys, kv_ref[1, ks, :], zero)
+        a, f = scores(q, g, k, v)
+        add_block(everything, ks, q, g, k, a, f, dq_ref, dk_ref, dv_ref)
+        return carry
+
+    first = jnp.where(query_rows > 0, key_row // block, key_blocks)
+    lax.fori_loop(first, key_blocks, key_block, 0)
+
+
+def halves(ref):
+    half = ref.shape[0] // 2
+    return ref.at[pl.ds(0, half)], ref.at[pl.ds(half, half)]
+
+
+def pack_kernel(q_hbm, g_hbm, k_hbm, v_hbm, qa_ref, qb_ref, kv_ref, sems):
+    half = qa_ref.shape[1]
     copies = [
-        pltpu.make_async_copy(q_hbm, qg_ref.at[0], sems.at[0]),
-        pltpu.make_async_copy(g_hbm, qg_ref.at[1], sems.at[1]),
-        pltpu.make_async_copy(k_hbm, kv_ref.at[0], sems.at[2]),
-        pltpu.make_async_copy(v_hbm, kv_ref.at[1], sems.at[3]),
+        pltpu.make_async_copy(k_hbm, kv_ref.at[0], sems.at[0]),
+        pltpu.make_async_copy(v_hbm, kv_ref.at[1], sems.at[1]),
     ]
+    for n, ref in enumerate((qa_ref, qb_ref)):
+        for m, hbm in enumerate((q_hbm, g_hbm)):
+            part = hbm.at[pl.ds(n * half, half)]
+            copies.append(pltpu.make_async_copy(part, ref.at[m], sems.at[2 + 2 * n + m]))
     for copy in copies:
         copy.start()
     for copy in copies:
         copy.wait()
 
 
-def own_kernel(lengths_ref, qg_ref, kv_ref, dq_ref, dk_ref, dv_ref):
-    q_ref, g_ref, k_ref, v_ref = qg_ref.at[0], qg_ref.at[1], kv_ref.at[0], kv_ref.at[1]
-    rows = q_ref.shape[0]
-    start = lax.axis_index("seq") * rows
+def own_kernel(lengths_ref, qa_ref, qb_ref, kv_ref, dq_ref, dk_ref, dv_ref):
+    block = qa_ref.shape[1]
+    strip = block // 2
+    start = lax.axis_index("seq") * (2 * block)
     dq_ref[...] = jnp.zeros_like(dq_ref)
     dk_ref[...] = jnp.zeros_like(dk_ref)
     dv_ref[...] = jnp.zeros_like(dv_ref)
 
-    def diagonal(b, carry):
-        off = pl.multiple_of(b * BLOCK, BLOCK)
-        rs = pl.ds(off, BLOCK)
-        query = lax.broadcasted_iota(jnp.int32, (1, BLOCK), 1) + start + off
+    for b, qg_ref in enumerate((qa_ref, qb_ref)):
+        query = lax.broadcasted_iota(jnp.int32, (1, block), 1) + start + b * block
 
         def step(u, carry):
             end, first = carry
@@ -133,54 +132,62 @@
             return end, jnp.where(end <= query, end, first)
 
         _, first = lax.fori_loop(
-            0, lengths_ref.shape[0], step, (jnp.int32(0), jnp.zeros((1, BLOCK), jnp.int32))
+            0, lengths_ref.shape[0], step, (jnp.int32(0), jnp.zeros((1, block), jnp.int32))
         )
-        key = lax.broadcasted_iota(jnp.int32, (BLOCK, BLOCK), 0) + start + off
-        mask = (key <= query) & (key >= first)
-        q, g, k, v = q_ref[rs, :], g_ref[rs, :], k_ref[rs, :], v_ref[rs, :]
-        a, f = scores(q, g, k, v, mask)
-        add_block(rs, rs, q, g, k, a, f, dq_ref, dk_ref, dv_ref)
-        return carry
-
-    lax.fori_loop(0, rows // BLOCK, diagonal, 0)
-    for b in range(1, rows // BLOCK):
-        query_rows, key_row = pair_limits(lengths_ref, start + b * BLOCK, start, b * BLOCK)
-        query_rows = jnp.minimum(query_rows, BLOCK)
-        sweep(
-            q_ref, g_ref, k_ref, v_ref, dq_ref, dk_ref, dv_ref, query_rows, key_row,
-            q0=b * BLOCK, nk=b,
-        )
-
-
-def next_kernel(lengths_ref, qgn_ref, kv_ref, dk_in, dv_in, dqn_ref, dk_ref, dv_ref):
-    rows = qgn_ref.shape[1]
+        for off in range(0, block, strip):
+            ks, qs = pl.ds(b * block + off, strip), pl.ds(b * block + off, block - off)
+            key = lax.broadcasted_iota(jnp.int32, (strip, block - off), 0) + start + b * block + off
+            mask = (key <= query[:, off:]) & (key >= first[:, off:])
+            q, g = qg_ref[0, off:, :], qg_ref[1, off:, :]
+            k, v = kv_ref[0, ks, :], kv_ref[1, ks, :]
+            a, f = scores(q, g, k, v, mask)
+            add_block(qs, ks, q, g, k, a, f, dq_ref, dk_ref, dv_ref)
+
+    query_rows, key_row = pair_limits(lengths_ref, start + block, start, block)
+    sweep(qb_ref, kv_ref, halves(dq_ref)[1], dk_ref, dv_ref, query_rows, key_row, 1)
+
+
+def next_kernel(lengths_ref, qan_ref, kv_ref, dk_in, dv_in, dqn_ref, dk_ref, dv_ref):
+    rows = kv_ref.shape[1]
     me = lax.axis_index("seq")
     dqn_ref[...] = jnp.zeros_like(dqn_ref)
     dk_ref[...] = dk_in[...]
     dv_ref[...] = dv_in[...]
-    limits = pair_limits(lengths_ref, (me + 1) * rows, me * rows, rows)
-    sweep(
-        qgn_ref.at[0], qgn_ref.at[1], kv_ref.at[0], kv_ref.at[1], dqn_ref, dk_ref, dv_ref, *limits
-    )
-
-
-def far_kernel(
-    lengths_ref, qg_ref, qgn_ref, kv_ref, dq_in, dqn_in, dk_own, dv_own,
-    keep_ref, send_ref, dq_same, dq_cross, dkv_same, dkv_cross,
-    dq_ref, dqn_ref, dk_ref, dv_ref,
-):
-    rows, width = dq_in.shape
+    query_rows, key_row = pair_limits(lengths_ref, (me + 1) * rows, me * rows, rows)
+    sweep(qan_ref, kv_ref, dqn_ref, dk_ref, dv_ref, query_rows, key_row, 2)
+
+
+def near_kernel(lengths_ref, qa_ref, qb_ref, kvn_ref, dq_in, dq_ref, dkn_ref, dvn_ref):
+    half, rows = qa_ref.shape[1], kvn_ref.shape[1]
     me = lax.axis_index("seq")
     dq_ref[...] = dq_in[...]
-    dqn_ref[...] = dqn_in[...]
-    dk_ref[...] = jnp.zeros_like(dk_ref)
-    dv_ref[...] = jnp.zeros_like(dv_ref)
-    k_ref, v_ref = kv_ref.at[0], kv_ref.at[1]
-    key_start = (me - 2) * rows
-    near = pair_limits(lengths_ref, me * rows, key_start, rows)
-    sweep(qg_ref.at[0], qg_ref.at[1], k_ref, v_ref, dq_ref, dk_ref, dv_ref, *near)
-    far = pair_limits(lengths_ref, (me + 1) * rows, key_start, rows)
-    sweep(qgn_ref.at[0], qgn_ref.at[1], k_ref, v_ref, dqn_ref, dk_ref, dv_ref, *far)
+    dkn_ref[...] = jnp.zeros_like(dkn_ref)
+    dvn_ref[...] = jnp.zeros_like(dvn_ref)
+    query_rows, key_row = pair_limits(lengths_ref, me * rows, (me - 2) * rows, rows)
+    for n, (qg_ref, dq) in enumerate(zip((qa_ref, qb_ref), halves(dq_ref))):
+        sweep(qg_ref, kvn_ref, dq, dkn_ref, dvn_ref, query_rows - n * half, key_row, 2)
+
+
+def rest_kernel(
+    lengths_ref, qan_ref, qbn_ref, kv_ref, kvn_ref,
+    dq_ref, dqa_in, dk_in, dv_in, dkn_in, dvn_in,
+    keep_ref, send_ref, dq_same, dq_cross, dkv_same, dkv_cross,
+    dqa_ref, dqb_ref, dk_own, dv_own, dk_ref, dv_ref,
+):
+    width = dq_ref.shape[1]
+    rows = kv_ref.shape[1]
+    me = lax.axis_index("seq")
+    dqa_ref[...] = dqa_in[...]
+    dqb_ref[...] = jnp.zeros_like(dqb_ref)
+    dk_own[...] = dk_in[...]
+    dv_own[...] = dv_in[...]
+    dk_ref[...] = dkn_in[...]
+    dv_ref[...] = dvn_in[...]
+    query_rows, key_row = pair_limits(lengths_ref, (me + 1) * rows, me * rows, rows)
+    sweep(qbn_ref, kv_ref, dqb_ref, dk_own, dv_own, query_rows - rows // 2, key_row, 2)
+    query_rows, key_row = pair_limits(lengths_ref, (me + 1) * rows, (me - 2) * rows, rows)
+    sweep(qan_ref, kvn_ref, dqa_ref, dk_ref, dv_ref, query_rows, key_row, 2)
+    sweep(qbn_ref, kvn_ref, dqb_ref, dk_ref, dv_ref, query_rows - rows // 2, key_row, 2)
 
     norm = MAXLEN**-0.5
     inner = 0.5 * norm * width**-0.5
@@ -190,7 +197,7 @@
     high, low = head // 2, head % 2
     for bit, dq_out, dkv_out in ((high, dq_same, dkv_same), (1 - high, dq_cross, dkv_cross)):
         src = pl.ds(pl.multiple_of(bit * half, half), half)
-        dq_out[...] = (dqn_ref[src, :] * inner).astype(BF16)
+        dq_out[...] = (jnp.where(bit == 0, dqa_ref[...], dqb_ref[...]) * inner).astype(BF16)
         dkv_out[0] = (dk_ref[src, :] * inner).astype(BF16)
         dkv_out[1] = (dv_ref[src, :] * norm).astype(BF16)
     for bit, out_ref in ((low, keep_ref), (1 - low, send_ref)):
@@ -260,34 +267,36 @@
     block = rows // heads
     like = jax.ShapeDtypeStruct
     wide = like((rows, width), F32)
-    pair = like((2, rows, width), BF16)
     pair_flops = 10 * rows * rows * width
 
-    query_grad, key_value = call(
-        pack_kernel, (pair, pair), tuple(pltpu.with_memory_space_constraint(x, pltpu.HBM) for x in (queries, out_grad, keys, values)), 1000,
-        scratch=[pltpu.SemaphoreType.DMA((4,))], lengths=False,
+    half = like((2, rows // 2, width), BF16)
+    half_wide = like((rows // 2, width), F32)
+    inputs = (queries, out_grad, keys, values)
+    qa, qb, kv = call(
+        pack_kernel, (half, half, like((2, rows, width), BF16)),
+        tuple(pltpu.with_memory_space_constraint(x, pltpu.HBM) for x in inputs), 1000,
+        scratch=[pltpu.SemaphoreType.DMA((6,))], lengths=False,
         space=pl.BlockSpec(memory_space=pltpu.HBM),
     )
-    query_grad_got = shift(query_grad, -1)
-    key_value_got = shift(key_value, 2)
-    w1, w2, w3 = (shift(w_proj, 0, flip) for flip in (1, 2, 3))
-
-    dq, dk, dv = call(own_kernel, (wide, wide, wide), (lengths, query_grad, key_value), pair_flops)
-    dqn, dk, dv = call(
-        next_kernel, (wide, wide, wide),
-        (lengths, query_grad_got, key_value, dk, dv), pair_flops,
-    )
+    kvn = shift(kv, 2)
+    qan = shift(qa, -1)
+    qbn = shift(qb, -1)
+    w2 = shift(w_proj, 0, 2)
+
+    dq, dk, dv = call(own_kernel, (wide, wide, wide), (lengths, qa, qb, kv), pair_flops)
+    dqn, dk, dv = call(next_kernel, (half_wide, wide, wide), (lengths, qan, kv, dk, dv), pair_flops)
+    dq, dkn, dvn = call(near_kernel, (wide, wide, wide), (lengths, qa, qb, kvn, dq), pair_flops)
     keep, send, dq_same, dq_cross, dkv_same, dkv_cross = call(
-        far_kernel,
+        rest_kernel,
         (
             like((3, 2 * block, width), BF16), like((3, 2 * block, width), BF16),
             like((2 * block, width), BF16), like((2 * block, width), BF16),
             like((2, 2 * block, width), BF16), like((2, 2 * block, width), BF16),
         ),
-        (lengths, query_grad, query_grad_got, key_value_got, dq, dqn, dk, dv),
-        pair_flops,
-        scratch=[pltpu.VMEM((rows, width), F32)] * 4,
-    )
+        (lengths, qan, qbn, kv, kvn, dq, dqn, dk, dv, dkn, dvn), pair_flops,
+        scratch=[pltpu.VMEM((rows // 2, width), F32)] * 2 + [pltpu.VMEM((rows, width), F32)] * 4,
+    )
+    w1, w3 = shift(w_proj, 0, 1), shift(w2, 0, 1)
     dkv_cross = shift(dkv_cross, -2, 2)
     dkv_same = shift(dkv_same, -2)
     dq_cross = shift(dq_cross, 1, 2)

time: 74.1 us -> 58.6 us (0.79)
  the two profiles are of different devices: /device:TPU:20 before, /device:TPU:22 now
where the time goes in v6:
time: 58.6 us; the launch traced here: 58.3 us
  starting transfers between devices  21 us (36%)
  waiting for transfers between devices  20.2 us (34%)
  Pallas kernels  16.9 us (29%)
    ppermute x13, starting transfers between devices, shift(): return lax.ppermute(value, ('seq', 'head'), pairs)  21 us
    ppermute x13, waiting for transfers between devices, shift(): return lax.ppermute(value, ('seq', 'head'), pairs)  20.2 us
    pallas_call x8, Pallas kernels, call(): pl.pallas_call(body, out_shape=outs, in_specs=specs, out_specs=tuple((VME...  16.9 us
  transfers between devices with their start and end apart: 13, of which 6 were waited for; matrix products, arithmetic and copies ran while one was open for 0% of the time, Pallas kernels for 24%

profile of v6, /device:TPU:22, one launch (start us, length us, event | category | flops | bytes accessed | tf_op | source)
XLA Modules:
  0.0 58.3 jit_solution(13298149769947448033)
XLA Ops:
  0.0 0.0 copy-start
  0.0 1.3 %shard_map.64 = (bf16[2,512,128]{2,1,0:T(8,128)(2,1)S(1)}, bf16[2,512,128]{2,1,0:T(8,128)(2,1)S(1)}, bf16[2,1024,128]{2,1,0:T(8,128)(2,1)S(1)}) custom-call(bf16[1024,128]{1,0:T(8,128)(2,1)} %q_hbm.1, bf16[1024,128]{1,0:T(8,128)(2,1)} %g_hbm.1, bf16[1024,128]{1,0:T(8,128)(2,1)} %k_hbm.1, bf16[1024,128]{1,0:T(8,128)(2,1)} %v_hbm.1), custom_call_target="tpu_custom_call" | custom-call | flops 1000 | bytes 2097152 | tf_op jit(solution)/shard_map/pallas_call | solution.py:252
  1.3 3.5 %collective-permute-start.2 = (bf16[2,1024,128]{2,1,0:T(8,128)(2,1)S(1)}, bf16[2,1024,128]{2,1,0:T(8,128)(2,1)S(1)}, u32[]{:S(2)}, u32[]{:S(2)}) collective-permute-start(bf16[2,1024,128]{2,1,0:T(8,128)(2,1)S(1)} %get-tuple-element.29.kv_ref), channel_id=1, source_target_pairs={{0,8},{1,9},{2,10},{3,11},{4,12},{5,13},{6,14},{7,15},{8,16},{9,17... | collective-permute-start | bytes 1572872 | tf_op jit(solution)/shard_map/ppermute | solution.py:26
  4.8 0.0 copy-start.1
  4.8 2.4 %collective-permute-start = (bf16[2,512,128]{2,1,0:T(8,128)(2,1)S(1)}, bf16[2,512,128]{2,1,0:T(8,128)(2,1)S(1)}, u32[]{:S(2)}, u32[]{:S(2)}) collective-permute-start(bf16[2,512,128]{2,1,0:T(8,128)(2,1)S(1)} %get-tuple-element.27.qa_ref), channel_id=1, source_target_pairs={{4,0},{5,1},{6,2},{7,3},{8,4},{9,5},{10,6},{11,7},{12,8},{13,9},{1... | collective-permute-start | bytes 786440 | tf_op jit(solution)/shard_map/ppermute | solution.py:26
  7.2 0.0 copy-done
  7.2 0.1 collective-permute-start.9
  7.3 0.6 %collective-permute-start.11 = (bf16[3,512,128]{2,1,0:T(8,128)(2,1)S(1)}, bf16[3,512,128]{2,1,0:T(8,128)(2,1)S(1)}, u32[]{:S(2)}, u32[]{:S(2)}) collective-permute-start(bf16[3,512,128]{2,1,0:T(8,128)(2,1)S(1)} %copy-done), channel_id=1, source_target_pairs={{0,2},{1,3},{2,0},{3,1},{4,6},{5,7},{6,4},{7,5},{8,10},{9,11},{10,... | collective-permute-start | bytes 1179656 | tf_op jit(solution)/shard_map/ppermute | solution.py:26
  7.9 3.3 %collective-permute-start.1 = (bf16[2,512,128]{2,1,0:T(8,128)(2,1)S(1)}, bf16[2,512,128]{2,1,0:T(8,128)(2,1)S(1)}, u32[]{:S(2)}, u32[]{:S(2)}) collective-permute-start(bf16[2,512,128]{2,1,0:T(8,128)(2,1)S(1)} %get-tuple-element.28.qb_ref), channel_id=1, source_target_pairs={{4,0},{5,1},{6,2},{7,3},{8,4},{9,5},{10,6},{11,7},{12,8},{13,9},{1... | collective-permute-start | bytes 786440 | tf_op jit(solution)/shard_map/ppermute | solution.py:26
  11.2 0.0 copy-done.1
  11.2 4.3 %shard_map.65 = (f32[1024,128]{1,0:T(8,128)S(1)}, f32[1024,128]{1,0:T(8,128)S(1)}, f32[1024,128]{1,0:T(8,128)S(1)}) custom-call(s32[4]{0:T(128)S(1)} %copy-done.1, bf16[2,512,128]{2,1,0:T(8,128)(2,1)S(1)} %get-tuple-element.27.qa_ref, bf16[2,512,128]{2,1,0:T(8,128)(2,1)S(1)} %get-tuple-element.28.qb_ref, bf16[2,1024,128]{2,1,0:T(8,128)(2,1)S(1)} %get-tuple-element.29.kv_ref), custom_call_target="tpu_custom_call" | custom-call | flops 1342177280 | bytes 2621456 | tf_op jit(solution)/shard_map/pallas_call | solution.py:252
  15.5 1.3 %collective-permute-done.qan_ref = bf16[2,512,128]{2,1,0:T(8,128)(2,1)S(1)} collective-permute-done((bf16[2,512,128]{2,1,0:T(8,128)(2,1)S(1)}, bf16[2,512,128]{2,1,0:T(8,128)(2,1)S(1)}, u32[]{:S(2)}, u32[]{:S(2)}) %collective-permute-start) | collective-permute-done | bytes 262176 | tf_op jit(solution)/shard_map/ppermute | solution.py:26
  16.8 3.0 %shard_map.67 = (f32[512,128]{1,0:T(8,128)S(1)}, f32[1024,128]{1,0:T(8,128)S(1)}, f32[1024,128]{1,0:T(8,128)S(1)}) custom-call(s32[4]{0:T(128)S(1)} %copy-done.1, bf16[2,512,128]{2,1,0:T(8,128)(2,1)S(1)} %collective-permute-done.qan_ref, bf16[2,1024,128]{2,1,0:T(8,128)(2,1)S(1)} %get-tuple-element.29.kv_ref, f32[1024,128]{1,0:T(8,128)S(1)} %get-tuple-element.32.dk_in, ...), custom_call_target="tpu_custom_call" | custom-call | flops 1342177280 | bytes 3145744 | tf_op jit(solution)/shard_map/pallas_call | solution.py:252
  19.7 0.0 collective-permute-done.2.kvn_ref
  19.8 3.0 %shard_map.66 = (f32[1024,128]{1,0:T(8,128)S(1)}, f32[1024,128]{1,0:T(8,128)S(1)}, f32[1024,128]{1,0:T(8,128)S(1)}) custom-call(s32[4]{0:T(128)S(1)} %copy-done.1, bf16[2,512,128]{2,1,0:T(8,128)(2,1)S(1)} %get-tuple-element.27.qa_ref, bf16[2,512,128]{2,1,0:T(8,128)(2,1)S(1)} %get-tuple-element.28.qb_ref, ...), custom_call_target="tpu_custom_call" | custom-call | flops 1342177280 | bytes 3145744 | tf_op jit(solution)/shard_map/pallas_call | solution.py:252
  22.7 0.0 collective-permute-done.1.qbn_ref
  22.7 3.3 %shard_map.68 = (bf16[3,512,128]{2,1,0:T(8,128)(2,1)S(1)}, bf16[3,512,128]{2,1,0:T(8,128)(2,1)S(1)}, bf16[512,128]{1,0:T(8,128)(2,1)S(1)}, bf16[512,128]{1,0:T(8...) custom-call(s32[4]{0:T(128)S(1)} %copy-done.1, ...), custom_call_target="tpu_custom_call" | custom-call | flops 1342177280 | bytes 6029328 | tf_op jit(solution)/shard_map/pallas_call | solution.py:252
  26.1 0.1 collective-permute-start.8
  26.2 1.9 %collective-permute-start.3 = (bf16[512,128]{1,0:T(8,128)(2,1)S(1)}, bf16[512,128]{1,0:T(8,128)(2,1)S(1)}, u32[]{:S(2)}, u32[]{:S(2)}) collective-permute-start(bf16[512,128]{1,0:T(8,128)(2,1)S(1)} %get-tuple-element.39), channel_id=1, source_target_pairs={{0,4},{1,5},{2,6},{3,7},{4,8},{5,9},{6,10},{7,11},{8,12},{9,13},{1... | collective-permute-start | bytes 393224 | tf_op jit(solution)/shard_map/ppermute | solution.py:26
  28.1 1.9 %collective-permute-start.4 = (bf16[2,512,128]{2,1,0:T(8,128)(2,1)S(1)}, bf16[2,512,128]{2,1,0:T(8,128)(2,1)S(1)}, u32[]{:S(2)}, u32[]{:S(2)}) collective-permute-start(bf16[2,512,128]{2,1,0:T(8,128)(2,1)S(1)} %get-tuple-element.40), channel_id=1, source_target_pairs={{8,0},{9,1},{10,2},{11,3},{12,4},{13,5},{14,6},{15,7},{16,8},{17,9... | collective-permute-start | bytes 786440 | tf_op jit(solution)/shard_map/ppermute | solution.py:26
  30.0 0.0 collective-permute-done.11.w2_ref
  30.0 1.9 %collective-permute-start.6 = (bf16[2,512,128]{2,1,0:T(8,128)(2,1)S(1)}, bf16[2,512,128]{2,1,0:T(8,128)(2,1)S(1)}, u32[]{:S(2)}, u32[]{:S(2)}) collective-permute-start(bf16[2,512,128]{2,1,0:T(8,128)(2,1)S(1)} %get-tuple-element.42), channel_id=1, source_target_pairs={{8,2},{9,3},{10,0},{11,1},{12,6},{13,7},{14,4},{15,5},{16,10},{17,... | collective-permute-start | bytes 786440 | tf_op jit(solution)/shard_map/ppermute | solution.py:26
  32.0 2.0 %collective-permute-done.3.dq_same = bf16[512,128]{1,0:T(8,128)(2,1)S(1)} collective-permute-done((bf16[512,128]{1,0:T(8,128)(2,1)S(1)}, bf16[512,128]{1,0:T(8,128)(2,1)S(1)}, u32[]{:S(2)}, u32[]{:S(2)}) %collective-permute-start.3) | collective-permute-done | bytes 131104 | tf_op jit(solution)/shard_map/ppermute | solution.py:26
  34.0 4.3 %collective-permute-start.5 = (bf16[512,128]{1,0:T(8,128)(2,1)S(1)}, bf16[512,128]{1,0:T(8,128)(2,1)S(1)}, u32[]{:S(2)}, u32[]{:S(2)}) collective-permute-start(bf16[512,128]{1,0:T(8,128)(2,1)S(1)} %get-tuple-element.41), channel_id=1, source_target_pairs={{0,6},{1,7},{2,4},{3,5},{4,10},{5,11},{6,8},{7,9},{8,14},{9,15},{1... | collective-permute-start | bytes 393224 | tf_op jit(solution)/shard_map/ppermute | solution.py:26
  38.3 9.0 %collective-permute-done.5.dq_cross = bf16[512,128]{1,0:T(8,128)(2,1)S(1)} collective-permute-done((bf16[512,128]{1,0:T(8,128)(2,1)S(1)}, bf16[512,128]{1,0:T(8,128)(2,1)S(1)}, u32[]{:S(2)}, u32[]{:S(2)}) %collective-permute-start.5) | collective-permute-done | bytes 131104 | tf_op jit(solution)/shard_map/ppermute | solution.py:26
  47.3 0.0 collective-permute-start.12
  47.3 0.0 collective-permute-done.4.dkv_same
  47.3 0.0 collective-permute-done.6.dkv_cross
  47.3 0.1 shard_map.69
  47.4 0.6 collective-permute-start.7
  47.9 0.0 collective-permute-done.9.w1_ref
  48.0 0.0 collective-permute-done.8.got_ref
  48.0 0.6 %shard_map.70 = (f32[256,512]{1,0:T(8,128)S(1)}, bf16[256,512]{1,0:T(8,128)(2,1)S(1)}) custom-call(bf16[3,512,128]{2,1,0:T(8,128)(2,1)S(1)} %get-tuple-element.45.keep_ref, bf16[3,512,128]{2,1,0:T(8,128)(2,1)S(1)} %collective-permute-done.8.got_ref, bf16[3,512,128]{2,1,0:T(8,128)(2,1)S(1)} %copy-done, bf16[3,512,128]{2,1,0:T(8,128)(2,1)S(1)} %collective-permute-done.9.w1_ref), custom_call_target="tpu_custom_call" | custom-call | flops 201326592 | bytes 2359296 | tf_op jit(solution)/shard_map/pallas_call | solution.py:252
  48.6 0.4 collective-permute-start.10
  49.0 0.1 collective-permute-done.12.w3_ref
  49.0 0.6 collective-permute-done.7.got_ref
  49.6 7.3 %collective-permute-done.10.arrived_ref = bf16[256,512]{1,0:T(8,128)(2,1)S(1)} collective-permute-done((bf16[256,512]{1,0:T(8,128)(2,1)S(1)}, bf16[256,512]{1,0:T(8,128)(2,1)S(1)}, u32[]{:S(2)}, u32[]{:S(2)}) %collective-permute-start.10) | collective-permute-done | bytes 262176 | tf_op jit(solution)/shard_map/ppermute | solution.py:26
  56.9 1.4 %shard_map.71 = f32[256,512]{1,0:T(8,128)} custom-call(bf16[2,3,256,128]{3,2,1,0:T(8,128)(2,1)S(1)} %get-tuple-element.43.keep_ref, bf16[2,3,256,128]{3,2,1,0:T(8,128)(2,1)S(1)} %collective-permute-done.7.got_ref, f32[256,512]{1,0:T(8,128)S(1)} %get-tuple-element.47.mine_ref, bf16[256,512]{1,0:T(8,128)(2,1)S(1)} %collective-permute-done.10.arrived_ref, ...), custom_call_target="tpu_custom_call" | custom-call | flops 402653184 | bytes 3670016 | tf_op jit(solution)/shard_map/pallas_call | solution.py:252
Async XLA Ops:
  0.0 7.2 %copy-start = (bf16[3,512,128]{2,1,0:T(8,128)(2,1)S(1)}, bf16[3,512,128]{2,1,0:T(8,128)(2,1)}, u32[]{:S(2)}) copy-start(bf16[3,512,128]{2,1,0:T(8,128)(2,1)} %w_ref.3) | copy-start | bytes 1179652
  1.3 18.5 %collective-permute-start.2 = (bf16[2,1024,128]{2,1,0:T(8,128)(2,1)S(1)}, bf16[2,1024,128]{2,1,0:T(8,128)(2,1)S(1)}, u32[]{:S(2)}, u32[]{:S(2)}) collective-permute-start(bf16[2,1024,128]{2,1,0:T(8,128)(2,1)S(1)} %get-tuple-element.29.kv_ref), channel_id=1, source_target_pairs={{0,8},{1,9},{2,10},{3,11},{4,12},{5,13},{6,14},{7,15},{8,16},{9,17... | collective-permute-start | bytes 1572872 | tf_op jit(solution)/shard_map/ppermute | solution.py:26
  4.8 6.4 %copy-start.1 = (s32[4]{0:T(128)S(1)}, s32[4]{0:T(128)}, u32[]{:S(2)}) copy-start(s32[4]{0:T(128)} %lengths_ref.7) | copy-start | bytes 52
  4.8 12.0 %collective-permute-start = (bf16[2,512,128]{2,1,0:T(8,128)(2,1)S(1)}, bf16[2,512,128]{2,1,0:T(8,128)(2,1)S(1)}, u32[]{:S(2)}, u32[]{:S(2)}) collective-permute-start(bf16[2,512,128]{2,1,0:T(8,128)(2,1)S(1)} %get-tuple-element.27.qa_ref), channel_id=1, source_target_pairs={{4,0},{5,1},{6,2},{7,3},{8,4},{9,5},{10,6},{11,7},{12,8},{13,9},{1... | collective-permute-start | bytes 786440 | tf_op jit(solution)/shard_map/ppermute | solution.py:26
  7.2 40.7 %collective-permute-start.9 = (bf16[3,512,128]{2,1,0:T(8,128)(2,1)S(1)}, bf16[3,512,128]{2,1,0:T(8,128)(2,1)S(1)}, u32[]{:S(2)}, u32[]{:S(2)}) collective-permute-start(bf16[3,512,128]{2,1,0:T(8,128)(2,1)S(1)} %copy-done), channel_id=1, source_target_pairs={{0,1},{1,0},{2,3},{3,2},{4,5},{5,4},{6,7},{7,6},{8,9},{9,8},{10,11... | collective-permute-start | bytes 1179656 | tf_op jit(solution)/shard_map/ppermute | solution.py:26
  7.3 22.7 %collective-permute-start.11 = (bf16[3,512,128]{2,1,0:T(8,128)(2,1)S(1)}, bf16[3,512,128]{2,1,0:T(8,128)(2,1)S(1)}, u32[]{:S(2)}, u32[]{:S(2)}) collective-permute-start(bf16[3,512,128]{2,1,0:T(8,128)(2,1)S(1)} %copy-done), channel_id=1, source_target_pairs={{0,2},{1,3},{2,0},{3,1},{4,6},{5,7},{6,4},{7,5},{8,10},{9,11},{10,... | collective-permute-start | bytes 1179656 | tf_op jit(solution)/shard_map/ppermute | solution.py:26
  7.9 14.8 %collective-permute-start.1 = (bf16[2,512,128]{2,1,0:T(8,128)(2,1)S(1)}, bf16[2,512,128]{2,1,0:T(8,128)(2,1)S(1)}, u32[]{:S(2)}, u32[]{:S(2)}) collective-permute-start(bf16[2,512,128]{2,1,0:T(8,128)(2,1)S(1)} %get-tuple-element.28.qb_ref), channel_id=1, source_target_pairs={{4,0},{5,1},{6,2},{7,3},{8,4},{9,5},{10,6},{11,7},{12,8},{13,9},{1... | collective-permute-start | bytes 786440 | tf_op jit(solution)/shard_map/ppermute | solution.py:26
  26.1 21.9 %collective-permute-start.8 = (bf16[3,512,128]{2,1,0:T(8,128)(2,1)S(1)}, bf16[3,512,128]{2,1,0:T(8,128)(2,1)S(1)}, u32[]{:S(2)}, u32[]{:S(2)}) collective-permute-start(bf16[3,512,128]{2,1,0:T(8,128)(2,1)S(1)} %get-tuple-element.46), channel_id=1, source_target_pairs={{0,1},{1,0},{2,3},{3,2},{4,5},{5,4},{6,7},{7,6},{8,9},{9,8},{10,11... | collective-permute-start | bytes 1179656 | tf_op jit(solution)/shard_map/ppermute | solution.py:26
  26.2 7.8 %collective-permute-start.3 = (bf16[512,128]{1,0:T(8,128)(2,1)S(1)}, bf16[512,128]{1,0:T(8,128)(2,1)S(1)}, u32[]{:S(2)}, u32[]{:S(2)}) collective-permute-start(bf16[512,128]{1,0:T(8,128)(2,1)S(1)} %get-tuple-element.39), channel_id=1, source_target_pairs={{0,4},{1,5},{2,6},{3,7},{4,8},{5,9},{6,10},{7,11},{8,12},{9,13},{1... | collective-permute-start | bytes 393224 | tf_op jit(solution)/shard_map/ppermute | solution.py:26
  28.1 19.2 %collective-permute-start.4 = (bf16[2,512,128]{2,1,0:T(8,128)(2,1)S(1)}, bf16[2,512,128]{2,1,0:T(8,128)(2,1)S(1)}, u32[]{:S(2)}, u32[]{:S(2)}) collective-permute-start(bf16[2,512,128]{2,1,0:T(8,128)(2,1)S(1)} %get-tuple-element.40), channel_id=1, source_target_pairs={{8,0},{9,1},{10,2},{11,3},{12,4},{13,5},{14,6},{15,7},{16,8},{17,9... | collective-permute-start | bytes 786440 | tf_op jit(solution)/shard_map/ppermute | solution.py:26
  30.0 17.3 %collective-permute-start.6 = (bf16[2,512,128]{2,1,0:T(8,128)(2,1)S(1)}, bf16[2,512,128]{2,1,0:T(8,128)(2,1)S(1)}, u32[]{:S(2)}, u32[]{:S(2)}) collective-permute-start(bf16[2,512,128]{2,1,0:T(8,128)(2,1)S(1)} %get-tuple-element.42), channel_id=1, source_target_pairs={{8,2},{9,3},{10,0},{11,1},{12,6},{13,7},{14,4},{15,5},{16,10},{17,... | collective-permute-start | bytes 786440 | tf_op jit(solution)/shard_map/ppermute | solution.py:26
  34.0 13.4 %collective-permute-start.5 = (bf16[512,128]{1,0:T(8,128)(2,1)S(1)}, bf16[512,128]{1,0:T(8,128)(2,1)S(1)}, u32[]{:S(2)}, u32[]{:S(2)}) collective-permute-start(bf16[512,128]{1,0:T(8,128)(2,1)S(1)} %get-tuple-element.41), channel_id=1, source_target_pairs={{0,6},{1,7},{2,4},{3,5},{4,10},{5,11},{6,8},{7,9},{8,14},{9,15},{1... | collective-permute-start | bytes 393224 | tf_op jit(solution)/shard_map/ppermute | solution.py:26
  47.3 1.7 %collective-permute-start.12 = (bf16[3,512,128]{2,1,0:T(8,128)(2,1)S(1)}, bf16[3,512,128]{2,1,0:T(8,128)(2,1)S(1)}, u32[]{:S(2)}, u32[]{:S(2)}) collective-permute-start(bf16[3,512,128]{2,1,0:T(8,128)(2,1)S(1)} %collective-permute-done.11.w2_ref), channel_id=1, source_target_pairs={{0,1},{1,0},{2,3},{3,2},{4,5},{5,4},{6,7},{7,6},{8,9},{9,8},{10,11... | collective-permute-start | bytes 1179656 | tf_op jit(solution)/shard_map/ppermute | solution.py:26
  47.4 2.2 %collective-permute-start.7 = (bf16[2,3,256,128]{3,2,1,0:T(8,128)(2,1)S(1)}, bf16[2,3,256,128]{3,2,1,0:T(8,128)(2,1)S(1)}, u32[]{:S(2)}, u32[]{:S(2)}) collective-permute-start(bf16[2,3,256,128]{3,2,1,0:T(8,128)(2,1)S(1)} %get-tuple-element.44), channel_id=1, source_target_pairs={{0,1},{1,0},{2,3},{3,2},{4,5},{5,4},{6,7},{7,6},{8,9},{9,8},{10,11... | collective-permute-start | bytes 1179656 | tf_op jit(solution)/shard_map/ppermute | solution.py:26
  48.6 8.3 %collective-permute-start.10 = (bf16[256,512]{1,0:T(8,128)(2,1)S(1)}, bf16[256,512]{1,0:T(8,128)(2,1)S(1)}, u32[]{:S(2)}, u32[]{:S(2)}) collective-permute-start(bf16[256,512]{1,0:T(8,128)(2,1)S(1)} %get-tuple-element.48), channel_id=1, source_target_pairs={{0,2},{1,3},{2,0},{3,1},{4,6},{5,7},{6,4},{7,5},{8,10},{9,11},{10,... | collective-permute-start | bytes 786440 | tf_op jit(solution)/shard_map/ppermute | solution.py:26
